TPU v7x, 256 devices: a whole 4x4x8 slice. The times are simulated.
256 devices in a mesh: lat: 8 (over x_hi, y), lon: 32 (over x_lo, z, core).
Axes of the slice: x: 4 (x_hi: 2, x_lo: 2; x = x_hi * 2 + x_lo), y: 4, z: 8, core: 2. Of those that a mesh axis runs over, the one named last changes fastest.
Arguments:
- sea_state: bfloat16 [64, 256, 4096], P(None, 'lat', 'lon'), may hold values from -60 to 60
- conv_kernel: bfloat16 [64, 49], replicated, may hold values from -0.875 to 0.875
- conv_bias: bfloat16 [64], replicated, may hold values from -3 to 3
- norm_gain: bfloat16 [64], replicated, may hold values from 0.25 to 1.75
- norm_shift: bfloat16 [64], replicated, may hold values from -3 to 3
- w_in: bfloat16 [64, 256], replicated, may hold values from -0.75 to 0.75
- b_in: bfloat16 [256], replicated, may hold values from -3 to 3
- w_out: bfloat16 [256, 64], replicated, may hold values from -0.375 to 0.375
- b_out: bfloat16 [64], replicated, may hold values from -3 to 3
- layer_scale: bfloat16 [64], replicated, may hold values from 0.29882812 to 1
- sea_mask: int32 [256, 4096], P('lat', 'lon'), may hold values 0 or 1
- cotangent: bfloat16 [64, 256, 4096], P(None, 'lat', 'lon'), may hold values from -6 to 6
Outputs:
- new_state: bfloat16 [64, 256, 4096], P(None, 'lat', 'lon')
- state_grad: bfloat16 [64, 256, 4096], P(None, 'lat', 'lon')
- kernel_grad: float32 [64, 49], replicated
- w_in_grad: float32 [64, 256], replicated
- w_out_grad: float32 [256, 64], replicated
- b_in_grad: float32 [256], replicated
- channel_grads: float32 [5, 64], replicated
Inputs may be any that keep to these rules, and one draw needn't show every extreme that they name: `sea_mask`: 1 marks an ocean cell, 0 land.
All inputs are finite; a program needn't handle non-finite values. No bound on the sum of `sea_mask` on one device may be relied on, other than what follows from the above.
Results may differ from a plain program's by a relative error of at most 0.0062.
Values sent between devices are 32-bit elements; how exact they have to be, the bound alone decides.
No kernel may reach another device: no remote copies, remote signals or barrier semaphores. Data moves between devices by JAX's collectives and lax.ppermute only.
A program may use at most 128 MiB of HBM per device.

v0:
```python
import math

import jax
import jax.numpy as jnp
from jax import lax
from jax.sharding import PartitionSpec as P

slope_coef = 0.044715
tanh_scale = math.sqrt(2.0 / math.pi)
ln_epsilon = 1e-06


def with_halo(value, sides, width, wrap):
    for axis, dim in sides:
        size, length = (lax.axis_size(axis), value.shape[dim])
        up = [(i, (i + 1) % size) for i in range(size if wrap else size - 1)]
        down = [(j, i) for i, j in up]
        last = lax.slice_in_dim(value, length - width, length, axis=dim)
        initial = lax.slice_in_dim(value, 0, width, axis=dim)
        before = lax.ppermute(last, axis, up)
        after = lax.ppermute(initial, axis, down)
        value = jnp.concatenate([before, value, after], axis=dim)
    return value


def depthwise(padded, conv_kernel, conv_bias, row_count, col_count):
    weights = conv_kernel.astype(jnp.float32)
    running = (
        jnp.zeros((padded.shape[0], row_count, col_count), jnp.float32)
        + conv_bias.astype(jnp.float32)[:, None, None]
    )
    for row_off in range(7):
        for col_off in range(7):
            window = padded[:, row_off : row_off + row_count, col_off : col_off + col_count]
            running = running + weights[:, 7 * row_off + col_off][:, None, None] * window
    return running


def kernel_grads(padded, conv_grad):
    row_count = conv_grad.shape[1]
    col_count = conv_grad.shape[2]
    columns = []
    for row_off in range(7):
        for col_off in range(7):
            window = padded[:, row_off : row_off + row_count, col_off : col_off + col_count]
            columns.append(jnp.sum(conv_grad * window, axis=(1, 2)))
    return jnp.stack(columns, axis=1)


def spread_back(conv_grad, conv_kernel):
    row_count = conv_grad.shape[1]
    col_count = conv_grad.shape[2]
    weights = conv_kernel.astype(jnp.float32)
    widened = jnp.pad(conv_grad, ((0, 0), (6, 6), (6, 6)))
    running = jnp.zeros((conv_grad.shape[0], row_count + 6, col_count + 6), jnp.float32)
    for row_off in range(7):
        for col_off in range(7):
            window = widened[
                :, 6 - row_off : 12 - row_off + row_count, 6 - col_off : 12 - col_off + col_count
            ]
            running = running + weights[:, 7 * row_off + col_off][:, None, None] * window
    return running


def pointwise(
    conv_out,
    sea_state,
    cotangent,
    sea_mask,
    norm_gain,
    norm_shift,
    w_in,
    b_in,
    w_out,
    b_out,
    layer_scale,
):
    chan_count = conv_out.shape[0]
    flat_conv = conv_out.reshape(chan_count, -1)
    centre = flat_conv - jnp.mean(flat_conv, axis=0, keepdims=True)
    inv_std = lax.rsqrt(jnp.mean(centre * centre, axis=0, keepdims=True) + ln_epsilon)
    unit_norm = centre * inv_std
    gain_col = norm_gain.astype(jnp.float32)[:, None]
    normed = (unit_norm * gain_col + norm_shift.astype(jnp.float32)[:, None]).astype(jnp.bfloat16)
    pre_act = (
        jnp.dot(w_in.T, normed, preferred_element_type=jnp.float32)
        + b_in.astype(jnp.float32)[:, None]
    )
    tangent = jnp.tanh(tanh_scale * (pre_act + slope_coef * pre_act * pre_act * pre_act))
    hidden = (0.5 * pre_act * (1.0 + tangent)).astype(jnp.bfloat16)
    mixed_out = (
        jnp.dot(w_out.T, hidden, preferred_element_type=jnp.float32)
        + b_out.astype(jnp.float32)[:, None]
    )
    ocean_mask = sea_mask.reshape(1, -1).astype(jnp.float32)
    scale_col = layer_scale.astype(jnp.float32)[:, None]
    state_flat = sea_state.reshape(chan_count, -1).astype(jnp.float32)
    new_state = (ocean_mask * (state_flat + scale_col * mixed_out)).astype(jnp.bfloat16)
    masked_cot = ocean_mask * cotangent.reshape(chan_count, -1).astype(jnp.float32)
    mixed_grad = (scale_col * masked_cot).astype(jnp.bfloat16)
    scale_sum = jnp.sum(masked_cot * mixed_out, axis=1)
    out_bias_sum = jnp.sum(mixed_grad.astype(jnp.float32), axis=1)
    cell_axes = (((1,), (1,)), ((), ()))
    out_weight_sum = lax.dot_general(
        hidden, mixed_grad, cell_axes, preferred_element_type=jnp.float32
    )
    hidden_grad = jnp.dot(w_out, mixed_grad, preferred_element_type=jnp.float32)
    gelu_slope = 0.5 * (1.0 + tangent) + 0.5 * pre_act * (1.0 - tangent * tangent) * tanh_scale * (
        1.0 + 3.0 * slope_coef * pre_act * pre_act
    )
    pre_grad = (hidden_grad * gelu_slope).astype(jnp.bfloat16)
    in_bias_sum = jnp.sum(pre_grad.astype(jnp.float32), axis=1)
    in_weight_sum = lax.dot_general(normed, pre_grad, cell_axes, preferred_element_type=jnp.float32)
    normed_grad = jnp.dot(w_in, pre_grad, preferred_element_type=jnp.float32)
    gain_sum = jnp.sum(normed_grad * unit_norm, axis=1)
    shift_sum = jnp.sum(normed_grad, axis=1)
    unit_grad = normed_grad * gain_col
    conv_grad = inv_std * (
        unit_grad
        - jnp.mean(unit_grad, axis=0, keepdims=True)
        - unit_norm * jnp.mean(unit_grad * unit_norm, axis=0, keepdims=True)
    )
    partial_sums = (
        scale_sum,
        out_bias_sum,
        out_weight_sum,
        in_bias_sum,
        in_weight_sum,
        gain_sum,
        shift_sum,
    )
    return (
        new_state.reshape(conv_out.shape),
        conv_grad.reshape(conv_out.shape),
        masked_cot.reshape(conv_out.shape),
        partial_sums,
    )


def lon_extend(values):
    return with_halo(values, (("lon", 2),), 3, True)


def lat_extend(values):
    return with_halo(values, (("lat", 1),), 3, False)


def fold_partner(top_rows):
    lon_count = lax.axis_size("lon")
    pieces = top_rows.reshape(lon_count, -1)
    scattered = lax.all_to_all(pieces, "lon", split_axis=0, concat_axis=0, tiled=True)
    collected = lax.all_to_all(scattered[::-1], "lon", split_axis=0, concat_axis=0, tiled=True)
    return collected.reshape(top_rows.shape)


def fold_columns(values, col_count):
    col_rims = jnp.concatenate([values[:, :, :3], values[:, :, col_count + 3 :]], axis=2)
    col_from = lon_extend(col_rims)
    folded = values[:, :, 3 : col_count + 3]
    folded = folded.at[:, :, :3].add(col_from[:, :, :3])
    return folded.at[:, :, col_count - 3 :].add(col_from[:, :, 9:])


def fold_rows(values, row_count, on_top):
    row_rims = jnp.concatenate([values[:, :3], values[:, row_count + 3 :]], axis=1)
    row_from = lat_extend(row_rims)
    folded = values[:, 3 : row_count + 3]
    folded = folded.at[:, :3].add(row_from[:, :3])
    folded = folded.at[:, row_count - 3 :].add(row_from[:, 9:])
    returned = fold_partner(values[:, row_count + 3 :])[:, ::-1, ::-1]
    return folded.at[:, row_count - 3 :].add(jnp.where(on_top, returned, 0.0))


def per_device(
    sea_state,
    conv_kernel,
    conv_bias,
    norm_gain,
    norm_shift,
    w_in,
    b_in,
    w_out,
    b_out,
    layer_scale,
    sea_mask,
    cotangent,
):
    chan_count, row_count, col_count = sea_state.shape
    on_top = lax.axis_index("lat") == lax.axis_size("lat") - 1
    widened = sea_state.astype(jnp.float32)
    tall_field = lat_extend(widened)
    mirrored = fold_partner(widened[:, row_count - 3 :, :])[:, ::-1, ::-1]
    tall_field = jnp.concatenate(
        [
            tall_field[:, : row_count + 3],
            jnp.where(on_top, mirrored, tall_field[:, row_count + 3 :]),
        ],
        axis=1,
    )
    padded = lon_extend(tall_field)
    conv_out = depthwise(padded, conv_kernel, conv_bias, row_count, col_count)
    new_state, conv_grad, masked_cot, partial_sums = pointwise(
        conv_out,
        sea_state,
        cotangent,
        sea_mask,
        norm_gain,
        norm_shift,
        w_in,
        b_in,
        w_out,
        b_out,
        layer_scale,
    )
    scale_sum, out_bias_sum, out_weight_sum, in_bias_sum, in_weight_sum, gain_sum, shift_sum = (
        partial_sums
    )
    kernel_sum = kernel_grads(padded, conv_grad)
    bias_sum = jnp.sum(conv_grad, axis=(1, 2))
    spread = spread_back(conv_grad, conv_kernel)
    grid_grad = fold_rows(fold_columns(spread, col_count), row_count, on_top)
    state_grad = (masked_cot + grid_grad).astype(jnp.bfloat16)
    totals = lax.psum(
        (
            kernel_sum,
            bias_sum,
            gain_sum,
            shift_sum,
            out_bias_sum,
            scale_sum,
            in_weight_sum,
            out_weight_sum,
            in_bias_sum,
        ),
        ("lat", "lon"),
    )
    (
        kernel_total,
        bias_total,
        gain_total,
        shift_total,
        out_bias_total,
        scale_total,
        in_weight_total,
        out_weight_total,
        in_bias_total,
    ) = totals
    grad_scale = 1.0 / math.sqrt(
        row_count * lax.axis_size("lat") * col_count * lax.axis_size("lon")
    )
    channel_grads = grad_scale * jnp.stack(
        [bias_total, gain_total, shift_total, out_bias_total, scale_total]
    )
    return (
        new_state,
        state_grad,
        grad_scale * kernel_total,
        grad_scale * in_weight_total,
        grad_scale * out_weight_total,
        grad_scale * in_bias_total,
        channel_grads,
    )


def solution(mesh):
    placed = (
        P(None, "lat", "lon"),
        P(),
        P(),
        P(),
        P(),
        P(),
        P(),
        P(),
        P(),
        P(),
        P("lat", "lon"),
        P(None, "lat", "lon"),
    )
    return jax.shard_map(
        per_device,
        mesh=mesh,
        in_specs=placed,
        out_specs=(P(None, "lat", "lon"), P(None, "lat", "lon"), P(), P(), P(), P(), P()),
        check_vma=False,
    )
```

profile of v0, /device:TPU:1, one launch (start us, length us, event | category | flops | bytes accessed | tf_op | source)
XLA Modules:
  0.0 568.5 jit_solution(2259703244371274148)
XLA Ops:
  7.2 1.1 fusion.125
  8.3 4.0 collective-permute-start
  12.3 0.8 all_to_all.38
  13.1 10.5 %all-to-all-start = ((f32[32,1,768]{2,1,0:T(1,128)}), f32[32,1,768]{2,1,0:T(1,128)S(1)}, u32[]{:S(2)}, u32[]{:S(2)}) async-start(f32[32,1,768]{2,1,0:T(1,128)} %all_to_all.38), calls=%async_computation | async-start | bytes 196608 | tf_op jit(solution)/shard_map/all_to_all | solution.py:151
  23.6 1.3 collective-permute-start.1
  24.9 0.7 convert_element_type.89
  25.6 0.7 fusion.126
  26.3 2.2 bitcast_convert_fusion
  28.5 0.6 slice_bitcast_fusion.48
  29.2 2.8 all-to-all-done
  32.1 0.7 copy.20
  32.8 5.6 all-to-all-start.1
  38.4 0.7 slice_bitcast_fusion.47
  39.3 7.5 %all-to-all-done.1 = f32[32,1,768]{2,1,0:T(1,128)S(1)} async-done(((f32[32,1,768]{2,1,0:T(1,128)}), f32[32,1,768]{2,1,0:T(1,128)S(1)}, u32[]{:S(2)}, u32[]{:S(2)}) %all-to-all-start.1) | async-done | bytes 98336 | tf_op jit(solution)/shard_map/all_to_all | solution.py:152
  47.6 1.5 fusion.124
  49.1 1.8 copy.21
  50.9 1.9 collective-permute-start.2
  53.4 0.6 slice_bitcast_fusion.46
  56.2 1.6 copy.22
  57.8 1.6 copy.24
  59.4 5.1 maximum_maximum_fusion
  64.6 37.0 %fusion.121 = (f32[32,128]{1,0:T(8,128)S(1)}, f32[64,32,128]{2,1,0:T(8,128)}) fusion(f32[64,38,131]{2,1,0:T(8,128)} %get-tuple-element.148, f32[64]{0:T(128)S(1)} %get-tuple-element.158, f32[64]{0:T(128)S(1)} %get-tuple-element.159, f32[64]{0:T(128)S(1)} %get-tuple-element.160, f32[64,3,128]{2,1,0:T(4,128)S(1)} %broadcast_select_fusion, ...), kind=kLoop, calls=%fused_computation.319 | loop fusion | flops 27521024 | bytes 46363136 | tf_op jit(solution)/shard_map/reduce_sum | solution.py:80
  101.6 1.4 multiply_reduce_fusion.51
  103.0 4.7 multiply_convert_fusion
  107.7 4.5 convert_reduce_fusion
  112.2 1.0 fusion.114
  113.3 1.8 fusion.113
  115.3 8.1 %multiply_reduce_fusion.5 = (f32[64]{0:T(128)}, f32[64]{0:T(128)}, f32[64]{0:T(128)}, f32[64]{0:T(128)}, f32[64]{0:T(128)}, /*index=5*/f32[64]{0:T(128)}, f32[64...) fusion(f32[64,38,131]{2,1,0:T(8,128)S(1)} %get-tuple-element.14, ...), kind=kLoop, calls=%fused_computation.195 | loop fusion | flops 9436032 | bytes 19927552 | tf_op jit(solution)/shard_map/reduce_sum | solution.py:46
  123.8 28.6 %multiply_reduce_fusion.1 = (f32[64]{0:T(128)}, f32[64]{0:T(128)}, f32[64]{0:T(128)}, f32[64]{0:T(128)}, f32[64]{0:T(128)}, /*index=5*/f32[64]{0:T(128)}, f32[64...) fusion(f32[64,38,131]{2,1,0:T(8,128)} %get-tuple-element.148, ...), kind=kLoop, calls=%fused_computation.191 | loop fusion | flops 9436032 | bytes 19927552 | tf_op jit(solution)/shard_map/reduce_sum | solution.py:46
  152.5 1.1 multiply_reduce_fusion.25
  154.0 35.4 %fusion.104 = f32[64,38,134]{2,1,0:T(8,128)S(1)} fusion(f32[64,32,128]{2,1,0:T(8,128)S(1)} %bitcast.300, f32[64]{0:T(128)S(1)} %get-tuple-element.158, f32[64]{0:T(128)S(1)} %copy-done.14, f32[64]{0:T(128)S(1)} %copy-done.16, f32[64]{0:T(128)S(1)} %copy-done.18, f32[64]{0:T(128)S(1)} %copy-done.20, f32[64]{0:T(128)S(1)} %copy-done.22, f32[64]{0:T(128)S(1)} %copy-done.24, ...), kind=kLoop, calls=%fused_computation.160 | loop fusion | flops 31611136 | bytes 2364672 | tf_op jit(solution)/shard_map/add | solution.py:61
  189.4 2.7 fusion.122
  192.1 1.5 slice.995
  193.5 1.5 fusion.120
  195.1 2.4 copy.25
  197.5 1.7 collective-permute-start.4
  199.2 1.8 copy.26
  201.0 2.4 copy.28
  203.4 1.9 collective-permute-start.5
  205.2 1.9 reduce_sum.587
  207.1 3.4 fusion.117
  210.5 4.4 multiply_reduce_fusion
  214.9 0.9 copy.37
  216.1 8.9 %multiply_reduce_fusion.4 = (f32[64]{0:T(128)S(1)}, f32[64]{0:T(128)S(1)}, f32[64]{0:T(128)S(1)}, f32[64]{0:T(128)S(1)}, f32[64]{0:T(128)S(1)}, /*index=5*/f32[6...) fusion(f32[64,3,128]{2,1,0:T(4,128)S(1)} %broadcast_select_fusi, ...), kind=kLoop, calls=%fused_computation.194 | loop fusion | flops 7863552 | bytes 8588288 | tf_op jit(solution)/shard_map/reduce_sum | solution.py:46
  225.6 0.8 add.525
  227.0 7.1 %scatter-add.16 = f32[64,38,128]{2,1,0:T(8,128)} dynamic-update-slice(f32[64,38,128]{2,1,0:T(8,128)} %slice.995, f32[64,38,3]{2,1,0:T(8,128)S(1)} %copy.27, s32[]{:T(128)} %constant.160.clone.1, s32[]{:T(128)} %constant.160.clone.1, s32[]{:T(128)} %constant.160.clone.1) | dynamic-update-slice | bytes 58372 | tf_op jit(solution)/shard_map/scatter-add | solution.py:160
  234.1 1.8 slice.998
  236.4 0.9 add.526
  237.8 21.4 %scatter-add.19 = f32[64,38,128]{2,1,0:T(8,128)S(1)} dynamic-update-slice(f32[64,38,128]{2,1,0:T(8,128)S(1)} %copy-done.5, f32[64,38,3]{2,1,0:T(8,128)S(1)} %copy.30, s32[]{:T(128)} %constant.160.clone.1, s32[]{:T(128)} %constant.160.clone.1, s32[]{:T(128)} %constant.161.clone.1) | dynamic-update-slice | bytes 58372 | tf_op jit(solution)/shard_map/scatter-add | solution.py:161
  259.5 4.3 collective-permute-start.6
  263.7 0.8 all_to_all.39
  264.5 7.6 %all-to-all-start.2 = ((f32[32,1,768]{2,1,0:T(1,128)}), f32[32,1,768]{2,1,0:T(1,128)S(1)}, u32[]{:S(2)}, u32[]{:S(2)}) async-start(f32[32,1,768]{2,1,0:T(1,128)} %all_to_all.39), calls=%async_computation.2 | async-start | bytes 196608 | tf_op jit(solution)/shard_map/all_to_all | solution.py:151
  272.2 1.3 collective-permute-start.7
  273.5 189.0 %all-reduce.5.cloned.1.call-done = (f32[64,256]{1,0:T(8,128)}, f32[256,64]{0,1:T(8,128)}) async-done(((f32[64,256]{1,0:T(8,128)}, f32[256,64]{0,1:T(8,128)}), (f32[64,256]{1,0:T(8,128)}, f32[256,64]{0,1:T(8,128)})) %all-reduce.5.cloned.1.call-update) | async-done | bytes 131088 | tf_op jit(solution)/shard_map/psum | solution.py:223
  462.4 1.5 broadcast_multiply_fusion
  463.9 1.5 broadcast_multiply_fusion.1
  465.6 0.7 copy.32
  466.3 6.6 %all-to-all-start.3 = ((f32[32,1,768]{2,1,0:T(1,128)}), f32[32,1,768]{2,1,0:T(1,128)S(1)}, u32[]{:S(2)}, u32[]{:S(2)}) async-start(f32[32,1,768]{2,1,0:T(1,128)} %copy.32), calls=%async_computation.3 | async-start | bytes 196608 | tf_op jit(solution)/shard_map/all_to_all | solution.py:152
  473.4 7.9 %all-to-all-done.3 = f32[32,1,768]{2,1,0:T(1,128)S(1)} async-done(((f32[32,1,768]{2,1,0:T(1,128)}), f32[32,1,768]{2,1,0:T(1,128)S(1)}, u32[]{:S(2)}, u32[]{:S(2)}) %all-to-all-start.3) | async-done | bytes 98336 | tf_op jit(solution)/shard_map/all_to_all | solution.py:152
  481.9 1.0 select_add_fusion
  483.6 1.6 convert_reduce_fusion.1
  485.3 74.4 %all-reduce.1 = (f32[64,49]{0,1:T(8,128)S(1)}, f32[256]{0:T(256)S(1)}, f32[1,64]{1,0:T(1,128)S(1)}, f32[1,64]{1,0:T(1,128)S(1)}, f32[1,64]{1,0:T(1,128)S(1)}, /*index=5*/f32[1,64]{1,0:T(1,128)S(1)}, f32[1,64]{1,0:T(1,128)S(1)}) all-reduce(f32[64,49]{0,1:T(8,128)S(1)} %stack.217, ...), channel_id=1, replica_groups=mesh['lat'=8,'lon'=32] {'lat','lon'}, use_global_device_ids=true, to_apply=%region_53.54 | all-reduce | flops 3712 | bytes 29696 | tf_op jit(solution)/shard_map/psum | solution.py:223
  559.7 0.6 broadcast_multiply_fusion.6
  560.3 0.6 broadcast_multiply_fusion.2
  (278 shorter events, 8.9 us)
Async XLA Ops:
  7.2 95.8 %copy-start = (bf16[64,256]{1,0:T(8,128)(2,1)S(1)}, bf16[64,256]{1,0:T(8,128)(2,1)}, u32[]{:S(2)}) copy-start(bf16[64,256]{1,0:T(8,128)(2,1)} %param.27) | copy-start | bytes 98308
  7.2 31.9 %copy-start.10 = (bf16[64,32,128]{2,1,0:T(8,128)(2,1)S(1)}, bf16[64,32,128]{2,1,0:T(8,128)(2,1)}, u32[]{:S(2)}) copy-start(bf16[64,32,128]{2,1,0:T(8,128)(2,1)} %param.22) | copy-start | bytes 1572868
  8.3 39.1 %collective-permute-start = (f32[64,3,128]{2,1,0:T(4,128)S(1)}, f32[64,3,128]{2,1,0:T(4,128)S(1)}, u32[]{:S(2)}, u32[]{:S(2)}) collective-permute-start(f32[64,3,128]{2,1,0:T(4,128)S(1)} %get-tuple-element.156), channel_id=1, source_target_pairs={{0,32},{32,64},{64,96},{96,128},{128,160},{160,192},{192,224},{1,3... | collective-permute-start | bytes 294920 | tf_op jit(solution)/shard_map/ppermute | solution.py:20
  13.1 18.9 %all-to-all-start = ((f32[32,1,768]{2,1,0:T(1,128)}), f32[32,1,768]{2,1,0:T(1,128)S(1)}, u32[]{:S(2)}, u32[]{:S(2)}) async-start(f32[32,1,768]{2,1,0:T(1,128)} %all_to_all.38), calls=%async_computation | async-start | bytes 196608 | tf_op jit(solution)/shard_map/all_to_all | solution.py:151
  23.6 23.8 %collective-permute-start.1 = (f32[64,3,128]{2,1,0:T(4,128)S(1)}, f32[64,3,128]{2,1,0:T(4,128)S(1)}, u32[]{:S(2)}, u32[]{:S(2)}) collective-permute-start(f32[64,3,128]{2,1,0:T(4,128)S(1)} %get-tuple-element.155), channel_id=1, source_target_pairs={{32,0},{64,32},{96,64},{128,96},{160,128},{192,160},{224,192},{33,... | collective-permute-start | bytes 294920 | tf_op jit(solution)/shard_map/ppermute | solution.py:21
  29.1 35.4 %copy-start.13 = (f32[64]{0:T(128)}, f32[64]{0:T(128)S(1)}, u32[]{:S(2)}) copy-start(f32[64]{0:T(128)S(1)} %get-tuple-element.159) | copy-start | bytes 772
  29.1 35.4 %copy-start.15 = (f32[64]{0:T(128)}, f32[64]{0:T(128)S(1)}, u32[]{:S(2)}) copy-start(f32[64]{0:T(128)S(1)} %get-tuple-element.160) | copy-start | bytes 772
  29.1 35.4 %copy-start.17 = (f32[64]{0:T(128)}, f32[64]{0:T(128)S(1)}, u32[]{:S(2)}) copy-start(f32[64]{0:T(128)S(1)} %get-tuple-element.161) | copy-start | bytes 772
  29.1 35.4 %copy-start.19 = (f32[64]{0:T(128)}, f32[64]{0:T(128)S(1)}, u32[]{:S(2)}) copy-start(f32[64]{0:T(128)S(1)} %get-tuple-element.162) | copy-start | bytes 772
  29.1 35.4 %copy-start.21 = (f32[64]{0:T(128)}, f32[64]{0:T(128)S(1)}, u32[]{:S(2)}) copy-start(f32[64]{0:T(128)S(1)} %get-tuple-element.163) | copy-start | bytes 772
  29.1 35.4 %copy-start.23 = (f32[64]{0:T(128)}, f32[64]{0:T(128)S(1)}, u32[]{:S(2)}) copy-start(f32[64]{0:T(128)S(1)} %get-tuple-element.164) | copy-start | bytes 772
  29.1 35.4 %copy-start.25 = (f32[64]{0:T(128)}, f32[64]{0:T(128)S(1)}, u32[]{:S(2)}) copy-start(f32[64]{0:T(128)S(1)} %get-tuple-element.165) | copy-start | bytes 772
  29.1 35.4 %copy-start.27 = (f32[64]{0:T(128)}, f32[64]{0:T(128)S(1)}, u32[]{:S(2)}) copy-start(f32[64]{0:T(128)S(1)} %get-tuple-element.166) | copy-start | bytes 772
  29.2 35.4 %copy-start.29 = (f32[64]{0:T(128)}, f32[64]{0:T(128)S(1)}, u32[]{:S(2)}) copy-start(f32[64]{0:T(128)S(1)} %get-tuple-element.167) | copy-start | bytes 772
  32.8 13.9 %all-to-all-start.1 = ((f32[32,1,768]{2,1,0:T(1,128)}), f32[32,1,768]{2,1,0:T(1,128)S(1)}, u32[]{:S(2)}, u32[]{:S(2)}) async-start(f32[32,1,768]{2,1,0:T(1,128)} %copy.20), calls=%async_computation.1 | async-start | bytes 196608 | tf_op jit(solution)/shard_map/all_to_all | solution.py:152
  38.4 424.0 %all-reduce.5.cloned.1.call-start = ((), (), s32[]{:S(2)}) async-start(), calls=%async_computation.4 | async-start | bytes 262144 | tf_op jit(solution)/shard_map/psum | solution.py:223
  50.9 5.2 collective-permute-start.2
  53.3 4.4 collective-permute-start.3
  115.3 38.2 %copy-start.2 = (f32[8,8,32,128]{3,2,1,0:T(8,128)}, f32[8,8,32,128]{3,2,1,0:T(8,128)S(1)}, u32[]{:S(2)}) copy-start(f32[8,8,32,128]{3,2,1,0:T(8,128)S(1)} %copy.39) | copy-start | bytes 3145732
  123.5 30.1 %copy-start.18 = (f32[64]{0:T(128)S(1)}, f32[64]{0:T(128)}, u32[]{:S(2)}) copy-start(f32[64]{0:T(128)} %copy-done.17) | copy-start | bytes 772
  123.5 30.1 %copy-start.20 = (f32[64]{0:T(128)S(1)}, f32[64]{0:T(128)}, u32[]{:S(2)}) copy-start(f32[64]{0:T(128)} %copy-done.19) | copy-start | bytes 772
  123.5 30.1 %copy-start.22 = (f32[64]{0:T(128)S(1)}, f32[64]{0:T(128)}, u32[]{:S(2)}) copy-start(f32[64]{0:T(128)} %copy-done.21) | copy-start | bytes 772
  123.5 30.1 %copy-start.24 = (f32[64]{0:T(128)S(1)}, f32[64]{0:T(128)}, u32[]{:S(2)}) copy-start(f32[64]{0:T(128)} %copy-done.23) | copy-start | bytes 772
  123.5 30.1 %copy-start.26 = (f32[64]{0:T(128)S(1)}, f32[64]{0:T(128)}, u32[]{:S(2)}) copy-start(f32[64]{0:T(128)} %copy-done.25) | copy-start | bytes 772
  123.5 30.1 %copy-start.28 = (f32[64]{0:T(128)S(1)}, f32[64]{0:T(128)}, u32[]{:S(2)}) copy-start(f32[64]{0:T(128)} %copy-done.27) | copy-start | bytes 772
  123.5 30.1 %copy-start.30 = (f32[64]{0:T(128)S(1)}, f32[64]{0:T(128)}, u32[]{:S(2)}) copy-start(f32[64]{0:T(128)} %copy-done.29) | copy-start | bytes 772
  123.5 30.1 %copy-start.32 = (f32[64]{0:T(128)S(1)}, f32[64]{0:T(128)}, u32[]{:S(2)}) copy-start(f32[64]{0:T(128)} %get-tuple-element.168) | copy-start | bytes 772
  123.5 30.1 %copy-start.34 = (f32[64]{0:T(128)S(1)}, f32[64]{0:T(128)}, u32[]{:S(2)}) copy-start(f32[64]{0:T(128)} %get-tuple-element.169) | copy-start | bytes 772
  123.5 30.1 %copy-start.36 = (f32[64]{0:T(128)S(1)}, f32[64]{0:T(128)}, u32[]{:S(2)}) copy-start(f32[64]{0:T(128)} %get-tuple-element.170) | copy-start | bytes 772
  123.6 30.1 %copy-start.37 = (f32[64]{0:T(128)S(1)}, f32[64]{0:T(128)}, u32[]{:S(2)}) copy-start(f32[64]{0:T(128)} %get-tuple-element.171) | copy-start | bytes 772
  123.6 30.1 %copy-start.38 = (f32[64]{0:T(128)S(1)}, f32[64]{0:T(128)}, u32[]{:S(2)}) copy-start(f32[64]{0:T(128)} %get-tuple-element.172) | copy-start | bytes 772
  123.6 30.1 %copy-start.39 = (f32[64]{0:T(128)S(1)}, f32[64]{0:T(128)}, u32[]{:S(2)}) copy-start(f32[64]{0:T(128)} %get-tuple-element.173) | copy-start | bytes 772
  123.6 30.1 %copy-start.40 = (f32[64]{0:T(128)S(1)}, f32[64]{0:T(128)}, u32[]{:S(2)}) copy-start(f32[64]{0:T(128)} %get-tuple-element.174) | copy-start | bytes 772
  123.6 30.1 %copy-start.41 = (f32[64]{0:T(128)S(1)}, f32[64]{0:T(128)}, u32[]{:S(2)}) copy-start(f32[64]{0:T(128)} %get-tuple-element.175) | copy-start | bytes 772
  123.6 30.1 %copy-start.42 = (f32[64]{0:T(128)S(1)}, f32[64]{0:T(128)}, u32[]{:S(2)}) copy-start(f32[64]{0:T(128)} %get-tuple-element.176) | copy-start | bytes 772
  123.6 30.1 %copy-start.43 = (f32[64]{0:T(128)S(1)}, f32[64]{0:T(128)}, u32[]{:S(2)}) copy-start(f32[64]{0:T(128)} %get-tuple-element.177) | copy-start | bytes 772
  123.6 30.1 %copy-start.44 = (f32[64]{0:T(128)S(1)}, f32[64]{0:T(128)}, u32[]{:S(2)}) copy-start(f32[64]{0:T(128)} %get-tuple-element.178) | copy-start | bytes 772
  123.6 30.1 %copy-start.45 = (f32[64]{0:T(128)S(1)}, f32[64]{0:T(128)}, u32[]{:S(2)}) copy-start(f32[64]{0:T(128)} %get-tuple-element.179) | copy-start | bytes 772
  123.6 30.1 %copy-start.46 = (f32[64]{0:T(128)S(1)}, f32[64]{0:T(128)}, u32[]{:S(2)}) copy-start(f32[64]{0:T(128)} %get-tuple-element.180) | copy-start | bytes 772
  123.7 30.1 %copy-start.47 = (f32[64]{0:T(128)S(1)}, f32[64]{0:T(128)}, u32[]{:S(2)}) copy-start(f32[64]{0:T(128)} %get-tuple-element.181) | copy-start | bytes 772
  123.7 30.1 %copy-start.48 = (f32[64]{0:T(128)S(1)}, f32[64]{0:T(128)}, u32[]{:S(2)}) copy-start(f32[64]{0:T(128)} %get-tuple-element.182) | copy-start | bytes 772
  123.7 30.1 %copy-start.49 = (f32[64]{0:T(128)S(1)}, f32[64]{0:T(128)}, u32[]{:S(2)}) copy-start(f32[64]{0:T(128)} %get-tuple-element.183) | copy-start | bytes 772
  123.7 30.1 %copy-start.50 = (f32[64]{0:T(128)S(1)}, f32[64]{0:T(128)}, u32[]{:S(2)}) copy-start(f32[64]{0:T(128)} %get-tuple-element.184) | copy-start | bytes 772
  123.7 30.1 %copy-start.51 = (f32[64]{0:T(128)S(1)}, f32[64]{0:T(128)}, u32[]{:S(2)}) copy-start(f32[64]{0:T(128)} %get-tuple-element.185) | copy-start | bytes 772
  123.7 30.1 %copy-start.52 = (f32[64]{0:T(128)S(1)}, f32[64]{0:T(128)}, u32[]{:S(2)}) copy-start(f32[64]{0:T(128)} %get-tuple-element.186) | copy-start | bytes 772
  123.7 30.1 %copy-start.53 = (f32[64]{0:T(128)S(1)}, f32[64]{0:T(128)}, u32[]{:S(2)}) copy-start(f32[64]{0:T(128)} %get-tuple-element.187) | copy-start | bytes 772
  123.7 30.1 %copy-start.54 = (f32[64]{0:T(128)S(1)}, f32[64]{0:T(128)}, u32[]{:S(2)}) copy-start(f32[64]{0:T(128)} %get-tuple-element.188) | copy-start | bytes 772
  123.7 30.1 %copy-start.55 = (f32[64]{0:T(128)S(1)}, f32[64]{0:T(128)}, u32[]{:S(2)}) copy-start(f32[64]{0:T(128)} %get-tuple-element.189) | copy-start | bytes 772
  123.7 30.1 %copy-start.56 = (f32[64]{0:T(128)S(1)}, f32[64]{0:T(128)}, u32[]{:S(2)}) copy-start(f32[64]{0:T(128)} %get-tuple-element.190) | copy-start | bytes 772
  123.8 30.1 %copy-start.57 = (f32[64]{0:T(128)S(1)}, f32[64]{0:T(128)}, u32[]{:S(2)}) copy-start(f32[64]{0:T(128)} %get-tuple-element.191) | copy-start | bytes 772
  123.8 30.1 %copy-start.58 = (f32[64]{0:T(128)S(1)}, f32[64]{0:T(128)}, u32[]{:S(2)}) copy-start(f32[64]{0:T(128)} %get-tuple-element.192) | copy-start | bytes 772
  123.8 30.1 %copy-start.59 = (f32[64]{0:T(128)S(1)}, f32[64]{0:T(128)}, u32[]{:S(2)}) copy-start(f32[64]{0:T(128)} %get-tuple-element.193) | copy-start | bytes 772
  123.8 30.1 %copy-start.60 = (f32[64]{0:T(128)S(1)}, f32[64]{0:T(128)}, u32[]{:S(2)}) copy-start(f32[64]{0:T(128)} %get-tuple-element.194) | copy-start | bytes 772
  123.8 30.1 %copy-start.61 = (f32[64]{0:T(128)S(1)}, f32[64]{0:T(128)}, u32[]{:S(2)}) copy-start(f32[64]{0:T(128)} %get-tuple-element.195) | copy-start | bytes 772
  123.8 30.1 %copy-start.62 = (f32[64]{0:T(128)S(1)}, f32[64]{0:T(128)}, u32[]{:S(2)}) copy-start(f32[64]{0:T(128)} %get-tuple-element.196) | copy-start | bytes 772
  123.8 30.1 %copy-start.63 = (f32[64]{0:T(128)S(1)}, f32[64]{0:T(128)}, u32[]{:S(2)}) copy-start(f32[64]{0:T(128)} %get-tuple-element.197) | copy-start | bytes 772
  123.8 30.1 %copy-start.64 = (f32[64]{0:T(128)S(1)}, f32[64]{0:T(128)}, u32[]{:S(2)}) copy-start(f32[64]{0:T(128)} %get-tuple-element.198) | copy-start | bytes 772
  197.5 28.2 %collective-permute-start.4 = (f32[64,38,3]{0,1,2:T(8,128)}, f32[64,38,3]{0,1,2:T(8,128)}, u32[]{:S(2)}, u32[]{:S(2)}) collective-permute-start(f32[64,38,3]{0,1,2:T(8,128)} %copy.25), channel_id=1, source_target_pairs={{0,1},{1,2},{2,3},{3,4},{4,5},{5,6},{6,7},{7,8},{8,9},{9,10},{10,1... | collective-permute-start | bytes 87560 | tf_op jit(solution)/shard_map/ppermute | solution.py:20
  203.4 33.0 %collective-permute-start.5 = (f32[64,38,3]{0,1,2:T(8,128)}, f32[64,38,3]{0,1,2:T(8,128)}, u32[]{:S(2)}, u32[]{:S(2)}) collective-permute-start(f32[64,38,3]{0,1,2:T(8,128)} %copy.28), channel_id=1, source_target_pairs={{1,0},{2,1},{3,2},{4,3},{5,4},{6,5},{7,6},{8,7},{9,8},{10,9},{11,1... | collective-permute-start | bytes 87560 | tf_op jit(solution)/shard_map/ppermute | solution.py:21
  259.3 224.3 %copy-start.11 = (bf16[64,32,128]{2,1,0:T(8,128)(2,1)S(1)}, bf16[64,32,128]{2,1,0:T(8,128)(2,1)}, u32[]{:S(2)}) copy-start(bf16[64,32,128]{2,1,0:T(8,128)(2,1)} %param.33) | copy-start | bytes 1572868
  259.5 213.5 %collective-permute-start.6 = (f32[64,3,128]{2,1,0:T(4,128)S(1)}, f32[64,3,128]{2,1,0:T(4,128)S(1)}, u32[]{:S(2)}, u32[]{:S(2)}) collective-permute-start(f32[64,3,128]{2,1,0:T(4,128)S(1)} %get-tuple-element.146), channel_id=1, source_target_pairs={{0,32},{32,64},{64,96},{96,128},{128,160},{160,192},{192,224},{1,3... | collective-permute-start | bytes 294920 | tf_op jit(solution)/shard_map/ppermute | solution.py:20
  264.5 200.9 %all-to-all-start.2 = ((f32[32,1,768]{2,1,0:T(1,128)}), f32[32,1,768]{2,1,0:T(1,128)S(1)}, u32[]{:S(2)}, u32[]{:S(2)}) async-start(f32[32,1,768]{2,1,0:T(1,128)} %all_to_all.39), calls=%async_computation.2 | async-start | bytes 196608 | tf_op jit(solution)/shard_map/all_to_all | solution.py:151
  272.2 209.7 %collective-permute-start.7 = (f32[64,3,128]{2,1,0:T(4,128)S(1)}, f32[64,3,128]{2,1,0:T(4,128)}, u32[]{:S(2)}, u32[]{:S(2)}) collective-permute-start(f32[64,3,128]{2,1,0:T(4,128)S(1)} %get-tuple-element.145), channel_id=1, source_target_pairs={{32,0},{64,32},{96,64},{128,96},{160,128},{192,160},{224,192},{33,... | collective-permute-start | bytes 294920 | tf_op jit(solution)/shard_map/ppermute | solution.py:21
  466.3 15.0 %all-to-all-start.3 = ((f32[32,1,768]{2,1,0:T(1,128)}), f32[32,1,768]{2,1,0:T(1,128)S(1)}, u32[]{:S(2)}, u32[]{:S(2)}) async-start(f32[32,1,768]{2,1,0:T(1,128)} %copy.32), calls=%async_computation.3 | async-start | bytes 196608 | tf_op jit(solution)/shard_map/all_to_all | solution.py:152
  (64 other events, 602.9 us)
Sparse Core Ops, SparseCore 0:
  215.9 246.4 all-reduce.4
where the time goes:
time: 575 us; the launch traced here: 568 us
  waiting for transfers between devices  207 us (36%)
  other arithmetic  145 us (25%)
  blocking collectives  74.4 us (13%)
  local copies, waits for them, and re-layouts  59.6 us (10%)
  starting transfers between devices  46.8 us (8%)
  matrix products  19.5 us (3%)
  between operations  16 us (3%)
    psum x1, waiting for transfers between devices, per_device(): lax.psum((kernel_sum, bias_sum, gain_sum, shift_sum, out_bias_sum, scale_...  189 us
    psum x1, blocking collectives, per_device(): lax.psum((kernel_sum, bias_sum, gain_sum, shift_sum, out_bias_sum, scale_...  74.4 us
    reduce_sum x4, other arithmetic, kernel_grads(): columns.append(jnp.sum(conv_grad * window, axis=(1, 2)))  46.8 us
    reduce_sum x1, other arithmetic, pointwise(): centre = flat_conv - jnp.mean(flat_conv, axis=0, keepdims=True)  37 us
    add x1, other arithmetic, spread_back(): running + weights[:, 7 * row_off + col_off][:, None, None] * window  35.4 us
    scatter-add x1, local copies, waits for them, and re-layouts, fold_columns(): return folded.at[:, :, col_count - 3:].add(col_from[:, :, 9:])  21.4 us
    all_to_all x2, starting transfers between devices, fold_partner(): lax.all_to_all(pieces, 'lon', split_axis=0, concat_axis=0, tiled=True)  18.1 us
    all_to_all x2, waiting for transfers between devices, fold_partner(): lax.all_to_all(scattered[::-1], 'lon', split_axis=0, concat_axis=0, tiled...  15.3 us
  transfers between devices with their start and end apart: 13, of which 4 were waited for; matrix products, arithmetic and copies ran while one was open for 13% of the time, Pallas kernels for 0%

commit v1 on v0

v1 whole, which is shorter than its diff:
```python
import functools
import math

import jax
import jax.numpy as jnp
from jax import lax
from jax.experimental import pallas as pl
from jax.experimental.pallas import tpu as pltpu
from jax.sharding import PartitionSpec as P

slope_coef = 0.044715
tanh_scale = math.sqrt(2.0 / math.pi)
ln_epsilon = 1e-06
f32, bf16 = jnp.float32, jnp.bfloat16

CH, ROWS, COLS, HID = 64, 32, 128, 256
PAD = ROWS + 6
AXES = ("lat", "lon")
VM = pl.BlockSpec(memory_space=pltpu.VMEM)
SM = pl.BlockSpec(memory_space=pltpu.SMEM)
VMEM_LIMIT = 60 * 1024 * 1024


def call(body, out_shape, args, scratch=(), smem_first=False, flops=0, nbytes=0, name=None):
    specs = [VM] * len(args)
    if smem_first:
        specs[0] = SM
    return pl.pallas_call(
        body,
        out_shape=out_shape,
        in_specs=specs,
        out_specs=jax.tree.map(lambda _: VM, out_shape),
        scratch_shapes=list(scratch),
        compiler_params=pltpu.CompilerParams(vmem_limit_bytes=VMEM_LIMIT),
        cost_estimate=pl.CostEstimate(flops=flops, bytes_accessed=nbytes, transcendentals=0),
        name=name,
    )(*args)


def lanes():
    return lax.broadcasted_iota(jnp.int32, (CH, COLS), 1)


def to_rows(src, tall, put):
    def fill(c, carry):
        part = src[pl.ds(c * 8, 8)].astype(f32)
        tall[pl.ds(pl.multiple_of(c * 8 * ROWS, 8 * ROWS), 8 * ROWS), :] = part.reshape(8 * ROWS, COLS)
        return carry

    lax.fori_loop(0, CH // 8, fill, 0)

    def take(r, carry):
        put(r, tall[pl.ds(r, CH, stride=ROWS), :])
        return carry

    lax.fori_loop(0, ROWS, take, 0)


def from_rows(tall, dst):
    def drain(c, carry):
        part = tall[pl.ds(pl.multiple_of(c * 8 * ROWS, 8 * ROWS), 8 * ROWS), :]
        dst[pl.ds(c * 8, 8)] = part.reshape(8, ROWS, COLS).astype(bf16)
        return carry

    lax.fori_loop(0, CH // 8, drain, 0)


def prepare_body(state, cot, mask, state_rows, cot_rows, tall, tall2):
    def put_state(r, value):
        state_rows[r] = value

    def put_cot(r, value):
        cot_rows[r] = value * mask[pl.ds(r, 1), :]

    to_rows(state, tall, put_state)
    to_rows(cot, tall2, put_cot)


def edges_body(flags, from_a, from_b, rows, north, south, to_west, to_east):
    even = flags[0] == 1
    on_top = flags[1] == 1
    for g in range(3):
        south[g] = jnp.where(even, from_b[g], from_a[g])

    @pl.when(jnp.logical_not(on_top))
    def _():
        for g in range(3):
            north[g] = jnp.where(even, from_a[g], from_b[g])

    @pl.when(on_top)
    def _():
        back = COLS - 1 - lanes()
        for g in range(3):
            got = jnp.where(even, from_a[2 - g], from_b[2 - g])
            north[g] = jnp.take_along_axis(got, back, axis=1)

    lane = lanes()

    def pack(spot, value, carry):
        west, east = carry
        here = jnp.logical_and(lane >= 3 * spot, lane < 3 * spot + 3)
        west = jnp.where(here, pltpu.roll(value, 3 * spot, 1), west)
        east = jnp.where(here, pltpu.roll(value, 3 * spot + 3, 1), east)
        return west, east

    carry = (jnp.zeros((CH, COLS), f32), jnp.zeros((CH, COLS), f32))
    for g in range(3):
        carry = pack(g, south[g], carry)
        carry = pack(g + 3 + ROWS, north[g], carry)
    carry = lax.fori_loop(0, ROWS, lambda r, c: pack(r + 3, rows[r], c), carry)
    to_west[...], to_east[...] = carry


def shift_row(shifted, spot, value, west, east, lane):
    west_here = pltpu.roll(west[...], 125 - 3 * spot, 1)
    east_here = pltpu.roll(east[...], lax.rem(COLS - 3 * spot, COLS), 1)
    for b in range(7):
        off = b - 3
        if off == 0:
            shifted[b, spot] = value
        elif off < 0:
            shifted[b, spot] = pltpu.roll(jnp.where(lane >= COLS + off, west_here, value), -off, 1)
        else:
            shifted[b, spot] = pltpu.roll(jnp.where(lane < off, east_here, value), COLS - off, 1)


def shift_all(shifted, rows, south, north, west, east):
    lane = lanes()

    def low(g, carry):
        shift_row(shifted, g, south[g], west, east, lane)
        shift_row(shifted, g + 3 + ROWS, north[g], west, east, lane)
        return carry

    def mid(r, carry):
        shift_row(shifted, r + 3, rows[r], west, east, lane)
        return carry

    lax.fori_loop(0, 3, low, 0)
    lax.fori_loop(0, ROWS, mid, 0)


def taps(shifted, weights, r0, c0, acc, flip):
    rows = acc.shape[0]
    for b in range(7):
        window = shifted[b, pl.ds(r0, rows + 6), pl.ds(c0, 8), :]
        for a in range(7):
            t = 7 * a + b
            t = 48 - t if flip else t
            acc = acc + weights[t, pl.ds(c0, 8), :][None] * window[a : a + rows]
    return acc


def main_body(
    state_rows,
    south,
    north,
    west,
    east,
    cot_rows,
    mask,
    weights,
    chan,
    b_in,
    w_in,
    w_in_t,
    w_out,
    w_out_t,
    new_rows,
    conv_grad,
    sums,
    shifted,
    conv_out,
    win_acc,
    wout_acc,
    bin_acc,
    gain_acc,
    shift_acc,
    obias_acc,
    scale_acc,
):
    shift_all(shifted, state_rows, south, north, west, east)

    def conv_step(i, carry):
        c0 = pl.multiple_of((i // 4) * 8, 8)
        r0 = (i % 4) * 8
        bias = chan[0, pl.ds(c0, 8), :]
        acc = jnp.broadcast_to(bias[None], (8, 8, COLS))
        conv_out[pl.ds(r0, 8), pl.ds(c0, 8), :] = taps(shifted, weights, r0, c0, acc, False)
        return carry

    lax.fori_loop(0, 32, conv_step, 0)

    for acc in (win_acc, wout_acc, bin_acc, gain_acc, shift_acc, obias_acc, scale_acc):
        acc[...] = jnp.zeros_like(acc)

    def wide(x):
        return jnp.concatenate([x, x], axis=1)

    def fold(x):
        return x[:, :COLS] + x[:, COLS:]

    def mean(x):
        return jnp.sum(x, axis=0, keepdims=True) * (1.0 / CH)

    cells = (((1,), (1,)), ((), ()))

    def point_step(g, carry):
        r = 2 * g
        gain, shift, out_bias, scale = (wide(chan[k]) for k in range(1, 5))
        x = jnp.concatenate([conv_out[r], conv_out[r + 1]], axis=1)
        centre = x - mean(x)
        inv_std = lax.rsqrt(mean(centre * centre) + ln_epsilon)
        unit = centre * inv_std
        normed = (unit * gain + shift).astype(bf16)
        masked_cot = jnp.concatenate([cot_rows[r], cot_rows[r + 1]], axis=1)
        mixed_grad = (scale * masked_cot).astype(bf16)
        u = jnp.dot(w_in_t[...], normed, preferred_element_type=f32) + wide(b_in[...])
        hidden_grad = jnp.dot(w_out[...], mixed_grad, preferred_element_type=f32)
        u2 = u * u
        t = jnp.tanh(u * (tanh_scale + (tanh_scale * slope_coef) * u2))
        half = 0.5 * u
        hidden = (half + half * t).astype(bf16)
        slope = 0.5 + 0.5 * t + half * (1.0 - t * t) * (
            tanh_scale + (3.0 * tanh_scale * slope_coef) * u2
        )
        pre_grad = (hidden_grad * slope).astype(bf16)
        bin_acc[...] += fold(pre_grad.astype(f32))
        mixed = jnp.dot(w_out_t[...], hidden, preferred_element_type=f32) + out_bias
        normed_grad = jnp.dot(w_in[...], pre_grad, preferred_element_type=f32)
        win_acc[...] += lax.dot_general(normed, pre_grad, cells, preferred_element_type=f32)
        wout_acc[...] += lax.dot_general(hidden, mixed_grad, cells, preferred_element_type=f32)
        state = jnp.concatenate([state_rows[r], state_rows[r + 1]], axis=1)
        ocean = jnp.concatenate([mask[pl.ds(r, 1), :], mask[pl.ds(r + 1, 1), :]], axis=1)
        new = ocean * (state + scale * mixed)
        new_rows[r] = new[:, :COLS]
        new_rows[r + 1] = new[:, COLS:]
        scale_acc[...] += fold(masked_cot * mixed)
        obias_acc[...] += fold(mixed_grad.astype(f32))
        gain_acc[...] += fold(normed_grad * unit)
        shift_acc[...] += fold(normed_grad)
        q = normed_grad * gain
        grad = inv_std * (q - mean(q) - unit * mean(q * unit))
        conv_grad[r] = grad[:, :COLS]
        conv_grad[r + 1] = grad[:, COLS:]
        return carry

    lax.fori_loop(0, ROWS // 2, point_step, 0)

    lane8 = lax.broadcasted_iota(jnp.int32, (8, COLS), 1)

    def total(x):
        return jnp.broadcast_to(jnp.sum(x, axis=1, keepdims=True), (8, COLS))

    def kernel_step(i, carry):
        c0 = pl.multiple_of(i * 8, 8)
        out = jnp.zeros((8, COLS), f32)
        bias = conv_grad[0, pl.ds(c0, 8), :]
        for r in range(1, ROWS):
            bias = bias + conv_grad[r, pl.ds(c0, 8), :]
        small = (
            bias,
            gain_acc[pl.ds(c0, 8), :],
            shift_acc[pl.ds(c0, 8), :],
            obias_acc[pl.ds(c0, 8), :],
            scale_acc[pl.ds(c0, 8), :],
        ) + tuple(bin_acc[pl.ds(CH * k + c0, 8), :] for k in range(4))
        for k, x in enumerate(small):
            out = jnp.where(lane8 == 49 + k, total(x), out)

        def column(b, out):
            window = [shifted[b, a, pl.ds(c0, 8), :] for a in range(7)]
            acc = None
            for r in range(ROWS):
                grad = conv_grad[r, pl.ds(c0, 8), :]
                terms = [grad * w for w in window]
                acc = terms if acc is None else [p + q for p, q in zip(acc, terms)]
                if r + 1 < ROWS:
                    window = window[1:] + [shifted[b, r + 7, pl.ds(c0, 8), :]]
            for a in range(7):
                out = jnp.where(lane8 == 7 * a + b, total(acc[a]), out)
            return out

        out = lax.fori_loop(0, 7, column, out)
        sums[pl.ds(pl.multiple_of(256 + c0, 8), 8), :] = out
        return carry

    lax.fori_loop(0, CH // 8, kernel_step, 0)
    sums[0:64, :] = win_acc[:, :COLS]
    sums[64:128, :] = win_acc[:, COLS:]
    sums[128:256, :] = jnp.concatenate([wout_acc[0:128, :], wout_acc[128:256, :]], axis=1)


def spread_body(
    flags,
    conv_grad,
    south,
    north,
    west,
    east,
    weights,
    cot_rows,
    new_rows,
    state_grad,
    new_state,
    shifted,
    tall,
):
    def put_new(r, carry):
        tall[pl.ds(r, CH, stride=ROWS), :] = new_rows[r]
        return carry

    lax.fori_loop(0, ROWS, put_new, 0)
    from_rows(tall, new_state)

    shift_all(shifted, conv_grad, south, north, west, east)
    on_top = flags[1] == 1

    def spread_step(i, carry):
        c0 = pl.multiple_of((i // 3) * 8, 8)
        r0 = (i % 3) * 8
        acc = cot_rows[pl.ds(r0, 8), pl.ds(c0, 8), :]
        acc = taps(shifted, weights, r0, c0, acc, True)
        for k in range(8):
            tall[pl.ds(c0 * ROWS + r0 + k, 8, stride=ROWS), :] = acc[k]
        return carry

    lax.fori_loop(0, 24, spread_step, 0)

    def top_step(i, carry):
        c0 = pl.multiple_of(i * 8, 8)
        acc = [cot_rows[24 + k, pl.ds(c0, 8), :] for k in range(8)]
        for b in range(7):
            for p in range(14):
                value = shifted[b, 24 + p, pl.ds(c0, 8), :]
                for k in range(8):
                    a = p - k
                    if not 0 <= a < 7:
                        continue
                    t = 7 * a + b
                    if p < 11:
                        w = weights[48 - t, pl.ds(c0, 8), :]
                    else:
                        w = weights[jnp.where(on_top, t, 48 - t), pl.ds(c0, 8), :]
                    acc[k] = acc[k] + w * value
        for k in range(8):
            tall[pl.ds(c0 * ROWS + 24 + k, 8, stride=ROWS), :] = acc[k]
        return carry

    lax.fori_loop(0, CH // 8, top_step, 0)
    from_rows(tall, state_grad)


def unpack_body(sums, kernel_grad, w_in_grad, w_out_grad, b_in_grad, channel_grads, *, scale):
    w_in_grad[:, :COLS] = sums[0:64, :] * scale
    w_in_grad[:, COLS:] = sums[64:128, :] * scale
    packed = sums[128:256, :] * scale
    w_out_grad[0:128, :] = packed[:, :CH]
    w_out_grad[128:256, :] = packed[:, CH:]
    tail = sums[256:320, :] * scale
    kernel_grad[...] = tail[:, :49]
    turned = jnp.transpose(jnp.concatenate([tail, tail], axis=0))
    channel_grads[...] = turned[49:54, :CH]
    for k in range(4):
        b_in_grad[:, CH * k : CH * k + CH] = turned[54 + k : 55 + k, :CH]


def row_pairs(lat_size, lon_size):
    first, second = [], []
    for i in range(lat_size):
        for j in range(lon_size):
            me = i * lon_size + j
            first.append((me, (i ^ 1) * lon_size + j))
            if i == lat_size - 1:
                second.append((me, i * lon_size + lon_size - 1 - j))
            elif i > 0:
                other = i + 1 if i % 2 else i - 1
                second.append((me, other * lon_size + j))
    return first, second


def exchange_rows(flags, top, bottom):
    first, second = row_pairs(lax.axis_size("lat"), lax.axis_size("lon"))
    even = flags[0] == 1
    from_a = lax.ppermute(jnp.where(even, top, bottom), AXES, first)
    from_b = lax.ppermute(jnp.where(even, bottom, top), AXES, second)
    return from_a, from_b


def settle_edges(flags, from_a, from_b, rows):
    slab = jax.ShapeDtypeStruct((3, CH, COLS), f32)
    flat = jax.ShapeDtypeStruct((CH, COLS), f32)
    return call(
        edges_body,
        (slab, slab, flat, flat),
        (flags, from_a, from_b, rows),
        smem_first=True,
        flops=1 << 20,
        nbytes=1 << 21,
        name="edges",
    )


def exchange_columns(to_west, to_east):
    lon_size = lax.axis_size("lon")
    up = [(j, (j + 1) % lon_size) for j in range(lon_size)]
    down = [(k, j) for j, k in up]
    west = lax.ppermute(to_east, "lon", up)
    east = lax.ppermute(to_west, "lon", down)
    return west, east


def core_pairs():
    return [(i, i ^ 1) for i in range(32)]


def lat_pairs(flip_y, flip_x):
    return [(i, ((i >> 2) ^ flip_x) * 4 + ((i & 3) ^ flip_y)) for i in range(8)]


def reduce_and_spread(sums, flags, conv_grad, finish):
    odd = lax.rem(lax.axis_index("lon"), 2) == 1
    half = sums.shape[0] // 2
    low, high = sums[:half], sums[half:]
    mine = jnp.where(odd, high, low) + lax.ppermute(jnp.where(odd, low, high), "lon", core_pairs())
    groups = [[2 * k + core for k in range(16)] for core in range(2)]
    piece = half // 16

    def swap(x):
        return lax.all_to_all(x, "lon", 0, 0, tiled=True, axis_index_groups=groups)

    from_a, from_b = exchange_rows(flags, conv_grad[ROWS - 3 :], conv_grad[:3])
    got = swap(mine.reshape(16, piece, COLS))
    north, south, to_west, to_east = settle_edges(flags, from_a, from_b, conv_grad)
    got, to_west, to_east = lax.optimization_barrier((got, to_west, to_east))
    part = jnp.sum(got, axis=0)
    west, east = exchange_columns(to_west, to_east)
    for pairs in (lat_pairs(1, 0), lat_pairs(3, 0), lat_pairs(0, 1)):
        part = part + lax.ppermute(part, "lat", pairs)
    part, west, east = lax.optimization_barrier((part, west, east))
    mine = swap(jnp.broadcast_to(part[None], (16, piece, COLS))).reshape(half, COLS)
    done = finish(south, north, west, east)
    mine, done = lax.optimization_barrier((mine, done))
    other = lax.ppermute(mine, "lon", core_pairs())
    total = jnp.concatenate([jnp.where(odd, other, mine), jnp.where(odd, mine, other)], axis=0)
    return total, done


def per_device(
    sea_state,
    conv_kernel,
    conv_bias,
    norm_gain,
    norm_shift,
    w_in,
    b_in,
    w_out,
    b_out,
    layer_scale,
    sea_mask,
    cotangent,
):
    lat_size, lon_size = lax.axis_size("lat"), lax.axis_size("lon")
    lat = lax.axis_index("lat")
    flags = jnp.stack([(lat % 2 == 0).astype(jnp.int32), (lat == lat_size - 1).astype(jnp.int32)])
    rows_shape = jax.ShapeDtypeStruct((ROWS, CH, COLS), f32)
    block = jax.ShapeDtypeStruct((CH, ROWS, COLS), bf16)

    top = jnp.transpose(sea_state[:, ROWS - 3 :, :].astype(f32), (1, 0, 2))
    bottom = jnp.transpose(sea_state[:, :3, :].astype(f32), (1, 0, 2))
    mask = sea_mask.astype(f32)
    tall = pltpu.VMEM((CH * ROWS, COLS), f32)
    state_rows, cot_rows = call(
        prepare_body,
        (rows_shape, rows_shape),
        (sea_state, cotangent, mask),
        [tall, tall],
        flops=1 << 20,
        nbytes=3 << 20,
        name="prepare",
    )
    weights = jnp.broadcast_to(conv_kernel.astype(f32).T[:, :, None], (49, CH, COLS))
    chan = jnp.stack([conv_bias, norm_gain, norm_shift, b_out, layer_scale]).astype(f32)
    chan = jnp.broadcast_to(chan[:, :, None], (5, CH, COLS))
    bias_in = jnp.broadcast_to(b_in.astype(f32)[:, None], (HID, COLS))

    from_a, from_b = exchange_rows(flags, top, bottom)
    north, south, to_west, to_east = settle_edges(flags, from_a, from_b, state_rows)
    halo = (south, north) + exchange_columns(to_west, to_east)
    shifted = pltpu.VMEM((7, PAD, CH, COLS), f32)
    flat = pltpu.VMEM((CH, COLS), f32)
    new_rows, conv_grad, sums = call(
        main_body,
        (rows_shape, rows_shape, jax.ShapeDtypeStruct((320, COLS), f32)),
        (state_rows,)
        + halo
        + (cot_rows, mask, weights, chan, bias_in, w_in, w_in.T, w_out, w_out.T),
        [
            shifted,
            pltpu.VMEM((ROWS, CH, COLS), f32),
            pltpu.VMEM((CH, HID), f32),
            pltpu.VMEM((HID, CH), f32),
            pltpu.VMEM((HID, COLS), f32),
            flat,
            flat,
            flat,
            flat,
        ],
        flops=1 << 30,
        nbytes=8 << 20,
        name="main",
    )

    def finish(*halo):
        return call(
            spread_body,
            (block, block),
            (flags, conv_grad) + halo + (weights, cot_rows, new_rows),
            [shifted, tall],
            smem_first=True,
            flops=1 << 26,
            nbytes=6 << 20,
            name="spread",
        )

    total, (state_grad, new_state) = reduce_and_spread(sums, flags, conv_grad, finish)
    grad_scale = 1.0 / math.sqrt(ROWS * lat_size * COLS * lon_size)
    kernel_grad, w_in_grad, w_out_grad, b_in_grad, channel_grads = call(
        functools.partial(unpack_body, scale=grad_scale),
        (
            jax.ShapeDtypeStruct((CH, 49), f32),
            jax.ShapeDtypeStruct((CH, HID), f32),
            jax.ShapeDtypeStruct((HID, CH), f32),
            jax.ShapeDtypeStruct((1, HID), f32),
            jax.ShapeDtypeStruct((5, CH), f32),
        ),
        (total,),
        flops=1 << 17,
        nbytes=1 << 18,
        name="unpack",
    )
    return (
        new_state,
        state_grad,
        kernel_grad,
        w_in_grad,
        w_out_grad,
        b_in_grad.reshape(HID),
        channel_grads,
    )


def solution(mesh):
    grid = P(None, "lat", "lon")
    placed = (grid,) + (P(),) * 9 + (P("lat", "lon"), grid)
    return jax.shard_map(
        per_device,
        mesh=mesh,
        in_specs=placed,
        out_specs=(grid, grid, P(), P(), P(), P(), P()),
        check_vma=False,
    )
```

time: 575 us -> 147 us (0.26)
  waiting for transfers between devices: 207 us -> 9.71 us
  other arithmetic: 145 us -> 5.48 us
  blocking collectives: 74.4 us -> 0 us
  Pallas kernels: 0 us -> 70.1 us
  local copies, waits for them, and re-layouts: 59.6 us -> 11.5 us
  matrix products: 19.5 us -> 0 us
  between operations: 16 us -> 0.89 us
    psum x1 -> x0, waiting for transfers between devices: 189 us -> none  [per_device(): lax.psum((kernel_sum, bias_sum, gain_sum, shift_sum, out_bias_sum, scale_...]
    reduce_sum x9 -> x1, other arithmetic: 90.5 us -> 0.02 us  [reduce_and_spread(): part = jnp.sum(got, axis=0)]
    psum x1 -> x0, blocking collectives: 74.4 us -> none  [per_device(): lax.psum((kernel_sum, bias_sum, gain_sum, shift_sum, out_bias_sum, scale_...]
    pallas_call x0 -> x6, Pallas kernels: none -> 70.1 us  [call(): pl.pallas_call(body, out_shape=out_shape, in_specs=specs, out_specs=jax.t...]
    add x5 -> x4, other arithmetic: 38.1 us -> 0.95 us  [the longest x1 0.94 us: reduce_and_spread(): jnp.where(odd, high, low)]
    scatter-add x5 -> x0, local copies, waits for them, and re-layouts: 29.7 us -> none  [the longest x1 21.4 us: fold_columns(): return folded.at[:, :, col_count - 3:].add(col_from[:, :, 9:])]
    dot_general x6 -> x0, matrix products: 19.5 us -> none  [the longest x1 4.67 us: pointwise(): jnp.dot(w_in.T, normed, preferred_element_type=jnp.float32)]
    ppermute x8 -> x13, starting transfers between devices: 16.5 us -> 34.6 us  [the longest x3 10.5 us: reduce_and_spread(): part = part + lax.ppermute(part, 'lat', pairs)]
  transfers between devices with their start and end apart: 13 -> 15, of which waited for: 4 -> 7; matrix products, arithmetic and copies ran while one was open for 13% -> 3% of each run, Pallas kernels for 0% -> 20%
where the time goes in v1:
time: 147 us; the launch traced here: 145 us
  Pallas kernels  70.1 us (48%)
  starting transfers between devices  47.3 us (32%)
  local copies, waits for them, and re-layouts  11.5 us (8%)
  waiting for transfers between devices  9.71 us (7%)
  other arithmetic  5.48 us (4%)
    pallas_call x6, Pallas kernels, call(): pl.pallas_call(body, out_shape=out_shape, in_specs=specs, out_specs=jax.t...  70.1 us
    all_to_all x2, starting transfers between devices, swap(): return lax.all_to_all(x, 'lon', 0, 0, tiled=True, axis_index_groups=groups)  12.7 us
    ppermute x3, starting transfers between devices, reduce_and_spread(): part = part + lax.ppermute(part, 'lat', pairs)  10.5 us
    ppermute x2, starting transfers between devices, exchange_rows(): from_a = lax.ppermute(jnp.where(even, top, bottom), AXES, first)  8.58 us
    ppermute x1, starting transfers between devices, reduce_and_spread(): other = lax.ppermute(mine, 'lon', core_pairs())  6.1 us
    unnamed x38, local copies, waits for them, and re-layouts  5.9 us
    ppermute x2, starting transfers between devices, exchange_columns(): west = lax.ppermute(to_east, 'lon', up)  5.49 us
    ppermute x3, waiting for transfers between devices, reduce_and_spread(): part = part + lax.ppermute(part, 'lat', pairs)  3.41 us
  transfers between devices with their start and end apart: 15, of which 7 were waited for; matrix products, arithmetic and copies ran while one was open for 3% of the time, Pallas kernels for 20%

profile of v1, /device:TPU:1, one launch (start us, length us, event | category | flops | bytes accessed | tf_op | source)
XLA Modules:
  0.0 145.0 jit_solution(13100984360126434352)
XLA Ops:
  0.6 0.0 copy-start
  0.7 0.0 copy-start.1
  0.7 1.1 fusion.2
  1.8 0.7 collective-permute-start.1
  2.5 4.7 %collective-permute-start = (f32[3,64,128]{2,1,0:T(8,128)S(1)}, f32[3,64,128]{2,1,0:T(8,128)S(1)}, u32[]{:S(2)}, u32[]{:S(2)}) collective-permute-start(f32[3,64,128]{2,1,0:T(8,128)S(1)} %get-tuple-element.86), channel_id=1, source_target_pairs={{0,32},{1,33},{2,34},{3,35},{4,36},{5,37},{6,38},{7,39},{8,40},{9,... | collective-permute-start | bytes 294920 | tf_op jit(solution)/shard_map/ppermute | solution.py:385
  7.2 1.3 convert_element_type.24.mask
  8.6 5.3 %prepare.1 = (f32[32,64,128]{2,1,0:T(8,128)}, f32[32,64,128]{2,1,0:T(8,128)}) custom-call(bf16[64,32,128]{2,1,0:T(8,128)(2,1)} %state.1, bf16[64,32,128]{2,1,0:T(8,128)(2,1)} %cot.1, f32[32,128]{1,0:T(8,128)} %convert_element_type.24.mask), custom_call_target="tpu_custom_call" | custom-call | flops 1048576 | bytes 3145728 | tf_op jit(solution)/shard_map/prepare/pallas_call | solution.py:28
  13.8 0.6 pad_add_fusion.flags
  14.4 0.0 collective-permute-done.1.from_b
  14.4 0.0 collective-permute-done.from_a
  14.4 0.0 copy-start.3
  14.4 0.6 copy-done.2
  15.1 0.0 copy-done.3
  15.1 4.9 %edges.2 = (f32[3,64,128]{2,1,0:T(8,128)}, f32[3,64,128]{2,1,0:T(8,128)}, f32[64,128]{1,0:T(8,128)}, f32[64,128]{1,0:T(8,128)}) custom-call(s32[2]{0:T(128)} %pad_add_fusion.flags, f32[3,64,128]{2,1,0:T(8,128)} %copy-done.3, f32[3,64,128]{2,1,0:T(8,128)} %copy-done.2, f32[32,64,128]{2,1,0:T(8,128)} %get-tuple-element.36.rows.state_rows), custom_call_target="tpu_custom_call" | custom-call | flops 1048576 | bytes 2097152 | tf_op jit(solution)/shard_map/edges/pallas_call | solution.py:28
  20.0 2.8 %collective-permute-start.2 = (f32[64,128]{1,0:T(8,128)}, f32[64,128]{1,0:T(8,128)S(1)}, u32[]{:S(2)}, u32[]{:S(2)}) collective-permute-start(f32[64,128]{1,0:T(8,128)} %get-tuple-element.39), channel_id=1, source_target_pairs={{0,1},{1,2},{2,3},{3,4},{4,5},{5,6},{6,7},{7,8},{8,9},{9,10},{10,1... | collective-permute-start | bytes 98312 | tf_op jit(solution)/shard_map/ppermute | solution.py:408
  22.7 0.0 collective-permute-start.3
  22.7 0.7 copy.27
  23.5 0.7 copy.28.w_out
  24.2 0.0 copy-done.12
  24.2 0.0 copy-done.16
  24.3 0.0 collective-permute-done.2.west
  24.3 2.0 %collective-permute-done.3.east = f32[64,128]{1,0:T(8,128)S(1)} collective-permute-done((f32[64,128]{1,0:T(8,128)}, f32[64,128]{1,0:T(8,128)S(1)}, u32[]{:S(2)}, u32[]{:S(2)}) %collective-permute-start.3) | collective-permute-done | bytes 32800 | tf_op jit(solution)/shard_map/ppermute | solution.py:409
  26.3 0.7 broadcast_in_dim.10.b_in
  27.0 0.8 broadcast_in_dim.9.chan
  27.8 1.7 %broadcast_in_dim.8.weights = f32[49,64,128]{2,1,0:T(8,128)} broadcast(f32[49,64]{1,0:T(8,128)S(1)} %convert_bitcast_fusion), dimensions={0,1} | broadcast | bytes 1618176 | tf_op jit(solution)/shard_map/broadcast_in_dim | solution.py:482
  29.4 0.0 copy-done.7
  29.5 35.2 %main.1 = (f32[32,64,128]{2,1,0:T(8,128)}, f32[32,64,128]{2,1,0:T(8,128)}, f32[320,128]{1,0:T(8,128)}) custom-call(f32[32,64,128]{2,1,0:T(8,128)} %get-tuple-element.36.rows.state_rows, f32[3,64,128]{2,1,0:T(8,128)} %get-tuple-element.37.south, f32[3,64,128]{2,1,0:T(8,128)} %get-tuple-element.38.north, f32[64,128]{1,0:T(8,128)} %copy-done.6, ...), custom_call_target="tpu_custom_call" | custom-call | flops 1073741824 | bytes 8388608 | tf_op jit(solution)/shard_map/main/pallas_call | solution.py:28
  64.7 0.9 slice_select_fusion.2
  65.6 2.6 %collective-permute-start.4 = (f32[160,128]{1,0:T(8,128)S(1)}, f32[160,128]{1,0:T(8,128)S(1)}, u32[]{:S(2)}, u32[]{:S(2)}) collective-permute-start(f32[160,128]{1,0:T(8,128)S(1)} %slice_select_fusion.2), channel_id=1, source_target_pairs={{0,1},{1,0},{2,3},{3,2},{4,5},{5,4},{6,7},{7,6},{8,9},{9,8},{10,11... | collective-permute-start | bytes 245768 | tf_op jit(solution)/shard_map/ppermute | solution.py:425
  68.3 0.9 collective-permute-done.4
  69.2 0.9 select_add_fusion
  70.1 0.7 reshape.67
  70.8 6.9 %all-to-all-start = ((f32[16,10,128]{2,1,0:T(8,128)}), f32[16,10,128]{2,1,0:T(8,128)S(1)}, u32[]{:S(2)}, u32[]{:S(2)}) async-start(f32[16,10,128]{2,1,0:T(8,128)} %reshape.67), calls=%async_computation | async-start | bytes 262144 | tf_op jit(solution)/shard_map/all_to_all | solution.py:430
  77.7 1.0 slice_select_fusion
  78.6 0.7 collective-permute-start.6
  79.3 3.8 %collective-permute-start.5 = (f32[3,64,128]{2,1,0:T(8,128)S(1)}, f32[3,64,128]{2,1,0:T(8,128)S(1)}, u32[]{:S(2)}, u32[]{:S(2)}) collective-permute-start(f32[3,64,128]{2,1,0:T(8,128)S(1)} %get-tuple-element.80), channel_id=1, source_target_pairs={{0,32},{1,33},{2,34},{3,35},{4,36},{5,37},{6,38},{7,39},{8,40},{9,... | collective-permute-start | bytes 294920 | tf_op jit(solution)/shard_map/ppermute | solution.py:385
  83.2 0.0 collective-permute-done.6.from_b
  83.2 2.5 %collective-permute-done.5.from_a = f32[3,64,128]{2,1,0:T(8,128)S(1)} collective-permute-done((f32[3,64,128]{2,1,0:T(8,128)S(1)}, f32[3,64,128]{2,1,0:T(8,128)S(1)}, u32[]{:S(2)}, u32[]{:S(2)}) %collective-permute-start.5) | collective-permute-done | bytes 98336 | tf_op jit(solution)/shard_map/ppermute | solution.py:385
  85.6 0.6 copy-done.5
  86.3 4.8 %edges.3 = (f32[3,64,128]{2,1,0:T(8,128)}, f32[3,64,128]{2,1,0:T(8,128)}, f32[64,128]{1,0:T(8,128)}, f32[64,128]{1,0:T(8,128)}) custom-call(s32[2]{0:T(128)} %pad_add_fusion.flags, f32[3,64,128]{2,1,0:T(8,128)} %copy-done.5, f32[3,64,128]{2,1,0:T(8,128)} %copy-done.4, f32[32,64,128]{2,1,0:T(8,128)} %get-tuple-element.43.rows.conv_grad), custom_call_target="tpu_custom_call" | custom-call | flops 1048576 | bytes 2097152 | tf_op jit(solution)/shard_map/edges/pallas_call | solution.py:28
  91.1 0.0 all-to-all-done
  91.1 2.7 %collective-permute-start.10 = (f32[64,128]{1,0:T(8,128)}, f32[64,128]{1,0:T(8,128)S(1)}, u32[]{:S(2)}, u32[]{:S(2)}) collective-permute-start(f32[64,128]{1,0:T(8,128)} %get-tuple-element.47), channel_id=1, source_target_pairs={{0,1},{1,2},{2,3},{3,4},{4,5},{5,6},{6,7},{7,8},{8,9},{9,10},{10,1... | collective-permute-start | bytes 98312 | tf_op jit(solution)/shard_map/ppermute | solution.py:408
  93.8 0.0 collective-permute-start.11
  93.9 1.8 %collective-permute-start.7 = (f32[10,128]{1,0:T(8,128)S(1)}, f32[10,128]{1,0:T(8,128)S(1)}, u32[]{:S(2)}, u32[]{:S(2)}) collective-permute-start(f32[10,128]{1,0:T(8,128)S(1)} %reduce_sum.9), channel_id=1, source_target_pairs={{0,32},{32,0},{64,96},{96,64},{128,160},{160,128},{192,224},{224,1... | collective-permute-start | bytes 15368 | tf_op jit(solution)/shard_map/ppermute | solution.py:439
  95.7 1.3 collective-permute-done.7
  97.0 4.3 %collective-permute-start.8 = (f32[10,128]{1,0:T(8,128)S(1)}, f32[10,128]{1,0:T(8,128)S(1)}, u32[]{:S(2)}, u32[]{:S(2)}) collective-permute-start(f32[10,128]{1,0:T(8,128)S(1)} %add.18), channel_id=1, source_target_pairs={{0,96},{32,64},{64,32},{96,0},{128,224},{160,192},{192,160},{224,1... | collective-permute-start | bytes 15368 | tf_op jit(solution)/shard_map/ppermute | solution.py:439
  101.3 1.0 collective-permute-done.8
  102.4 4.4 %collective-permute-start.9 = (f32[10,128]{1,0:T(8,128)S(1)}, f32[10,128]{1,0:T(8,128)S(1)}, u32[]{:S(2)}, u32[]{:S(2)}) collective-permute-start(f32[10,128]{1,0:T(8,128)S(1)} %add.19), channel_id=1, source_target_pairs={{0,128},{32,160},{64,192},{96,224},{128,0},{160,32},{192,64},{224,... | collective-permute-start | bytes 15368 | tf_op jit(solution)/shard_map/ppermute | solution.py:439
  106.7 1.0 collective-permute-done.9
  107.8 0.0 collective-permute-done.10.west
  107.8 0.0 collective-permute-done.11.east
  107.8 0.0 copy-start.9
  107.8 0.7 broadcast_in_dim.11
  108.5 5.8 %all-to-all-start.1 = ((f32[16,10,128]{2,1,0:T(8,128)}), f32[16,10,128]{2,1,0:T(8,128)S(1)}, u32[]{:S(2)}, u32[]{:S(2)}) async-start(f32[16,10,128]{2,1,0:T(8,128)} %broadcast_in_dim.11), calls=%async_computation.1 | async-start | bytes 262144 | tf_op jit(solution)/shard_map/all_to_all | solution.py:430
  114.3 0.0 copy-done.8
  114.3 0.0 copy-done.9
  114.3 18.2 %spread.1 = (bf16[64,32,128]{2,1,0:T(8,128)(2,1)}, bf16[64,32,128]{2,1,0:T(8,128)(2,1)}) custom-call(s32[2]{0:T(128)} %pad_add_fusion.flags, f32[32,64,128]{2,1,0:T(8,128)} %get-tuple-element.43.rows.conv_grad, f32[3,64,128]{2,1,0:T(8,128)} %get-tuple-element.50.south, f32[3,64,128]{2,1,0:T(8,128)} %get-tuple-element.51.north, f32[64,128]{1,0:T(8,128)} %copy-done.8, ...), custom_call_target="tpu_custom_call" | custom-call | flops 67108864 | bytes 6291456 | tf_op jit(solution)/shard_map/spread/pallas_call | solution.py:28
  132.5 0.0 all-to-all-done.1
  132.5 6.1 %collective-permute-start.12 = (f32[160,128]{1,0:T(8,128)S(1)}, f32[160,128]{1,0:T(8,128)S(1)}, u32[]{:S(2)}, u32[]{:S(2)}) collective-permute-start(f32[160,128]{1,0:T(8,128)S(1)} %reshape.68), channel_id=1, source_target_pairs={{0,1},{1,0},{2,3},{3,2},{4,5},{5,4},{6,7},{7,6},{8,9},{9,8},{10,11... | collective-permute-start | bytes 245768 | tf_op jit(solution)/shard_map/ppermute | solution.py:444
  138.6 0.9 collective-permute-done.12
  139.5 0.7 pad_maximum_fusion.sums
  140.2 1.7 %unpack.1 = (f32[64,49]{1,0:T(8,128)}, f32[64,256]{1,0:T(8,128)}, f32[256,64]{1,0:T(8,128)}, f32[1,256]{1,0:T(1,128)}, f32[5,64]{1,0:T(8,128)}) custom-call(f32[320,128]{1,0:T(8,128)} %pad_maximum_fusion.sums), custom_call_target="tpu_custom_call" | custom-call | flops 131072 | bytes 262144 | tf_op jit(solution)/shard_map/unpack/pallas_call | solution.py:28
  141.9 1.5 %copy.29 = f32[64,49]{0,1:T(8,128)} copy(f32[64,49]{1,0:T(8,128)} %get-tuple-element.74) | data formatting | bytes 25088
  143.4 1.6 %copy.30 = f32[256,64]{0,1:T(8,128)} copy(f32[256,64]{1,0:T(8,128)} %get-tuple-element.76) | data formatting | bytes 131072
  (31 shorter events, 0.2 us)
Async XLA Ops:
  0.6 22.1 %copy-start.10 = (bf16[64,49]{0,1:T(8,128)(2,1)S(1)}, bf16[64,49]{0,1:T(8,128)(2,1)}, u32[]{:S(2)}) copy-start(bf16[64,49]{0,1:T(8,128)(2,1)} %param.13) | copy-start | bytes 18820
  0.6 22.1 %copy-start = (bf16[64,256]{1,0:T(8,128)(2,1)S(1)}, bf16[64,256]{1,0:T(8,128)(2,1)}, u32[]{:S(2)}) copy-start(bf16[64,256]{1,0:T(8,128)(2,1)} %w_in.1) | copy-start | bytes 98308
  0.7 22.8 %copy-start.1 = (bf16[256,64]{0,1:T(8,128)(2,1)S(1)}, bf16[256,64]{0,1:T(8,128)(2,1)}, u32[]{:S(2)}) copy-start(bf16[256,64]{0,1:T(8,128)(2,1)} %param.19) | copy-start | bytes 98308
  0.7 23.5 %copy-start.12 = (bf16[64]{0:T(256)(128)(2,1)S(1)}, bf16[64]{0:T(256)(128)(2,1)}, u32[]{:S(2)}) copy-start(bf16[64]{0:T(256)(128)(2,1)} %param.14) | copy-start | bytes 388
  0.7 23.5 %copy-start.13 = (bf16[64]{0:T(256)(128)(2,1)S(1)}, bf16[64]{0:T(256)(128)(2,1)}, u32[]{:S(2)}) copy-start(bf16[64]{0:T(256)(128)(2,1)} %param.15) | copy-start | bytes 388
  0.7 23.5 %copy-start.14 = (bf16[64]{0:T(256)(128)(2,1)S(1)}, bf16[64]{0:T(256)(128)(2,1)}, u32[]{:S(2)}) copy-start(bf16[64]{0:T(256)(128)(2,1)} %param.16) | copy-start | bytes 388
  0.7 23.5 %copy-start.15 = (bf16[64]{0:T(256)(128)(2,1)S(1)}, bf16[64]{0:T(256)(128)(2,1)}, u32[]{:S(2)}) copy-start(bf16[64]{0:T(256)(128)(2,1)} %param.20) | copy-start | bytes 388
  0.7 23.5 %copy-start.16 = (bf16[64]{0:T(256)(128)(2,1)S(1)}, bf16[64]{0:T(256)(128)(2,1)}, u32[]{:S(2)}) copy-start(bf16[64]{0:T(256)(128)(2,1)} %param.21) | copy-start | bytes 388
  0.7 25.5 %copy-start.11 = (bf16[256]{0:T(256)(128)(2,1)S(1)}, bf16[256]{0:T(256)(128)(2,1)}, u32[]{:S(2)}) copy-start(bf16[256]{0:T(256)(128)(2,1)} %param.18) | copy-start | bytes 1540
  1.8 12.6 %collective-permute-start.1 = (f32[3,64,128]{2,1,0:T(8,128)S(1)}, f32[3,64,128]{2,1,0:T(8,128)S(1)}, u32[]{:S(2)}, u32[]{:S(2)}) collective-permute-start(f32[3,64,128]{2,1,0:T(8,128)S(1)} %get-tuple-element.85), channel_id=1, source_target_pairs={{32,64},{33,65},{34,66},{35,67},{36,68},{37,69},{38,70},{39,71},{4... | collective-permute-start | bytes 294920 | tf_op jit(solution)/shard_map/ppermute | solution.py:386
  2.5 11.9 %collective-permute-start = (f32[3,64,128]{2,1,0:T(8,128)S(1)}, f32[3,64,128]{2,1,0:T(8,128)S(1)}, u32[]{:S(2)}, u32[]{:S(2)}) collective-permute-start(f32[3,64,128]{2,1,0:T(8,128)S(1)} %get-tuple-element.86), channel_id=1, source_target_pairs={{0,32},{1,33},{2,34},{3,35},{4,36},{5,37},{6,38},{7,39},{8,40},{9,... | collective-permute-start | bytes 294920 | tf_op jit(solution)/shard_map/ppermute | solution.py:385
  14.4 0.6 copy-start.2
  14.4 0.7 copy-start.3
  20.0 4.3 %collective-permute-start.2 = (f32[64,128]{1,0:T(8,128)}, f32[64,128]{1,0:T(8,128)S(1)}, u32[]{:S(2)}, u32[]{:S(2)}) collective-permute-start(f32[64,128]{1,0:T(8,128)} %get-tuple-element.39), channel_id=1, source_target_pairs={{0,1},{1,2},{2,3},{3,4},{4,5},{5,6},{6,7},{7,8},{8,9},{9,10},{10,1... | collective-permute-start | bytes 98312 | tf_op jit(solution)/shard_map/ppermute | solution.py:408
  22.7 3.6 %collective-permute-start.3 = (f32[64,128]{1,0:T(8,128)}, f32[64,128]{1,0:T(8,128)S(1)}, u32[]{:S(2)}, u32[]{:S(2)}) collective-permute-start(f32[64,128]{1,0:T(8,128)} %get-tuple-element.40), channel_id=1, source_target_pairs={{1,0},{2,1},{3,2},{4,3},{5,4},{6,5},{7,6},{8,7},{9,8},{10,9},{11,1... | collective-permute-start | bytes 98312 | tf_op jit(solution)/shard_map/ppermute | solution.py:409
  24.3 5.2 %copy-start.6 = (f32[64,128]{1,0:T(8,128)}, f32[64,128]{1,0:T(8,128)S(1)}, u32[]{:S(2)}) copy-start(f32[64,128]{1,0:T(8,128)S(1)} %collective-permute-done.2.west) | copy-start | bytes 98308
  26.3 3.2 %copy-start.7 = (f32[64,128]{1,0:T(8,128)}, f32[64,128]{1,0:T(8,128)S(1)}, u32[]{:S(2)}) copy-start(f32[64,128]{1,0:T(8,128)S(1)} %collective-permute-done.3.east) | copy-start | bytes 98308
  65.6 3.6 %collective-permute-start.4 = (f32[160,128]{1,0:T(8,128)S(1)}, f32[160,128]{1,0:T(8,128)S(1)}, u32[]{:S(2)}, u32[]{:S(2)}) collective-permute-start(f32[160,128]{1,0:T(8,128)S(1)} %slice_select_fusion.2), channel_id=1, source_target_pairs={{0,1},{1,0},{2,3},{3,2},{4,5},{5,4},{6,7},{7,6},{8,9},{9,8},{10,11... | collective-permute-start | bytes 245768 | tf_op jit(solution)/shard_map/ppermute | solution.py:425
  70.8 20.3 %all-to-all-start = ((f32[16,10,128]{2,1,0:T(8,128)}), f32[16,10,128]{2,1,0:T(8,128)S(1)}, u32[]{:S(2)}, u32[]{:S(2)}) async-start(f32[16,10,128]{2,1,0:T(8,128)} %reshape.67), calls=%async_computation | async-start | bytes 262144 | tf_op jit(solution)/shard_map/all_to_all | solution.py:430
  78.6 4.5 %collective-permute-start.6 = (f32[3,64,128]{2,1,0:T(8,128)S(1)}, f32[3,64,128]{2,1,0:T(8,128)S(1)}, u32[]{:S(2)}, u32[]{:S(2)}) collective-permute-start(f32[3,64,128]{2,1,0:T(8,128)S(1)} %get-tuple-element.79), channel_id=1, source_target_pairs={{32,64},{33,65},{34,66},{35,67},{36,68},{37,69},{38,70},{39,71},{4... | collective-permute-start | bytes 294920 | tf_op jit(solution)/shard_map/ppermute | solution.py:386
  79.3 6.3 %collective-permute-start.5 = (f32[3,64,128]{2,1,0:T(8,128)S(1)}, f32[3,64,128]{2,1,0:T(8,128)S(1)}, u32[]{:S(2)}, u32[]{:S(2)}) collective-permute-start(f32[3,64,128]{2,1,0:T(8,128)S(1)} %get-tuple-element.80), channel_id=1, source_target_pairs={{0,32},{1,33},{2,34},{3,35},{4,36},{5,37},{6,38},{7,39},{8,40},{9,... | collective-permute-start | bytes 294920 | tf_op jit(solution)/shard_map/ppermute | solution.py:385
  83.2 2.5 %copy-start.4 = (f32[3,64,128]{2,1,0:T(8,128)}, f32[3,64,128]{2,1,0:T(8,128)S(1)}, u32[]{:S(2)}) copy-start(f32[3,64,128]{2,1,0:T(8,128)S(1)} %collective-permute-done.6.from_b) | copy-start | bytes 294916
  85.6 0.6 copy-start.5
  91.1 16.7 %collective-permute-start.10 = (f32[64,128]{1,0:T(8,128)}, f32[64,128]{1,0:T(8,128)S(1)}, u32[]{:S(2)}, u32[]{:S(2)}) collective-permute-start(f32[64,128]{1,0:T(8,128)} %get-tuple-element.47), channel_id=1, source_target_pairs={{0,1},{1,2},{2,3},{3,4},{4,5},{5,6},{6,7},{7,8},{8,9},{9,10},{10,1... | collective-permute-start | bytes 98312 | tf_op jit(solution)/shard_map/ppermute | solution.py:408
  93.8 13.9 %collective-permute-start.11 = (f32[64,128]{1,0:T(8,128)}, f32[64,128]{1,0:T(8,128)S(1)}, u32[]{:S(2)}, u32[]{:S(2)}) collective-permute-start(f32[64,128]{1,0:T(8,128)} %get-tuple-element.48), channel_id=1, source_target_pairs={{1,0},{2,1},{3,2},{4,3},{5,4},{6,5},{7,6},{8,7},{9,8},{10,9},{11,1... | collective-permute-start | bytes 98312 | tf_op jit(solution)/shard_map/ppermute | solution.py:409
  93.9 3.2 %collective-permute-start.7 = (f32[10,128]{1,0:T(8,128)S(1)}, f32[10,128]{1,0:T(8,128)S(1)}, u32[]{:S(2)}, u32[]{:S(2)}) collective-permute-start(f32[10,128]{1,0:T(8,128)S(1)} %reduce_sum.9), channel_id=1, source_target_pairs={{0,32},{32,0},{64,96},{96,64},{128,160},{160,128},{192,224},{224,1... | collective-permute-start | bytes 15368 | tf_op jit(solution)/shard_map/ppermute | solution.py:439
  97.0 5.3 %collective-permute-start.8 = (f32[10,128]{1,0:T(8,128)S(1)}, f32[10,128]{1,0:T(8,128)S(1)}, u32[]{:S(2)}, u32[]{:S(2)}) collective-permute-start(f32[10,128]{1,0:T(8,128)S(1)} %add.18), channel_id=1, source_target_pairs={{0,96},{32,64},{64,32},{96,0},{128,224},{160,192},{192,160},{224,1... | collective-permute-start | bytes 15368 | tf_op jit(solution)/shard_map/ppermute | solution.py:439
  102.4 5.4 %collective-permute-start.9 = (f32[10,128]{1,0:T(8,128)S(1)}, f32[10,128]{1,0:T(8,128)S(1)}, u32[]{:S(2)}, u32[]{:S(2)}) collective-permute-start(f32[10,128]{1,0:T(8,128)S(1)} %add.19), channel_id=1, source_target_pairs={{0,128},{32,160},{64,192},{96,224},{128,0},{160,32},{192,64},{224,... | collective-permute-start | bytes 15368 | tf_op jit(solution)/shard_map/ppermute | solution.py:439
  107.8 6.5 %copy-start.8 = (f32[64,128]{1,0:T(8,128)}, f32[64,128]{1,0:T(8,128)S(1)}, u32[]{:S(2)}) copy-start(f32[64,128]{1,0:T(8,128)S(1)} %collective-permute-done.10.west) | copy-start | bytes 98308
  107.8 6.5 %copy-start.9 = (f32[64,128]{1,0:T(8,128)}, f32[64,128]{1,0:T(8,128)S(1)}, u32[]{:S(2)}) copy-start(f32[64,128]{1,0:T(8,128)S(1)} %collective-permute-done.11.east) | copy-start | bytes 98308
  108.5 24.0 %all-to-all-start.1 = ((f32[16,10,128]{2,1,0:T(8,128)}), f32[16,10,128]{2,1,0:T(8,128)S(1)}, u32[]{:S(2)}, u32[]{:S(2)}) async-start(f32[16,10,128]{2,1,0:T(8,128)} %broadcast_in_dim.11), calls=%async_computation.1 | async-start | bytes 262144 | tf_op jit(solution)/shard_map/all_to_all | solution.py:430
  132.5 7.0 %collective-permute-start.12 = (f32[160,128]{1,0:T(8,128)S(1)}, f32[160,128]{1,0:T(8,128)S(1)}, u32[]{:S(2)}, u32[]{:S(2)}) collective-permute-start(f32[160,128]{1,0:T(8,128)S(1)} %reshape.68), channel_id=1, source_target_pairs={{0,1},{1,0},{2,3},{3,2},{4,5},{5,4},{6,7},{7,6},{8,9},{9,8},{10,11... | collective-permute-start | bytes 245768 | tf_op jit(solution)/shard_map/ppermute | solution.py:444

commit v2 on v1

v2 whole, which is shorter than its diff:
```python
import functools
import math

import jax
import jax.numpy as jnp
import numpy as np
from jax import lax
from jax.experimental import pallas as pl
from jax.experimental.pallas import tpu as pltpu
from jax.sharding import PartitionSpec as P

slope_coef = 0.044715
tanh_scale = math.sqrt(2.0 / math.pi)
ln_epsilon = 1e-06
f32, bf16 = jnp.float32, jnp.bfloat16

CH, ROWS, COLS, HID = 64, 32, 128, 256
AXES = ("lat", "lon")
VM = pl.BlockSpec(memory_space=pltpu.VMEM)
SM = pl.BlockSpec(memory_space=pltpu.SMEM)
PITCH = ROWS + 1
SPAN = 40
NEAR = 9
PART = 16


def call(body, out_shape, args, scratch=(), smem_first=False, flops=0, nbytes=0, name=None, mib=8):
    specs = [VM] * len(args)
    if smem_first:
        specs[0] = SM
    return pl.pallas_call(
        body,
        out_shape=out_shape,
        in_specs=specs,
        out_specs=jax.tree.map(lambda _: VM, out_shape),
        scratch_shapes=list(scratch),
        compiler_params=pltpu.CompilerParams(vmem_limit_bytes=mib * 1024 * 1024),
        cost_estimate=pl.CostEstimate(flops=flops, bytes_accessed=nbytes, transcendentals=0),
        name=name,
    )(*args)


def iota(shape, dim):
    return lax.broadcasted_iota(jnp.int32, shape, dim)


def by_channel(step, group=8, count=CH):
    def run(i, carry):
        for j in range(group):
            step(i * group, j)
        return carry

    lax.fori_loop(0, count // group, run, 0)


def pitched(ref, base, j):
    return ref.at[pl.ds(pl.multiple_of(base * PITCH, 8) + j * PITCH, ROWS), :]


def row_of(ref, r):
    return ref.at[pl.ds(r, CH, stride=PITCH), :]


def near_fill(near, north, south):
    near[...] = jnp.zeros_like(near)
    count = north.shape[1]
    for g in range(3):
        near[pl.ds(g, count, stride=NEAR), :] = north[g]
        near[pl.ds(5 + g, count, stride=NEAR), :] = south[g]


def edges_body(flags, from_a, from_b, own, north, south, to_west, to_east, near):
    even = flags[0] == 1
    on_top = flags[1] == 1
    for g in range(3):
        south[g] = jnp.where(even, from_b[g], from_a[g])

    @pl.when(jnp.logical_not(on_top))
    def _():
        for g in range(3):
            north[g] = jnp.where(even, from_a[g], from_b[g])

    @pl.when(on_top)
    def _():
        back = COLS - 1 - iota((CH, COLS), 1)
        for g in range(3):
            got = jnp.where(even, from_a[2 - g], from_b[2 - g])
            north[g] = jnp.take_along_axis(got, back, axis=1)

    near_fill(near, north, south)
    lane = iota((SPAN, COLS), 1)
    for t in range(2):
        west = jnp.zeros((SPAN, COLS), f32)
        east = jnp.zeros((SPAN, COLS), f32)
        for m in range(32):
            k = 32 * t + m
            mine = own[k * PITCH : k * PITCH + ROWS, :] if len(own.shape) == 2 else own[k].astype(f32)
            value = jnp.concatenate([mine, near[k * NEAR : k * NEAR + 8, :]], axis=0)
            here = jnp.logical_and(lane >= 3 * m, lane < 3 * m + 3)
            west = jnp.where(here, pltpu.roll(value, 3 * m, 1) if m else value, west)
            east = jnp.where(here, pltpu.roll(value, 3 * m + 3, 1), east)
        to_west[t] = west
        to_east[t] = east


def build_shifted(shifted, own, near, west, east, count, find):
    lane = iota((SPAN, COLS), 1)
    blank = jnp.zeros((8, COLS), f32)

    def step(base, j):
        k = base + j
        value = jnp.concatenate([own(base, j), near[pl.ds(base * NEAR + j * NEAR, 8), :]], axis=0)
        t, m = find(base, j)
        from_west = pltpu.roll(west[t], 125 - 3 * m, 1)
        from_east = pltpu.roll(east[t], lax.rem(COLS - 3 * m, COLS), 1)
        for b in range(7):
            off = b - 3
            if off == 0:
                v = value
            elif off < 0:
                v = pltpu.roll(jnp.where(lane >= COLS + off, from_west, value), -off, 1)
            else:
                v = pltpu.roll(jnp.where(lane < off, from_east, value), COLS - off, 1)
            p, g = divmod(b, 2)
            mine, other = 128 * p + 64 * g, 128 * p + 64 * (1 - g)
            edge = v[ROWS:]
            shifted[k, mine : mine + 32, :] = v[:ROWS].astype(bf16)
            shifted[k, mine + 32 : mine + 48, :] = jnp.concatenate([edge, blank], 0).astype(bf16)
            shifted[k, other + 48 : other + 64, :] = jnp.concatenate([blank, edge], 0).astype(bf16)
        zero = jnp.zeros((16, COLS), bf16)
        for spot in (384 + 48, 384 + 64, 384 + 80, 384 + 96):
            shifted[k, spot : spot + 16, :] = zero

    by_channel(step, 4, count)


def banded(taps, base, j):
    rows = taps[pl.ds(pl.multiple_of(base, 8), 8), :]
    tiles = []
    for p in range(4):
        row = jnp.broadcast_to(rows[j : j + 1, 128 * p : 128 * p + 128], (8, COLS))
        parts = [pltpu.roll(row, 8 * i, 1, stride=1, stride_axis=0) for i in range(4)]
        tiles.append(jnp.concatenate(parts, axis=0))
    return jnp.concatenate(tiles, axis=1)


def main_body(
    state,
    south,
    north,
    west,
    east,
    cot,
    mask,
    taps,
    chan,
    w_in,
    w_in_t,
    w_out,
    w_out_t,
    delta,
    conv_grad,
    top,
    bottom,
    sums,
    shifted,
    near,
    conv_out,
    cot_rows,
    grad_back,
    win_acc,
    wout_acc,
    gain_acc,
    shift_acc,
    obias_acc,
    scale_acc,
    taps_acc,
):
    near_fill(near, north, south)
    build_shifted(
        shifted,
        lambda base, j: state[base + j].astype(f32),
        near,
        west,
        east,
        CH,
        lambda base, j: (base // 32, lax.rem(base, 32) + j),
    )

    def conv_step(base, j):
        k = base + j
        out = jnp.dot(banded(taps, base, j).astype(bf16), shifted[k], preferred_element_type=f32)
        pitched(conv_out, base, j)[...] = out
        pitched(cot_rows, base, j)[...] = cot[k].astype(f32) * mask[...]

    by_channel(conv_step)

    for acc in (win_acc, wout_acc, gain_acc, shift_acc, obias_acc, scale_acc):
        acc[...] = jnp.zeros_like(acc)

    def wide(x):
        return jnp.concatenate([x, x], axis=1)

    def fold(x):
        return x[:, :COLS] + x[:, COLS:]

    def pair(ref, r):
        return jnp.concatenate([row_of(ref, r)[...], row_of(ref, r + 1)[...]], axis=1)

    def mean(x):
        return jnp.sum(x, axis=0, keepdims=True) * (1.0 / CH)

    cells = (((1,), (1,)), ((), ()))
    ones = jnp.where(iota((16, 2 * COLS), 0) == 0, 1.0, 0.0).astype(bf16)

    def point_step(i, carry):
        r = 2 * i
        conv_bias, gain, shift, out_bias, scale = (wide(chan[n]) for n in range(5))
        x = pair(conv_out, r) + conv_bias
        centre = x - mean(x)
        inv_std = lax.rsqrt(mean(centre * centre) + ln_epsilon)
        unit = centre * inv_std
        normed = jnp.concatenate([(unit * gain + shift).astype(bf16), ones], axis=0)
        masked_cot = pair(cot_rows, r)
        mixed_grad = (scale * masked_cot).astype(bf16)
        u = jnp.dot(w_in_t[...], normed, preferred_element_type=f32)
        half_grad = jnp.dot(w_out[...], mixed_grad, preferred_element_type=f32)
        bent = (tanh_scale * slope_coef) * (u * u)
        t = jnp.tanh(u * (tanh_scale + bent))
        s = 1.0 + t
        hidden = (u * s).astype(bf16)
        slope = s + s * (1.0 - t) * (u * (tanh_scale + 3.0 * bent))
        pre_grad = (half_grad * slope).astype(bf16)
        mixed = jnp.dot(w_out_t[...], hidden, preferred_element_type=f32) + out_bias
        normed_grad = jnp.dot(w_in[...], pre_grad, preferred_element_type=f32)
        win_acc[...] += lax.dot_general(normed, pre_grad, cells, preferred_element_type=f32)
        wout_acc[...] += lax.dot_general(hidden, mixed_grad, cells, preferred_element_type=f32)
        change = scale * mixed
        row_of(delta, r)[...] = change[:, :COLS]
        row_of(delta, r + 1)[...] = change[:, COLS:]
        scale_acc[...] += fold(masked_cot * mixed)
        obias_acc[...] += fold(mixed_grad.astype(f32))
        slant = normed_grad * unit
        gain_acc[...] += fold(slant)
        shift_acc[...] += fold(normed_grad)
        q = normed_grad * gain
        grad = inv_std * (q - mean(q) - unit * mean(slant * gain))
        for n in range(2):
            part = grad[:, n * COLS : (n + 1) * COLS]
            row_of(conv_grad, r + n)[...] = part
            row_of(grad_back, ROWS - 1 - r - n)[...] = part
        return carry

    lax.fori_loop(0, ROWS // 2, point_step, 0, unroll=2)

    for g in range(3):
        bottom[g] = row_of(conv_grad, g)[...]
        top[g] = row_of(conv_grad, ROWS - 3 + g)[...]

    def grad_step(base, j):
        k = base + j
        back = pitched(grad_back, base, j)[...]
        prod = lax.dot_general(back.astype(bf16), shifted[k], cells, preferred_element_type=f32)
        for p in range(4):
            acc = None
            for i in range(4):
                tile = prod[8 * i : 8 * i + 8, 128 * p : 128 * p + 128]
                tile = pltpu.roll(tile, 8 * i, 1, stride=1, stride_axis=0)
                acc = tile if acc is None else acc + tile
            taps_acc[p, pl.ds(k, 1), :] = jnp.sum(acc, axis=0, keepdims=True)

    by_channel(grad_step)

    lane = iota((CH, COLS), 1)

    def total(x):
        return jnp.broadcast_to(jnp.sum(x, axis=1, keepdims=True), (CH, COLS))

    bias = row_of(conv_grad, 0)[...]
    for r in range(1, ROWS):
        bias = bias + row_of(conv_grad, r)[...]
    small = (bias, gain_acc[...], shift_acc[...], obias_acc[...], scale_acc[...])
    tail = jnp.zeros((CH, COLS), f32)
    for n, x in enumerate(small):
        tail = jnp.where(lane == n, total(x), tail)
    used = jnp.logical_and(lax.rem(lane, 64) >= 28, lax.rem(lane, 64) < 35)
    for p in range(4):
        moved = jnp.where(used, taps_acc[p], 0.0)
        tail = tail + (pltpu.roll(moved, 7 * p, 1) if p else moved)
    extra = win_acc[CH : CH + 8, :]
    turned = jnp.transpose(
        jnp.concatenate([extra[:, :COLS], extra[:, COLS:], jnp.zeros((112, COLS), f32)], axis=0)
    )
    for n in range(4):
        part = turned[CH * (n % 2) : CH * (n % 2) + CH, :]
        tail = jnp.where(lane == 5 + n, pltpu.roll(part, (5 + n - 8 * (n // 2)) % COLS, 1), tail)
    sums[0:64, :] = win_acc[0:CH, :COLS]
    sums[64:128, :] = win_acc[0:CH, COLS:]
    sums[128:256, :] = 0.5 * jnp.concatenate([wout_acc[0:128, :], wout_acc[128:256, :]], axis=1)
    sums[256:320, :] = tail


def spread_body(
    flags,
    conv_grad,
    south,
    north,
    west,
    east,
    taps,
    turned_taps,
    cot,
    mask,
    state,
    delta,
    *rest,
    first,
):
    state_grad, new_state, shifted, near = rest[-4:]
    near_fill(near, north, south)
    build_shifted(
        shifted,
        lambda base, j: pitched(conv_grad, base, j)[...],
        near,
        west,
        east,
        PART,
        lambda base, j: (0, first + base + j),
    )
    on_top = flags[1] == 1
    spot = lax.rem(iota((ROWS, 512), 1), 64)
    beyond = jnp.logical_and(on_top, jnp.logical_and(spot >= 32, spot < 35))

    def step(base, j):
        k = base + j
        band = jnp.where(beyond, banded(taps, base, j), banded(turned_taps, base, j))
        out = jnp.dot(band.astype(bf16), shifted[k], preferred_element_type=f32)
        ocean = mask[...]
        state_grad[k] = (cot[k].astype(f32) * ocean + out).astype(bf16)
        new = ocean * (state[k].astype(f32) + pitched(delta, base, j)[...])
        new_state[k] = new.astype(bf16)

    by_channel(step, 8, PART)


def spread_part(c, held, flags, conv_grad, south, north, west, east, taps, turned, cot, mask, state, delta):
    tall = pl.BlockSpec((PART * PITCH, COLS), lambda _: (c, 0))
    slab = pl.BlockSpec((3, PART, COLS), lambda _: (0, c, 0))
    side = pl.BlockSpec((1, SPAN, COLS), lambda _: (c * PART // 32, 0, 0))
    band = pl.BlockSpec((PART, 512), lambda _: (c, 0))
    block = pl.BlockSpec((PART, ROWS, COLS), lambda _: (c, 0, 0))
    shape = jax.ShapeDtypeStruct((CH, ROWS, COLS), bf16)
    args = (flags, conv_grad, south, north, west, east, taps, turned, cot, mask, state, delta)
    whole = pl.BlockSpec((ROWS, COLS), lambda _: (0, 0))
    specs = [SM, tall, slab, slab, side, side, band, band, block, whole, block, tall]
    kept = [pl.BlockSpec(memory_space=pl.ANY)] * len(held)
    return pl.pallas_call(
        functools.partial(spread_body, first=c * PART % 32),
        grid=(1,),
        out_shape=(shape, shape),
        in_specs=specs + kept,
        out_specs=(block, block),
        scratch_shapes=[
            pltpu.VMEM((PART, 512, COLS), bf16),
            pltpu.VMEM((PART * NEAR, COLS), f32),
        ],
        input_output_aliases={len(args) + n: n for n in range(len(held))},
        compiler_params=pltpu.CompilerParams(vmem_limit_bytes=16 * 1024 * 1024),
        cost_estimate=pl.CostEstimate(flops=1 << 24, bytes_accessed=3 << 20, transcendentals=0),
        name="spread",
    )(*args, *held)


def unpack_body(
    sums, pick, kernel_grad, w_in_grad, w_out_grad, b_in_grad, channel_grads, *, scale
):
    w_in_grad[:, :COLS] = sums[0:64, :] * scale
    w_in_grad[:, COLS:] = sums[64:128, :] * scale
    packed = jnp.transpose(sums[128:256, :] * scale)
    w_out_grad[:, :COLS] = packed[:CH]
    w_out_grad[:, COLS:] = packed[CH:]
    tail = sums[256:320, :] * scale
    turned = jnp.transpose(jnp.concatenate([tail, tail], axis=0))
    kernel_grad[...] = jnp.dot(
        pick[...], turned, preferred_element_type=f32, precision=lax.Precision.HIGHEST
    )[:, :CH]
    channel_grads[...] = turned[0:5, :CH]
    for n in range(4):
        b_in_grad[:, CH * n : CH * n + CH] = turned[5 + n : 6 + n, :CH]


def tap_tables():
    place = np.zeros((49, 512), np.float32)
    turned = np.zeros((49, 512), np.float32)
    pick = np.zeros((49, COLS), np.float32)
    for a in range(7):
        for b in range(7):
            p, g = divmod(b, 2)
            spot = 128 * p + (64 * g + a - 3) % 128
            place[7 * a + b, spot] = 1.0
            turned[48 - (7 * a + b), spot] = 1.0
            pick[7 * a + b, 28 + 7 * p + a + 64 * g] = 1.0
    return place, turned, pick


def row_pairs(lat_size, lon_size):
    first, second = [], []
    for i in range(lat_size):
        for j in range(lon_size):
            me = i * lon_size + j
            first.append((me, (i ^ 1) * lon_size + j))
            if i == lat_size - 1:
                second.append((me, i * lon_size + lon_size - 1 - j))
            elif i > 0:
                other = i + 1 if i % 2 else i - 1
                second.append((me, other * lon_size + j))
    return first, second


def exchange_rows(flags, top, bottom):
    first, second = row_pairs(lax.axis_size("lat"), lax.axis_size("lon"))
    even = flags[0] == 1
    from_a = lax.ppermute(jnp.where(even, top, bottom), AXES, first)
    from_b = lax.ppermute(jnp.where(even, bottom, top), AXES, second)
    return from_a, from_b


def settle_edges(flags, from_a, from_b, rows):
    slab = jax.ShapeDtypeStruct((3, CH, COLS), f32)
    flat = jax.ShapeDtypeStruct((2, SPAN, COLS), f32)
    return call(
        edges_body,
        (slab, slab, flat, flat),
        (flags, from_a, from_b, rows),
        [pltpu.VMEM((CH * NEAR, COLS), f32)],
        smem_first=True,
        flops=1 << 20,
        nbytes=1 << 21,
        name="edges",
    )


def exchange_columns(to_west, to_east):
    lon_size = lax.axis_size("lon")
    up = [(j, (j + 1) % lon_size) for j in range(lon_size)]
    down = [(k, j) for j, k in up]
    west = lax.ppermute(to_east, "lon", up)
    east = lax.ppermute(to_west, "lon", down)
    return west, east


def core_pairs():
    return [(i, i ^ 1) for i in range(32)]


def chip_pairs(flip_x, flip_y, flip_z):
    pairs = []
    for i in range(256):
        lat, lon = divmod(i, 32)
        x = ((lat >> 2) * 2 + (lon >> 4)) ^ flip_x
        y = (lat & 3) ^ flip_y
        z = ((lon >> 1) & 7) ^ flip_z
        pairs.append((i, ((x >> 1) * 4 + y) * 32 + (x & 1) * 16 + z * 2 + (lon & 1)))
    return pairs


def tie(*values):
    return lax.optimization_barrier(values)


def reduce_and_spread(sums, flags, conv_grad, top, bottom, finish):
    odd = lax.rem(lax.axis_index("lon"), 2) == 1
    half = sums.shape[0] // 2
    low, high = sums[:half], sums[half:]
    mine = jnp.where(odd, high, low) + lax.ppermute(jnp.where(odd, low, high), "lon", core_pairs())
    from_a, from_b = exchange_rows(flags, top, bottom)

    def hop(x, *flips):
        return x + lax.ppermute(x, AXES, chip_pairs(*flips))

    mine, from_a, from_b = tie(hop(mine, 1, 0, 0), from_a, from_b)
    north, south, to_west, to_east = settle_edges(flags, from_a, from_b, conv_grad)
    mine, to_west, to_east = tie(hop(mine, 3, 0, 0), to_west, to_east)
    west, east = exchange_columns(to_west, to_east)
    mine, west, east = tie(hop(mine, 0, 1, 0), west, east)
    done = ()
    for c, flips in enumerate(((0, 3, 0), (0, 0, 1), (0, 0, 2), (0, 0, 4))):
        done = finish(c, done, south, north, west, east)
        mine, *done = tie(hop(mine, *flips), *done)
    other = lax.ppermute(mine, "lon", core_pairs())
    total = jnp.concatenate([jnp.where(odd, other, mine), jnp.where(odd, mine, other)], axis=0)
    return total, done


def per_device(
    sea_state,
    conv_kernel,
    conv_bias,
    norm_gain,
    norm_shift,
    w_in,
    b_in,
    w_out,
    b_out,
    layer_scale,
    sea_mask,
    cotangent,
):
    lat_size, lon_size = lax.axis_size("lat"), lax.axis_size("lon")
    lat = lax.axis_index("lat")
    flags = jnp.stack([(lat % 2 == 0).astype(jnp.int32), (lat == lat_size - 1).astype(jnp.int32)])
    top = jnp.transpose(sea_state[:, ROWS - 3 :, :].astype(f32), (1, 0, 2))
    bottom = jnp.transpose(sea_state[:, :3, :].astype(f32), (1, 0, 2))
    from_a, from_b = exchange_rows(flags, top, bottom)
    mask = sea_mask.astype(f32)
    place, turned, pick = (jnp.asarray(x) for x in tap_tables())
    taps = jnp.dot(conv_kernel, place.astype(bf16), preferred_element_type=f32)
    turned_taps = jnp.dot(conv_kernel, turned.astype(bf16), preferred_element_type=f32)
    chan = jnp.stack([conv_bias, norm_gain, norm_shift, b_out, layer_scale]).astype(f32)
    chan = jnp.broadcast_to(chan[:, :, None], (5, CH, COLS))
    w_in_t = jnp.concatenate([w_in.T, b_in[:, None], jnp.zeros((HID, 15), bf16)], axis=1)
    half_out = (w_out.astype(f32) * 0.5).astype(bf16)
    north, south, to_west, to_east = settle_edges(flags, from_a, from_b, sea_state)
    halo = (south, north) + exchange_columns(to_west, to_east)
    shifted = pltpu.VMEM((CH, 512, COLS), bf16)
    near = pltpu.VMEM((CH * NEAR, COLS), f32)
    flat = pltpu.VMEM((CH, COLS), f32)
    tall_shape = (CH * PITCH, COLS)
    tall = pltpu.VMEM(tall_shape, f32)
    slab = jax.ShapeDtypeStruct((3, CH, COLS), f32)
    delta, conv_grad, top, bottom, sums = call(
        main_body,
        (
            jax.ShapeDtypeStruct(tall_shape, f32),
            jax.ShapeDtypeStruct(tall_shape, f32),
            slab,
            slab,
            jax.ShapeDtypeStruct((320, COLS), f32),
        ),
        (sea_state,)
        + halo
        + (cotangent, mask, taps, chan, w_in, w_in_t, half_out, half_out.T),
        [
            shifted,
            near,
            tall,
            tall,
            tall,
            pltpu.VMEM((CH + 16, HID), f32),
            pltpu.VMEM((HID, CH), f32),
            flat,
            flat,
            flat,
            flat,
            pltpu.VMEM((4, CH, COLS), f32),
        ],
        flops=1 << 30,
        nbytes=8 << 20,
        name="main",
        mib=28,
    )

    def finish(c, held, *halo):
        rest = (taps, turned_taps, cotangent, mask, sea_state, delta)
        return spread_part(c, held, flags, conv_grad, *halo, *rest)

    total, (state_grad, new_state) = reduce_and_spread(
        sums, flags, conv_grad, top, bottom, finish
    )
    grad_scale = 1.0 / math.sqrt(ROWS * lat_size * COLS * lon_size)
    kernel_grad, w_in_grad, w_out_grad, b_in_grad, channel_grads = call(
        functools.partial(unpack_body, scale=grad_scale),
        (
            jax.ShapeDtypeStruct((49, CH), f32),
            jax.ShapeDtypeStruct((CH, HID), f32),
            jax.ShapeDtypeStruct((CH, HID), f32),
            jax.ShapeDtypeStruct((1, HID), f32),
            jax.ShapeDtypeStruct((5, CH), f32),
        ),
        (total, pick),
        flops=1 << 17,
        nbytes=1 << 18,
        name="unpack",
    )
    return (
        new_state,
        state_grad,
        kernel_grad.T,
        w_in_grad,
        w_out_grad.T,
        b_in_grad.reshape(HID),
        channel_grads,
    )


def solution(mesh):
    grid = P(None, "lat", "lon")
    placed = (grid,) + (P(),) * 9 + (P("lat", "lon"), grid)
    return jax.shard_map(
        per_device,
        mesh=mesh,
        in_specs=placed,
        out_specs=(grid, grid, P(), P(), P(), P(), P()),
        check_vma=False,
    )
```

time: 147 us -> 94.5 us (0.64); the launches traced: 145 us -> 94 us
  Pallas kernels: 70.1 us -> 32.5 us
  local copies, waits for them, and re-layouts: 11.5 us -> 3.09 us
  other arithmetic: 5.48 us -> 1.11 us
  starting transfers between devices: 47.3 us -> 44.4 us
    pallas_call x6 -> x4, Pallas kernels: 70.1 us -> 21.5 us  [call(): pl.pallas_call(body, out_shape=out_shape, in_specs=specs, out_specs=jax.t...]
    all_to_all x2 -> x0, starting transfers between devices: 12.7 us -> none  [swap(): return lax.all_to_all(x, 'lon', 0, 0, tiled=True, axis_index_groups=groups)]
    pallas_call x0 -> x4, Pallas kernels: none -> 11.1 us  [spread_part(): pl.pallas_call(functools.partial(spread_body, first=c * PART % 32), grid=...]
    ppermute x3 -> x7, starting transfers between devices: 10.5 us -> 20.5 us  [hop(): return x + lax.ppermute(x, AXES, chip_pairs(*flips))]
    unnamed x38 -> x25, local copies, waits for them, and re-layouts: 5.9 us -> 0.94 us
    ppermute x2, waiting for transfers between devices: 1.99 us -> 4.95 us  [exchange_columns(): east = lax.ppermute(to_west, 'lon', down)]
    ppermute x2, waiting for transfers between devices: 2.45 us -> 0.01 us  [exchange_rows(): from_a = lax.ppermute(jnp.where(even, top, bottom), AXES, first)]
    broadcast_in_dim x3 -> x2, local copies, waits for them, and re-layouts: 3.06 us -> 0.75 us  [the longest x1 0.75 us: per_device(): b_in[:, None]]
  transfers between devices with their start and end apart: 15 -> 17, of which waited for: 7 -> 9; matrix products, arithmetic and copies ran while one was open for 3% -> 4% of each run, Pallas kernels for 20% -> 13%
where the time goes in v2:
time: 94.5 us; the launch traced here: 94 us
  starting transfers between devices  44.4 us (47%)
  Pallas kernels  32.5 us (34%)
  waiting for transfers between devices  10.7 us (11%)
  local copies, waits for them, and re-layouts  3.09 us (3%)
  matrix products  1.22 us (1%)
  other arithmetic  1.11 us (1%)
  between operations  1.01 us (1%)
    pallas_call x4, Pallas kernels, call(): pl.pallas_call(body, out_shape=out_shape, in_specs=specs, out_specs=jax.t...  21.5 us
    ppermute x7, starting transfers between devices, hop(): return x + lax.ppermute(x, AXES, chip_pairs(*flips))  20.5 us
    pallas_call x4, Pallas kernels, spread_part(): pl.pallas_call(functools.partial(spread_body, first=c * PART % 32), grid=...  11.1 us
    ppermute x2, starting transfers between devices, exchange_rows(): from_a = lax.ppermute(jnp.where(even, top, bottom), AXES, first)  8.58 us
    ppermute x2, starting transfers between devices, exchange_columns(): west = lax.ppermute(to_east, 'lon', up)  6.5 us
    ppermute x2, waiting for transfers between devices, exchange_columns(): east = lax.ppermute(to_west, 'lon', down)  4.95 us
    ppermute x1, starting transfers between devices, reduce_and_spread(): other = lax.ppermute(mine, 'lon', core_pairs())  4.79 us
    ppermute x7, waiting for transfers between devices, hop(): return x + lax.ppermute(x, AXES, chip_pairs(*flips))  2.93 us
  transfers between devices with their start and end apart: 17, of which 9 were waited for; matrix products, arithmetic and copies ran while one was open for 4% of the time, Pallas kernels for 13%

profile of v2, /device:TPU:1, one launch (start us, length us, event | category | flops | bytes accessed | tf_op | source)
XLA Modules:
  0.0 94.0 jit_solution(14216992155809970564)
XLA Ops:
  0.6 0.0 copy-start
  0.7 0.0 copy-start.1
  0.7 0.0 copy-start.6
  0.7 1.1 %fusion.3 = (bf16[64,3,128]{2,1,0:T(4,128)(2,1)S(1)}, bf16[64,3,128]{2,1,0:T(4,128)(2,1)S(1)}) fusion(bf16[64,32,128]{2,1,0:T(8,128)(2,1)} %state.9), kind=kLoop, calls=%fused_computation.17 | loop fusion | bytes 196608 | tf_op jit(solution)/shard_map/slice | solution.py:512
  1.8 0.0 copy-start.2
  1.8 0.0 copy-start.3
  1.9 0.8 collective-permute-start.1
  2.7 4.7 %collective-permute-start = (f32[3,64,128]{2,1,0:T(8,128)S(1)}, f32[3,64,128]{2,1,0:T(8,128)S(1)}, u32[]{:S(2)}, u32[]{:S(2)}) collective-permute-start(f32[3,64,128]{2,1,0:T(8,128)S(1)} %get-tuple-element.108), channel_id=1, source_target_pairs={{0,32},{1,33},{2,34},{3,35},{4,36},{5,37},{6,38},{7,39},{8,40},{9,... | collective-permute-start | bytes 294920 | tf_op jit(solution)/shard_map/ppermute | solution.py:423
  7.4 0.7 broadcast_in_dim.15
  8.2 0.9 copy.34
  9.0 0.8 fusion.2
  9.8 0.1 pad.4.clone
  9.9 0.0 copy-done
  9.9 1.0 %convolution_bitcast_fusion.1.taps = f32[64,512]{1,0:T(8,128)S(1)} fusion(bf16[49,512]{1,0:T(8,128)(2,1)} %constant.41, bf16[64,49]{0,1:T(8,128)(2,1)S(1)} %copy-done), kind=kOutput, calls=%fused_computation.1 | convolution fusion | flops 3211264 | bytes 187520 | tf_op jit(solution)/shard_map/dot_general | solution.py:517
  10.9 0.1 pad_add_fusion.flags
  11.0 0.0 collective-permute-done.1.from_b
  11.0 0.0 collective-permute-done.from_a
  11.0 0.0 copy-done.1
  11.0 1.1 %edges.2 = (f32[3,64,128]{2,1,0:T(8,128)S(1)}, f32[3,64,128]{2,1,0:T(8,128)S(1)}, f32[2,40,128]{2,1,0:T(8,128)S(1)}, f32[2,40,128]{2,1,0:T(8,128)S(1)}) custom-call(s32[2]{0:T(128)S(1)} %pad_add_fusion.flags, f32[3,64,128]{2,1,0:T(8,128)S(1)} %collective-permute-done.from_a, f32[3,64,128]{2,1,0:T(8,128)S(1)} %collective-permute-done.1.from_b, ...), custom_call_target="tpu_custom_call" | custom-call | flops 1048576 | bytes 2097152 | tf_op jit(solution)/shard_map/edges/pallas_call | solution.py:31
  12.1 2.8 %collective-permute-start.2 = (f32[2,40,128]{2,1,0:T(8,128)S(1)}, f32[2,40,128]{2,1,0:T(8,128)S(1)}, u32[]{:S(2)}, u32[]{:S(2)}) collective-permute-start(f32[2,40,128]{2,1,0:T(8,128)S(1)} %get-tuple-element.56), channel_id=1, source_target_pairs={{0,1},{1,2},{2,3},{3,4},{4,5},{5,6},{6,7},{7,8},{8,9},{9,10},{10,1... | collective-permute-start | bytes 122888 | tf_op jit(solution)/shard_map/ppermute | solution.py:447
  14.9 0.0 collective-permute-start.3
  14.9 0.1 maximum_maximum_fusion.w_in_t
  15.0 0.0 copy-done.6
  15.1 0.1 copy.36.w_out
  15.3 0.8 collective-permute-done.2.west
  16.0 2.3 %collective-permute-done.3.east = f32[2,40,128]{2,1,0:T(8,128)S(1)} collective-permute-done((f32[2,40,128]{2,1,0:T(8,128)S(1)}, f32[2,40,128]{2,1,0:T(8,128)S(1)}, u32[]{:S(2)}, u32[]{:S(2)}) %collective-permute-start.3) | collective-permute-done | bytes 40992 | tf_op jit(solution)/shard_map/ppermute | solution.py:448
  18.4 0.1 broadcast_in_dim.12.chan
  18.5 18.2 %main.1 = (f32[2112,128]{1,0:T(8,128)S(1)}, f32[2112,128]{1,0:T(8,128)S(1)}, f32[3,64,128]{2,1,0:T(8,128)S(1)}, f32[3,64,128]{2,1,0:T(8,128)S(1)}, f32[320,128]{1,0:T(8,128)S(1)}) custom-call(bf16[64,32,128]{2,1,0:T(8,128)(2,1)S(1)} %copy-done.1, f32[3,64,128]{2,1,0:T(8,128)S(1)} %get-tuple-element.54.south, f32[3,64,128]{2,1,0:T(8,128)S(1)} %get-tuple-element.55.north, ...), custom_call_target="tpu_custom_call" | custom-call | flops 1073741824 | bytes 8388608 | tf_op jit(solution)/shard_map/main/pallas_call | solution.py:31
  36.7 2.6 %collective-permute-start.4 = (f32[160,128]{1,0:T(8,128)S(1)}, f32[160,128]{1,0:T(8,128)S(1)}, u32[]{:S(2)}, u32[]{:S(2)}) collective-permute-start(f32[160,128]{1,0:T(8,128)S(1)} %slice_select_fusion), channel_id=1, source_target_pairs={{0,1},{1,0},{2,3},{3,2},{4,5},{5,4},{6,7},{7,6},{8,9},{9,8},{10,11... | collective-permute-start | bytes 245768 | tf_op jit(solution)/shard_map/ppermute | solution.py:475
  39.3 0.7 collective-permute-start.7
  40.0 3.8 %collective-permute-start.6 = (f32[3,64,128]{2,1,0:T(8,128)S(1)}, f32[3,64,128]{2,1,0:T(8,128)S(1)}, u32[]{:S(2)}, u32[]{:S(2)}) collective-permute-start(f32[3,64,128]{2,1,0:T(8,128)S(1)} %get-tuple-element.104), channel_id=1, source_target_pairs={{0,32},{1,33},{2,34},{3,35},{4,36},{5,37},{6,38},{7,39},{8,40},{9,... | collective-permute-start | bytes 294920 | tf_op jit(solution)/shard_map/ppermute | solution.py:423
  43.8 0.0 collective-permute-done.4
  43.8 0.0 copy-start.5
  43.8 1.2 %collective-permute-start.5 = (f32[160,128]{1,0:T(8,128)S(1)}, f32[160,128]{1,0:T(8,128)S(1)}, u32[]{:S(2)}, u32[]{:S(2)}) collective-permute-start(f32[160,128]{1,0:T(8,128)S(1)} %select_add_fusion), channel_id=1, source_target_pairs={{0,16},{1,17},{2,18},{3,19},{4,20},{5,21},{6,22},{7,23},{8,24},{9,... | collective-permute-start | bytes 245768 | tf_op jit(solution)/shard_map/ppermute | solution.py:479
  45.1 2.1 %collective-permute-done.5 = f32[160,128]{1,0:T(8,128)S(1)} collective-permute-done((f32[160,128]{1,0:T(8,128)S(1)}, f32[160,128]{1,0:T(8,128)S(1)}, u32[]{:S(2)}, u32[]{:S(2)}) %collective-permute-start.5) | collective-permute-done | bytes 81952 | tf_op jit(solution)/shard_map/ppermute | solution.py:479
  47.2 0.0 collective-permute-done.7.from_b
  47.2 0.0 collective-permute-done.6.from_a
  47.2 4.8 %collective-permute-start.8 = (f32[160,128]{1,0:T(8,128)S(1)}, f32[160,128]{1,0:T(8,128)S(1)}, u32[]{:S(2)}, u32[]{:S(2)}) collective-permute-start(f32[160,128]{1,0:T(8,128)S(1)} %add.30), channel_id=1, source_target_pairs={{0,144},{1,145},{2,146},{3,147},{4,148},{5,149},{6,150},{7,151},{8... | collective-permute-start | bytes 245768 | tf_op jit(solution)/shard_map/ppermute | solution.py:479
  52.0 1.3 %edges.3 = (f32[3,64,128]{2,1,0:T(8,128)S(1)}, f32[3,64,128]{2,1,0:T(8,128)S(1)}, f32[2,40,128]{2,1,0:T(8,128)S(1)}, f32[2,40,128]{2,1,0:T(8,128)S(1)}) custom-call(s32[2]{0:T(128)S(1)} %pad_add_fusion.flags, f32[3,64,128]{2,1,0:T(8,128)S(1)} %collective-permute-done.6.from_a, f32[3,64,128]{2,1,0:T(8,128)S(1)} %collective-permute-done.7.from_b, ...), custom_call_target="tpu_custom_call" | custom-call | flops 1048576 | bytes 2097152 | tf_op jit(solution)/shard_map/edges/pallas_call | solution.py:31
  53.4 0.5 collective-permute-done.8
  53.9 0.5 collective-permute-start.9
  54.4 3.7 %collective-permute-start.10 = (f32[2,40,128]{2,1,0:T(8,128)S(1)}, f32[2,40,128]{2,1,0:T(8,128)S(1)}, u32[]{:S(2)}, u32[]{:S(2)}) collective-permute-start(f32[2,40,128]{2,1,0:T(8,128)S(1)} %get-tuple-element.68), channel_id=1, source_target_pairs={{0,1},{1,2},{2,3},{3,4},{4,5},{5,6},{6,7},{7,8},{8,9},{9,10},{10,1... | collective-permute-start | bytes 122888 | tf_op jit(solution)/shard_map/ppermute | solution.py:447
  58.1 0.0 collective-permute-start.11
  58.1 0.0 collective-permute-done.9
  58.1 1.1 %collective-permute-done.10.west = f32[2,40,128]{2,1,0:T(8,128)S(1)} collective-permute-done((f32[2,40,128]{2,1,0:T(8,128)S(1)}, f32[2,40,128]{2,1,0:T(8,128)S(1)}, u32[]{:S(2)}, u32[]{:S(2)}) %collective-permute-start.10) | collective-permute-done | bytes 40992 | tf_op jit(solution)/shard_map/ppermute | solution.py:447
  59.2 2.6 %collective-permute-done.11.east = f32[2,40,128]{2,1,0:T(8,128)S(1)} collective-permute-done((f32[2,40,128]{2,1,0:T(8,128)S(1)}, f32[2,40,128]{2,1,0:T(8,128)S(1)}, u32[]{:S(2)}, u32[]{:S(2)}) %collective-permute-start.11) | collective-permute-done | bytes 40992 | tf_op jit(solution)/shard_map/ppermute | solution.py:448
  61.8 5.4 %collective-permute-start.12 = (f32[160,128]{1,0:T(8,128)S(1)}, f32[160,128]{1,0:T(8,128)S(1)}, u32[]{:S(2)}, u32[]{:S(2)}) collective-permute-start(f32[160,128]{1,0:T(8,128)S(1)} %add.32), channel_id=1, source_target_pairs={{0,96},{1,97},{2,98},{3,99},{4,100},{5,101},{6,102},{7,103},{8,104... | collective-permute-start | bytes 245768 | tf_op jit(solution)/shard_map/ppermute | solution.py:479
  67.1 0.0 copy-done.5
  67.1 0.2 convolution_bitcast_fusion.turned_taps
  67.3 2.7 %spread.4 = (bf16[64,32,128]{2,1,0:T(8,128)(2,1)}, bf16[64,32,128]{2,1,0:T(8,128)(2,1)}) custom-call(s32[2]{0:T(128)S(1)} %pad_add_fusion.flags, f32[2112,128]{1,0:T(8,128)S(1)} %get-tuple-element.64.own.conv_grad, f32[3,64,128]{2,1,0:T(8,128)S(1)} %get-tuple-element.71.south, f32[3,64,128]{2,1,0:T(8,128)S(1)} %get-tuple-element.72.north, ...), custom_call_target="tpu_custom_call" | custom-call | flops 16777216 | bytes 3145728 | tf_op jit(solution)/shard_map/spread/pallas_call | solution.py:357
  70.1 0.0 collective-permute-done.12
  70.1 0.5 collective-permute-start.13
  70.6 2.8 %spread.5 = (bf16[64,32,128]{2,1,0:T(8,128)(2,1)}, bf16[64,32,128]{2,1,0:T(8,128)(2,1)}) custom-call(s32[2]{0:T(128)S(1)} %pad_add_fusion.flags, f32[2112,128]{1,0:T(8,128)S(1)} %get-tuple-element.64.own.conv_grad, f32[3,64,128]{2,1,0:T(8,128)S(1)} %get-tuple-element.71.south, ...), custom_call_target="tpu_custom_call", output_to_operand_aliasing={{0}: (12, {}), {1}: (13, {})} | custom-call | flops 16777216 | bytes 3145728 | tf_op jit(solution)/shard_map/spread/pallas_call | solution.py:357
  73.4 0.1 collective-permute-done.13
  73.5 3.7 %collective-permute-start.14 = (f32[160,128]{1,0:T(8,128)S(1)}, f32[160,128]{1,0:T(8,128)S(1)}, u32[]{:S(2)}, u32[]{:S(2)}) collective-permute-start(f32[160,128]{1,0:T(8,128)S(1)} %add.34), channel_id=1, source_target_pairs={{0,4},{1,5},{2,6},{3,7},{4,0},{5,1},{6,2},{7,3},{8,12},{9,13},{10,... | collective-permute-start | bytes 245768 | tf_op jit(solution)/shard_map/ppermute | solution.py:479
  77.2 2.8 %spread.6 = (bf16[64,32,128]{2,1,0:T(8,128)(2,1)}, bf16[64,32,128]{2,1,0:T(8,128)(2,1)}) custom-call(s32[2]{0:T(128)S(1)} %pad_add_fusion.flags, f32[2112,128]{1,0:T(8,128)S(1)} %get-tuple-element.64.own.conv_grad, f32[3,64,128]{2,1,0:T(8,128)S(1)} %get-tuple-element.71.south, ...), custom_call_target="tpu_custom_call", output_to_operand_aliasing={{0}: (12, {}), {1}: (13, {})} | custom-call | flops 16777216 | bytes 3145728 | tf_op jit(solution)/shard_map/spread/pallas_call | solution.py:357
  80.0 0.0 collective-permute-done.14
  80.0 0.0 copy-start.4
  80.0 4.4 %collective-permute-start.15 = (f32[160,128]{1,0:T(8,128)S(1)}, f32[160,128]{1,0:T(8,128)S(1)}, u32[]{:S(2)}, u32[]{:S(2)}) collective-permute-start(f32[160,128]{1,0:T(8,128)S(1)} %add.35), channel_id=1, source_target_pairs={{0,8},{1,9},{2,10},{3,11},{4,12},{5,13},{6,14},{7,15},{8,0},{9,1},... | collective-permute-start | bytes 245768 | tf_op jit(solution)/shard_map/ppermute | solution.py:479
  84.4 2.8 %spread.7 = (bf16[64,32,128]{2,1,0:T(8,128)(2,1)}, bf16[64,32,128]{2,1,0:T(8,128)(2,1)}) custom-call(s32[2]{0:T(128)S(1)} %pad_add_fusion.flags, f32[2112,128]{1,0:T(8,128)S(1)} %get-tuple-element.64.own.conv_grad, f32[3,64,128]{2,1,0:T(8,128)S(1)} %get-tuple-element.71.south, ...), custom_call_target="tpu_custom_call", output_to_operand_aliasing={{0}: (12, {}), {1}: (13, {})} | custom-call | flops 16777216 | bytes 3145728 | tf_op jit(solution)/shard_map/spread/pallas_call | solution.py:357
  87.2 0.2 collective-permute-done.15
  87.4 4.8 %collective-permute-start.16 = (f32[160,128]{1,0:T(8,128)S(1)}, f32[160,128]{1,0:T(8,128)S(1)}, u32[]{:S(2)}, u32[]{:S(2)}) collective-permute-start(f32[160,128]{1,0:T(8,128)S(1)} %add.36), channel_id=1, source_target_pairs={{0,1},{1,0},{2,3},{3,2},{4,5},{5,4},{6,7},{7,6},{8,9},{9,8},{10,11... | collective-permute-start | bytes 245768 | tf_op jit(solution)/shard_map/ppermute | solution.py:490
  92.2 0.9 collective-permute-done.16
  93.1 0.9 unpack.1
  (29 shorter events, 0.2 us)
Async XLA Ops:
  0.6 9.3 %copy-start = (bf16[64,49]{0,1:T(8,128)(2,1)S(1)}, bf16[64,49]{0,1:T(8,128)(2,1)}, u32[]{:S(2)}) copy-start(bf16[64,49]{0,1:T(8,128)(2,1)} %param.16) | copy-start | bytes 18820
  0.7 10.4 %copy-start.1 = (bf16[64,32,128]{2,1,0:T(8,128)(2,1)S(1)}, bf16[64,32,128]{2,1,0:T(8,128)(2,1)}, u32[]{:S(2)}) copy-start(bf16[64,32,128]{2,1,0:T(8,128)(2,1)} %state.9) | copy-start | bytes 1572868
  0.7 14.4 %copy-start.6 = (s32[32,128]{1,0:T(8,128)S(1)}, s32[32,128]{1,0:T(8,128)}, u32[]{:S(2)}) copy-start(s32[32,128]{1,0:T(8,128)} %param.25) | copy-start | bytes 49156
  0.7 14.5 %copy-start.7 = (bf16[64]{0:T(256)(128)(2,1)S(1)}, bf16[64]{0:T(256)(128)(2,1)}, u32[]{:S(2)}) copy-start(bf16[64]{0:T(256)(128)(2,1)} %param.17) | copy-start | bytes 388
  0.7 14.5 %copy-start.8 = (bf16[64]{0:T(256)(128)(2,1)S(1)}, bf16[64]{0:T(256)(128)(2,1)}, u32[]{:S(2)}) copy-start(bf16[64]{0:T(256)(128)(2,1)} %param.18) | copy-start | bytes 388
  0.7 14.5 %copy-start.9 = (bf16[64]{0:T(256)(128)(2,1)S(1)}, bf16[64]{0:T(256)(128)(2,1)}, u32[]{:S(2)}) copy-start(bf16[64]{0:T(256)(128)(2,1)} %param.19) | copy-start | bytes 388
  0.7 14.5 %copy-start.10 = (bf16[64]{0:T(256)(128)(2,1)S(1)}, bf16[64]{0:T(256)(128)(2,1)}, u32[]{:S(2)}) copy-start(bf16[64]{0:T(256)(128)(2,1)} %param.23) | copy-start | bytes 388
  0.7 14.5 %copy-start.11 = (bf16[64]{0:T(256)(128)(2,1)S(1)}, bf16[64]{0:T(256)(128)(2,1)}, u32[]{:S(2)}) copy-start(bf16[64]{0:T(256)(128)(2,1)} %param.24) | copy-start | bytes 388
  1.8 16.6 %copy-start.2 = (bf16[64,32,128]{2,1,0:T(8,128)(2,1)S(1)}, bf16[64,32,128]{2,1,0:T(8,128)(2,1)}, u32[]{:S(2)}) copy-start(bf16[64,32,128]{2,1,0:T(8,128)(2,1)} %cot.9) | copy-start | bytes 1572868
  1.8 16.6 %copy-start.3 = (bf16[64,256]{1,0:T(8,128)(2,1)S(1)}, bf16[64,256]{1,0:T(8,128)(2,1)}, u32[]{:S(2)}) copy-start(bf16[64,256]{1,0:T(8,128)(2,1)} %w_in.1) | copy-start | bytes 98308
  1.9 9.1 %collective-permute-start.1 = (f32[3,64,128]{2,1,0:T(8,128)S(1)}, f32[3,64,128]{2,1,0:T(8,128)S(1)}, u32[]{:S(2)}, u32[]{:S(2)}) collective-permute-start(f32[3,64,128]{2,1,0:T(8,128)S(1)} %get-tuple-element.107), channel_id=1, source_target_pairs={{32,64},{33,65},{34,66},{35,67},{36,68},{37,69},{38,70},{39,71},{4... | collective-permute-start | bytes 294920 | tf_op jit(solution)/shard_map/ppermute | solution.py:424
  2.7 8.3 %collective-permute-start = (f32[3,64,128]{2,1,0:T(8,128)S(1)}, f32[3,64,128]{2,1,0:T(8,128)S(1)}, u32[]{:S(2)}, u32[]{:S(2)}) collective-permute-start(f32[3,64,128]{2,1,0:T(8,128)S(1)} %get-tuple-element.108), channel_id=1, source_target_pairs={{0,32},{1,33},{2,34},{3,35},{4,36},{5,37},{6,38},{7,39},{8,40},{9,... | collective-permute-start | bytes 294920 | tf_op jit(solution)/shard_map/ppermute | solution.py:423
  12.1 3.9 %collective-permute-start.2 = (f32[2,40,128]{2,1,0:T(8,128)S(1)}, f32[2,40,128]{2,1,0:T(8,128)S(1)}, u32[]{:S(2)}, u32[]{:S(2)}) collective-permute-start(f32[2,40,128]{2,1,0:T(8,128)S(1)} %get-tuple-element.56), channel_id=1, source_target_pairs={{0,1},{1,2},{2,3},{3,4},{4,5},{5,6},{6,7},{7,8},{8,9},{9,10},{10,1... | collective-permute-start | bytes 122888 | tf_op jit(solution)/shard_map/ppermute | solution.py:447
  14.9 3.4 %collective-permute-start.3 = (f32[2,40,128]{2,1,0:T(8,128)S(1)}, f32[2,40,128]{2,1,0:T(8,128)S(1)}, u32[]{:S(2)}, u32[]{:S(2)}) collective-permute-start(f32[2,40,128]{2,1,0:T(8,128)S(1)} %get-tuple-element.57), channel_id=1, source_target_pairs={{1,0},{2,1},{3,2},{4,3},{5,4},{6,5},{7,6},{8,7},{9,8},{10,9},{11,1... | collective-permute-start | bytes 122888 | tf_op jit(solution)/shard_map/ppermute | solution.py:448
  36.7 7.1 %collective-permute-start.4 = (f32[160,128]{1,0:T(8,128)S(1)}, f32[160,128]{1,0:T(8,128)S(1)}, u32[]{:S(2)}, u32[]{:S(2)}) collective-permute-start(f32[160,128]{1,0:T(8,128)S(1)} %slice_select_fusion), channel_id=1, source_target_pairs={{0,1},{1,0},{2,3},{3,2},{4,5},{5,4},{6,7},{7,6},{8,9},{9,8},{10,11... | collective-permute-start | bytes 245768 | tf_op jit(solution)/shard_map/ppermute | solution.py:475
  39.3 7.9 %collective-permute-start.7 = (f32[3,64,128]{2,1,0:T(8,128)S(1)}, f32[3,64,128]{2,1,0:T(8,128)S(1)}, u32[]{:S(2)}, u32[]{:S(2)}) collective-permute-start(f32[3,64,128]{2,1,0:T(8,128)S(1)} %get-tuple-element.103), channel_id=1, source_target_pairs={{32,64},{33,65},{34,66},{35,67},{36,68},{37,69},{38,70},{39,71},{4... | collective-permute-start | bytes 294920 | tf_op jit(solution)/shard_map/ppermute | solution.py:424
  40.0 7.3 %collective-permute-start.6 = (f32[3,64,128]{2,1,0:T(8,128)S(1)}, f32[3,64,128]{2,1,0:T(8,128)S(1)}, u32[]{:S(2)}, u32[]{:S(2)}) collective-permute-start(f32[3,64,128]{2,1,0:T(8,128)S(1)} %get-tuple-element.104), channel_id=1, source_target_pairs={{0,32},{1,33},{2,34},{3,35},{4,36},{5,37},{6,38},{7,39},{8,40},{9,... | collective-permute-start | bytes 294920 | tf_op jit(solution)/shard_map/ppermute | solution.py:423
  43.8 23.3 %copy-start.5 = (bf16[49,512]{1,0:T(8,128)(2,1)S(1)}, bf16[49,512]{1,0:T(8,128)(2,1)}, u32[]{:S(2)}) copy-start(bf16[49,512]{1,0:T(8,128)(2,1)} %constant.42) | copy-start | bytes 150532
  43.8 3.4 %collective-permute-start.5 = (f32[160,128]{1,0:T(8,128)S(1)}, f32[160,128]{1,0:T(8,128)S(1)}, u32[]{:S(2)}, u32[]{:S(2)}) collective-permute-start(f32[160,128]{1,0:T(8,128)S(1)} %select_add_fusion), channel_id=1, source_target_pairs={{0,16},{1,17},{2,18},{3,19},{4,20},{5,21},{6,22},{7,23},{8,24},{9,... | collective-permute-start | bytes 245768 | tf_op jit(solution)/shard_map/ppermute | solution.py:479
  47.2 6.6 %collective-permute-start.8 = (f32[160,128]{1,0:T(8,128)S(1)}, f32[160,128]{1,0:T(8,128)S(1)}, u32[]{:S(2)}, u32[]{:S(2)}) collective-permute-start(f32[160,128]{1,0:T(8,128)S(1)} %add.30), channel_id=1, source_target_pairs={{0,144},{1,145},{2,146},{3,147},{4,148},{5,149},{6,150},{7,151},{8... | collective-permute-start | bytes 245768 | tf_op jit(solution)/shard_map/ppermute | solution.py:479
  53.9 4.2 %collective-permute-start.9 = (f32[160,128]{1,0:T(8,128)S(1)}, f32[160,128]{1,0:T(8,128)S(1)}, u32[]{:S(2)}, u32[]{:S(2)}) collective-permute-start(f32[160,128]{1,0:T(8,128)S(1)} %add.31), channel_id=1, source_target_pairs={{0,32},{1,33},{2,34},{3,35},{4,36},{5,37},{6,38},{7,39},{8,40},{9,... | collective-permute-start | bytes 245768 | tf_op jit(solution)/shard_map/ppermute | solution.py:479
  54.4 4.8 %collective-permute-start.10 = (f32[2,40,128]{2,1,0:T(8,128)S(1)}, f32[2,40,128]{2,1,0:T(8,128)S(1)}, u32[]{:S(2)}, u32[]{:S(2)}) collective-permute-start(f32[2,40,128]{2,1,0:T(8,128)S(1)} %get-tuple-element.68), channel_id=1, source_target_pairs={{0,1},{1,2},{2,3},{3,4},{4,5},{5,6},{6,7},{7,8},{8,9},{9,10},{10,1... | collective-permute-start | bytes 122888 | tf_op jit(solution)/shard_map/ppermute | solution.py:447
  58.1 3.7 %collective-permute-start.11 = (f32[2,40,128]{2,1,0:T(8,128)S(1)}, f32[2,40,128]{2,1,0:T(8,128)S(1)}, u32[]{:S(2)}, u32[]{:S(2)}) collective-permute-start(f32[2,40,128]{2,1,0:T(8,128)S(1)} %get-tuple-element.69), channel_id=1, source_target_pairs={{1,0},{2,1},{3,2},{4,3},{5,4},{6,5},{7,6},{8,7},{9,8},{10,9},{11,1... | collective-permute-start | bytes 122888 | tf_op jit(solution)/shard_map/ppermute | solution.py:448
  61.8 8.3 %collective-permute-start.12 = (f32[160,128]{1,0:T(8,128)S(1)}, f32[160,128]{1,0:T(8,128)S(1)}, u32[]{:S(2)}, u32[]{:S(2)}) collective-permute-start(f32[160,128]{1,0:T(8,128)S(1)} %add.32), channel_id=1, source_target_pairs={{0,96},{1,97},{2,98},{3,99},{4,100},{5,101},{6,102},{7,103},{8,104... | collective-permute-start | bytes 245768 | tf_op jit(solution)/shard_map/ppermute | solution.py:479
  70.1 3.4 %collective-permute-start.13 = (f32[160,128]{1,0:T(8,128)S(1)}, f32[160,128]{1,0:T(8,128)S(1)}, u32[]{:S(2)}, u32[]{:S(2)}) collective-permute-start(f32[160,128]{1,0:T(8,128)S(1)} %add.33), channel_id=1, source_target_pairs={{0,2},{1,3},{2,0},{3,1},{4,6},{5,7},{6,4},{7,5},{8,10},{9,11},{10,... | collective-permute-start | bytes 245768 | tf_op jit(solution)/shard_map/ppermute | solution.py:479
  73.5 6.5 %collective-permute-start.14 = (f32[160,128]{1,0:T(8,128)S(1)}, f32[160,128]{1,0:T(8,128)S(1)}, u32[]{:S(2)}, u32[]{:S(2)}) collective-permute-start(f32[160,128]{1,0:T(8,128)S(1)} %add.34), channel_id=1, source_target_pairs={{0,4},{1,5},{2,6},{3,7},{4,0},{5,1},{6,2},{7,3},{8,12},{9,13},{10,... | collective-permute-start | bytes 245768 | tf_op jit(solution)/shard_map/ppermute | solution.py:479
  80.0 13.1 %copy-start.4 = (f32[49,128]{1,0:T(8,128)S(1)}, f32[49,128]{1,0:T(8,128)}, u32[]{:S(2)}) copy-start(f32[49,128]{1,0:T(8,128)} %constant.40.clone.pick) | copy-start | bytes 75268
  80.0 7.3 %collective-permute-start.15 = (f32[160,128]{1,0:T(8,128)S(1)}, f32[160,128]{1,0:T(8,128)S(1)}, u32[]{:S(2)}, u32[]{:S(2)}) collective-permute-start(f32[160,128]{1,0:T(8,128)S(1)} %add.35), channel_id=1, source_target_pairs={{0,8},{1,9},{2,10},{3,11},{4,12},{5,13},{6,14},{7,15},{8,0},{9,1},... | collective-permute-start | bytes 245768 | tf_op jit(solution)/shard_map/ppermute | solution.py:479
  87.4 5.7 %collective-permute-start.16 = (f32[160,128]{1,0:T(8,128)S(1)}, f32[160,128]{1,0:T(8,128)S(1)}, u32[]{:S(2)}, u32[]{:S(2)}) collective-permute-start(f32[160,128]{1,0:T(8,128)S(1)} %add.36), channel_id=1, source_target_pairs={{0,1},{1,0},{2,3},{3,2},{4,5},{5,4},{6,7},{7,6},{8,9},{9,8},{10,11... | collective-permute-start | bytes 245768 | tf_op jit(solution)/shard_map/ppermute | solution.py:490

commit v3 on v2

--- a/solution.py
+++ b/solution.py
@@ -22,6 +22,7 @@
 SPAN = 40
 NEAR = 9
 PART = 16
+TOGETHER = 8
 
 
 def call(body, out_shape, args, scratch=(), smem_first=False, flops=0, nbytes=0, name=None, mib=8):
@@ -199,22 +200,22 @@
         acc[...] = jnp.zeros_like(acc)
 
     def wide(x):
-        return jnp.concatenate([x, x], axis=1)
+        return jnp.concatenate([x] * TOGETHER, axis=1)
 
     def fold(x):
-        return x[:, :COLS] + x[:, COLS:]
+        return sum(x[:, n * COLS : (n + 1) * COLS] for n in range(TOGETHER))
 
     def pair(ref, r):
-        return jnp.concatenate([row_of(ref, r)[...], row_of(ref, r + 1)[...]], axis=1)
+        return jnp.concatenate([row_of(ref, r + n)[...] for n in range(TOGETHER)], axis=1)
 
     def mean(x):
         return jnp.sum(x, axis=0, keepdims=True) * (1.0 / CH)
 
     cells = (((1,), (1,)), ((), ()))
-    ones = jnp.where(iota((16, 2 * COLS), 0) == 0, 1.0, 0.0).astype(bf16)
+    ones = jnp.where(iota((16, TOGETHER * COLS), 0) == 0, 1.0, 0.0).astype(bf16)
 
     def point_step(i, carry):
-        r = 2 * i
+        r = TOGETHER * i
         conv_bias, gain, shift, out_bias, scale = (wide(chan[n]) for n in range(5))
         x = pair(conv_out, r) + conv_bias
         centre = x - mean(x)
@@ -229,15 +230,15 @@
         t = jnp.tanh(u * (tanh_scale + bent))
         s = 1.0 + t
         hidden = (u * s).astype(bf16)
-        slope = s + s * (1.0 - t) * (u * (tanh_scale + 3.0 * bent))
+        slope = s * (1.0 + (1.0 - t) * (u * (tanh_scale + 3.0 * bent)))
         pre_grad = (half_grad * slope).astype(bf16)
         mixed = jnp.dot(w_out_t[...], hidden, preferred_element_type=f32) + out_bias
         normed_grad = jnp.dot(w_in[...], pre_grad, preferred_element_type=f32)
         win_acc[...] += lax.dot_general(normed, pre_grad, cells, preferred_element_type=f32)
         wout_acc[...] += lax.dot_general(hidden, mixed_grad, cells, preferred_element_type=f32)
         change = scale * mixed
-        row_of(delta, r)[...] = change[:, :COLS]
-        row_of(delta, r + 1)[...] = change[:, COLS:]
+        for n in range(TOGETHER):
+            row_of(delta, r + n)[...] = change[:, n * COLS : (n + 1) * COLS]
         scale_acc[...] += fold(masked_cot * mixed)
         obias_acc[...] += fold(mixed_grad.astype(f32))
         slant = normed_grad * unit
@@ -245,13 +246,13 @@
         shift_acc[...] += fold(normed_grad)
         q = normed_grad * gain
         grad = inv_std * (q - mean(q) - unit * mean(slant * gain))
-        for n in range(2):
+        for n in range(TOGETHER):
             part = grad[:, n * COLS : (n + 1) * COLS]
             row_of(conv_grad, r + n)[...] = part
             row_of(grad_back, ROWS - 1 - r - n)[...] = part
         return carry
 
-    lax.fori_loop(0, ROWS // 2, point_step, 0, unroll=2)
+    lax.fori_loop(0, ROWS // TOGETHER, point_step, 0)
 
     for g in range(3):
         bottom[g] = row_of(conv_grad, g)[...]
@@ -269,7 +270,7 @@
                 acc = tile if acc is None else acc + tile
             taps_acc[p, pl.ds(k, 1), :] = jnp.sum(acc, axis=0, keepdims=True)
 
-    by_channel(grad_step)
+    by_channel(grad_step, 16)
 
     lane = iota((CH, COLS), 1)
 
@@ -473,20 +474,25 @@
     half = sums.shape[0] // 2
     low, high = sums[:half], sums[half:]
     mine = jnp.where(odd, high, low) + lax.ppermute(jnp.where(odd, low, high), "lon", core_pairs())
+    mine, top, bottom = tie(mine, top, bottom)
     from_a, from_b = exchange_rows(flags, top, bottom)
 
     def hop(x, *flips):
         return x + lax.ppermute(x, AXES, chip_pairs(*flips))
 
-    mine, from_a, from_b = tie(hop(mine, 1, 0, 0), from_a, from_b)
+    mine = hop(mine, 1, 0, 0)
+    mine, from_a, from_b = tie(hop(mine, 3, 0, 0), from_a, from_b)
     north, south, to_west, to_east = settle_edges(flags, from_a, from_b, conv_grad)
-    mine, to_west, to_east = tie(hop(mine, 3, 0, 0), to_west, to_east)
+    mine, to_west, to_east = tie(hop(mine, 0, 1, 0), to_west, to_east)
     west, east = exchange_columns(to_west, to_east)
-    mine, west, east = tie(hop(mine, 0, 1, 0), west, east)
-    done = ()
-    for c, flips in enumerate(((0, 3, 0), (0, 0, 1), (0, 0, 2), (0, 0, 4))):
-        done = finish(c, done, south, north, west, east)
-        mine, *done = tie(hop(mine, *flips), *done)
+    mine, west, east = tie(hop(mine, 0, 3, 0), west, east)
+    done = finish(0, (), south, north, west, east)
+    mine, *done = tie(hop(mine, 0, 0, 1), *done)
+    done = finish(1, done, south, north, west, east)
+    mine, *done = tie(hop(mine, 0, 0, 2), *done)
+    done = finish(2, done, south, north, west, east)
+    done = finish(3, done, south, north, west, east)
+    mine, *done = tie(hop(mine, 0, 0, 4), *done)
     other = lax.ppermute(mine, "lon", core_pairs())
     total = jnp.concatenate([jnp.where(odd, other, mine), jnp.where(odd, mine, other)], axis=0)
     return total, done

time: 94.5 us -> 89.6 us (0.948)
  starting transfers between devices: 44.4 us -> 37.2 us
  waiting for transfers between devices: 10.7 us -> 15.9 us
  Pallas kernels: 32.5 us -> 29.8 us
    ppermute x7, waiting for transfers between devices: 2.93 us -> 7.5 us  [hop(): return x + lax.ppermute(x, AXES, chip_pairs(*flips))]
    ppermute x1, starting transfers between devices: 4.79 us -> 0.82 us  [reduce_and_spread(): other = lax.ppermute(mine, 'lon', core_pairs())]
    ppermute x7, starting transfers between devices: 20.5 us -> 17.6 us  [hop(): return x + lax.ppermute(x, AXES, chip_pairs(*flips))]
    pallas_call x4, Pallas kernels: 21.5 us -> 18.7 us  [call(): pl.pallas_call(body, out_shape=out_shape, in_specs=specs, out_specs=jax.t...]
    ppermute x2, starting transfers between devices: 6.5 us -> 5.26 us  [exchange_columns(): west = lax.ppermute(to_east, 'lon', up)]
  transfers between devices with their start and end apart: 17 -> 17, of which waited for: 9 -> 10; matrix products, arithmetic and copies ran while one was open for 4% -> 5% of each run, Pallas kernels for 13% -> 14%
where the time goes in v3:
time: 89.6 us; the launch traced here: 89.3 us
  starting transfers between devices  37.2 us (42%)
  Pallas kernels  29.8 us (33%)
  waiting for transfers between devices  15.9 us (18%)
  local copies, waits for them, and re-layouts  3.08 us (3%)
  matrix products  1.22 us (1%)
  other arithmetic  1.11 us (1%)
  between operations  1.01 us (1%)
    pallas_call x4, Pallas kernels, call(): pl.pallas_call(body, out_shape=out_shape, in_specs=specs, out_specs=jax.t...  18.7 us
    ppermute x7, starting transfers between devices, hop(): return x + lax.ppermute(x, AXES, chip_pairs(*flips))  17.6 us
    pallas_call x4, Pallas kernels, spread_part(): pl.pallas_call(functools.partial(spread_body, first=c * PART % 32), grid=...  11.1 us
    ppermute x2, starting transfers between devices, exchange_rows(): from_a = lax.ppermute(jnp.where(even, top, bottom), AXES, first)  9.46 us
    ppermute x7, waiting for transfers between devices, hop(): return x + lax.ppermute(x, AXES, chip_pairs(*flips))  7.5 us
    ppermute x2, starting transfers between devices, exchange_columns(): west = lax.ppermute(to_east, 'lon', up)  5.26 us
    ppermute x2, waiting for transfers between devices, exchange_columns(): east = lax.ppermute(to_west, 'lon', down)  4.65 us
    ppermute x1, starting transfers between devices, reduce_and_spread(): lax.ppermute(jnp.where(odd, low, high), 'lon', core_pairs())  2.57 us
  transfers between devices with their start and end apart: 17, of which 10 were waited for; matrix products, arithmetic and copies ran while one was open for 5% of the time, Pallas kernels for 14%

profile of v3, /device:TPU:1, one launch (start us, length us, event | category | flops | bytes accessed | tf_op | source)
XLA Modules:
  0.0 89.3 jit_solution(18356736684579963930)
XLA Ops:
  0.6 0.0 copy-start
  0.7 0.0 copy-start.1
  0.7 0.0 copy-start.6
  0.7 0.0 copy-start.7
  0.7 0.0 copy-start.8
  0.7 0.0 copy-start.9
  0.7 0.0 copy-start.10
  0.7 1.1 %fusion.3 = (bf16[64,3,128]{2,1,0:T(4,128)(2,1)S(1)}, bf16[64,3,128]{2,1,0:T(4,128)(2,1)S(1)}) fusion(bf16[64,32,128]{2,1,0:T(8,128)(2,1)} %state.9), kind=kLoop, calls=%fused_computation.17 | loop fusion | bytes 196608 | tf_op jit(solution)/shard_map/slice | solution.py:518
  1.8 0.0 copy-start.2
  1.8 0.0 copy-start.3
  1.9 0.8 collective-permute-start.1
  2.7 4.7 %collective-permute-start = (f32[3,64,128]{2,1,0:T(8,128)S(1)}, f32[3,64,128]{2,1,0:T(8,128)S(1)}, u32[]{:S(2)}, u32[]{:S(2)}) collective-permute-start(f32[3,64,128]{2,1,0:T(8,128)S(1)} %get-tuple-element.108), channel_id=1, source_target_pairs={{0,32},{1,33},{2,34},{3,35},{4,36},{5,37},{6,38},{7,39},{8,40},{9,... | collective-permute-start | bytes 294920 | tf_op jit(solution)/shard_map/ppermute | solution.py:424
  7.4 0.7 broadcast_in_dim.15
  8.2 0.9 copy.34
  9.0 0.8 fusion.2
  9.8 0.1 pad.4.clone
  9.9 1.0 %convolution_bitcast_fusion.1.taps = f32[64,512]{1,0:T(8,128)S(1)} fusion(bf16[49,512]{1,0:T(8,128)(2,1)} %constant.41, bf16[64,49]{0,1:T(8,128)(2,1)S(1)} %copy-done), kind=kOutput, calls=%fused_computation.1 | convolution fusion | flops 3211264 | bytes 187520 | tf_op jit(solution)/shard_map/dot_general | solution.py:523
  10.9 0.1 pad_add_fusion.flags
  11.0 0.0 collective-permute-done.1.from_b
  11.0 0.0 collective-permute-done.from_a
  11.0 0.0 copy-done.1
  11.0 1.1 %edges.2 = (f32[3,64,128]{2,1,0:T(8,128)S(1)}, f32[3,64,128]{2,1,0:T(8,128)S(1)}, f32[2,40,128]{2,1,0:T(8,128)S(1)}, f32[2,40,128]{2,1,0:T(8,128)S(1)}) custom-call(s32[2]{0:T(128)S(1)} %pad_add_fusion.flags, f32[3,64,128]{2,1,0:T(8,128)S(1)} %collective-permute-done.from_a, f32[3,64,128]{2,1,0:T(8,128)S(1)} %collective-permute-done.1.from_b, ...), custom_call_target="tpu_custom_call" | custom-call | flops 1048576 | bytes 2097152 | tf_op jit(solution)/shard_map/edges/pallas_call | solution.py:32
  12.1 2.8 %collective-permute-start.2 = (f32[2,40,128]{2,1,0:T(8,128)S(1)}, f32[2,40,128]{2,1,0:T(8,128)S(1)}, u32[]{:S(2)}, u32[]{:S(2)}) collective-permute-start(f32[2,40,128]{2,1,0:T(8,128)S(1)} %get-tuple-element.56), channel_id=1, source_target_pairs={{0,1},{1,2},{2,3},{3,4},{4,5},{5,6},{6,7},{7,8},{8,9},{9,10},{10,1... | collective-permute-start | bytes 122888 | tf_op jit(solution)/shard_map/ppermute | solution.py:448
  14.9 0.0 collective-permute-start.3
  14.9 0.1 maximum_maximum_fusion.w_in_t
  15.1 0.1 copy.36.w_out
  15.3 0.8 collective-permute-done.2.west
  16.0 2.3 %collective-permute-done.3.east = f32[2,40,128]{2,1,0:T(8,128)S(1)} collective-permute-done((f32[2,40,128]{2,1,0:T(8,128)S(1)}, f32[2,40,128]{2,1,0:T(8,128)S(1)}, u32[]{:S(2)}, u32[]{:S(2)}) %collective-permute-start.3) | collective-permute-done | bytes 40992 | tf_op jit(solution)/shard_map/ppermute | solution.py:449
  18.4 0.1 broadcast_in_dim.12.chan
  18.5 15.4 %main.1 = (f32[2112,128]{1,0:T(8,128)S(1)}, f32[2112,128]{1,0:T(8,128)S(1)}, f32[3,64,128]{2,1,0:T(8,128)S(1)}, f32[3,64,128]{2,1,0:T(8,128)S(1)}, f32[320,128]{1,0:T(8,128)S(1)}) custom-call(bf16[64,32,128]{2,1,0:T(8,128)(2,1)S(1)} %copy-done.1, f32[3,64,128]{2,1,0:T(8,128)S(1)} %get-tuple-element.54.south, f32[3,64,128]{2,1,0:T(8,128)S(1)} %get-tuple-element.55.north, ...), custom_call_target="tpu_custom_call" | custom-call | flops 1073741824 | bytes 8388608 | tf_op jit(solution)/shard_map/main/pallas_call | solution.py:32
  34.0 2.6 %collective-permute-start.4 = (f32[160,128]{1,0:T(8,128)S(1)}, f32[160,128]{1,0:T(8,128)S(1)}, u32[]{:S(2)}, u32[]{:S(2)}) collective-permute-start(f32[160,128]{1,0:T(8,128)S(1)} %slice_select_fusion), channel_id=1, source_target_pairs={{0,1},{1,0},{2,3},{3,2},{4,5},{5,4},{6,7},{7,6},{8,9},{9,8},{10,11... | collective-permute-start | bytes 245768 | tf_op jit(solution)/shard_map/ppermute | solution.py:476
  36.5 0.9 %collective-permute-done.4 = f32[160,128]{1,0:T(8,128)S(1)} collective-permute-done((f32[160,128]{1,0:T(8,128)S(1)}, f32[160,128]{1,0:T(8,128)S(1)}, u32[]{:S(2)}, u32[]{:S(2)}) %collective-permute-start.4) | collective-permute-done | bytes 81952 | tf_op jit(solution)/shard_map/ppermute | solution.py:476
  37.5 0.3 collective-permute-start.5
  37.8 0.7 collective-permute-start.8
  38.5 0.0 copy-start.5
  38.5 4.7 %collective-permute-start.7 = (f32[3,64,128]{2,1,0:T(8,128)S(1)}, f32[3,64,128]{2,1,0:T(8,128)S(1)}, u32[]{:S(2)}, u32[]{:S(2)}) collective-permute-start(f32[3,64,128]{2,1,0:T(8,128)S(1)} %get-tuple-element.104), channel_id=1, source_target_pairs={{0,32},{1,33},{2,34},{3,35},{4,36},{5,37},{6,38},{7,39},{8,40},{9,... | collective-permute-start | bytes 294920 | tf_op jit(solution)/shard_map/ppermute | solution.py:424
  43.2 0.0 collective-permute-done.5
  43.3 4.2 %collective-permute-start.6 = (f32[160,128]{1,0:T(8,128)S(1)}, f32[160,128]{1,0:T(8,128)S(1)}, u32[]{:S(2)}, u32[]{:S(2)}) collective-permute-start(f32[160,128]{1,0:T(8,128)S(1)} %add.30), channel_id=1, source_target_pairs={{0,144},{1,145},{2,146},{3,147},{4,148},{5,149},{6,150},{7,151},{8... | collective-permute-start | bytes 245768 | tf_op jit(solution)/shard_map/ppermute | solution.py:481
  47.5 2.7 %collective-permute-done.6 = f32[160,128]{1,0:T(8,128)S(1)} collective-permute-done((f32[160,128]{1,0:T(8,128)S(1)}, f32[160,128]{1,0:T(8,128)S(1)}, u32[]{:S(2)}, u32[]{:S(2)}) %collective-permute-start.6) | collective-permute-done | bytes 81952 | tf_op jit(solution)/shard_map/ppermute | solution.py:481
  50.2 0.0 collective-permute-done.8.from_b
  50.3 0.0 collective-permute-done.7.from_a
  50.3 0.1 collective-permute-start.9
  50.4 1.3 %edges.3 = (f32[3,64,128]{2,1,0:T(8,128)S(1)}, f32[3,64,128]{2,1,0:T(8,128)S(1)}, f32[2,40,128]{2,1,0:T(8,128)S(1)}, f32[2,40,128]{2,1,0:T(8,128)S(1)}) custom-call(s32[2]{0:T(128)S(1)} %pad_add_fusion.flags, f32[3,64,128]{2,1,0:T(8,128)S(1)} %collective-permute-done.7.from_a, f32[3,64,128]{2,1,0:T(8,128)S(1)} %collective-permute-done.8.from_b, ...), custom_call_target="tpu_custom_call" | custom-call | flops 1048576 | bytes 2097152 | tf_op jit(solution)/shard_map/edges/pallas_call | solution.py:32
  51.7 1.9 %collective-permute-done.9 = f32[160,128]{1,0:T(8,128)S(1)} collective-permute-done((f32[160,128]{1,0:T(8,128)S(1)}, f32[160,128]{1,0:T(8,128)S(1)}, u32[]{:S(2)}, u32[]{:S(2)}) %collective-permute-start.9) | collective-permute-done | bytes 81952 | tf_op jit(solution)/shard_map/ppermute | solution.py:481
  53.7 5.3 %collective-permute-start.10 = (f32[160,128]{1,0:T(8,128)S(1)}, f32[160,128]{1,0:T(8,128)S(1)}, u32[]{:S(2)}, u32[]{:S(2)}) collective-permute-start(f32[160,128]{1,0:T(8,128)S(1)} %add.32), channel_id=1, source_target_pairs={{0,96},{1,97},{2,98},{3,99},{4,100},{5,101},{6,102},{7,103},{8,104... | collective-permute-start | bytes 245768 | tf_op jit(solution)/shard_map/ppermute | solution.py:481
  58.9 2.4 %collective-permute-start.11 = (f32[2,40,128]{2,1,0:T(8,128)S(1)}, f32[2,40,128]{2,1,0:T(8,128)S(1)}, u32[]{:S(2)}, u32[]{:S(2)}) collective-permute-start(f32[2,40,128]{2,1,0:T(8,128)S(1)} %get-tuple-element.71), channel_id=1, source_target_pairs={{0,1},{1,2},{2,3},{3,4},{4,5},{5,6},{6,7},{7,8},{8,9},{9,10},{10,1... | collective-permute-start | bytes 122888 | tf_op jit(solution)/shard_map/ppermute | solution.py:448
  61.4 0.0 collective-permute-start.12
  61.4 0.0 collective-permute-done.10
  61.4 1.1 %collective-permute-done.11.west = f32[2,40,128]{2,1,0:T(8,128)S(1)} collective-permute-done((f32[2,40,128]{2,1,0:T(8,128)S(1)}, f32[2,40,128]{2,1,0:T(8,128)S(1)}, u32[]{:S(2)}, u32[]{:S(2)}) %collective-permute-start.11) | collective-permute-done | bytes 40992 | tf_op jit(solution)/shard_map/ppermute | solution.py:448
  62.5 2.3 %collective-permute-done.12.east = f32[2,40,128]{2,1,0:T(8,128)S(1)} collective-permute-done((f32[2,40,128]{2,1,0:T(8,128)S(1)}, f32[2,40,128]{2,1,0:T(8,128)S(1)}, u32[]{:S(2)}, u32[]{:S(2)}) %collective-permute-start.12) | collective-permute-done | bytes 40992 | tf_op jit(solution)/shard_map/ppermute | solution.py:449
  64.8 0.5 collective-permute-start.13
  65.3 0.2 convolution_bitcast_fusion.turned_taps
  65.5 2.7 %spread.4 = (bf16[64,32,128]{2,1,0:T(8,128)(2,1)}, bf16[64,32,128]{2,1,0:T(8,128)(2,1)}) custom-call(s32[2]{0:T(128)S(1)} %pad_add_fusion.flags, f32[2112,128]{1,0:T(8,128)S(1)} %get-tuple-element.67.own.conv_grad, f32[3,64,128]{2,1,0:T(8,128)S(1)} %get-tuple-element.74.south, f32[3,64,128]{2,1,0:T(8,128)S(1)} %get-tuple-element.75.north, ...), custom_call_target="tpu_custom_call" | custom-call | flops 16777216 | bytes 3145728 | tf_op jit(solution)/shard_map/spread/pallas_call | solution.py:358
  68.2 0.0 collective-permute-done.13
  68.3 4.2 %collective-permute-start.14 = (f32[160,128]{1,0:T(8,128)S(1)}, f32[160,128]{1,0:T(8,128)S(1)}, u32[]{:S(2)}, u32[]{:S(2)}) collective-permute-start(f32[160,128]{1,0:T(8,128)S(1)} %add.34), channel_id=1, source_target_pairs={{0,4},{1,5},{2,6},{3,7},{4,0},{5,1},{6,2},{7,3},{8,12},{9,13},{10,... | collective-permute-start | bytes 245768 | tf_op jit(solution)/shard_map/ppermute | solution.py:481
  72.5 2.8 %spread.5 = (bf16[64,32,128]{2,1,0:T(8,128)(2,1)}, bf16[64,32,128]{2,1,0:T(8,128)(2,1)}) custom-call(s32[2]{0:T(128)S(1)} %pad_add_fusion.flags, f32[2112,128]{1,0:T(8,128)S(1)} %get-tuple-element.67.own.conv_grad, f32[3,64,128]{2,1,0:T(8,128)S(1)} %get-tuple-element.74.south, ...), custom_call_target="tpu_custom_call", output_to_operand_aliasing={{0}: (12, {}), {1}: (13, {})} | custom-call | flops 16777216 | bytes 3145728 | tf_op jit(solution)/shard_map/spread/pallas_call | solution.py:358
  75.3 1.4 %collective-permute-done.14 = f32[160,128]{1,0:T(8,128)S(1)} collective-permute-done((f32[160,128]{1,0:T(8,128)S(1)}, f32[160,128]{1,0:T(8,128)S(1)}, u32[]{:S(2)}, u32[]{:S(2)}) %collective-permute-start.14) | collective-permute-done | bytes 81952 | tf_op jit(solution)/shard_map/ppermute | solution.py:481
  76.7 2.9 %collective-permute-start.15 = (f32[160,128]{1,0:T(8,128)S(1)}, f32[160,128]{1,0:T(8,128)S(1)}, u32[]{:S(2)}, u32[]{:S(2)}) collective-permute-start(f32[160,128]{1,0:T(8,128)S(1)} %add.35), channel_id=1, source_target_pairs={{0,8},{1,9},{2,10},{3,11},{4,12},{5,13},{6,14},{7,15},{8,0},{9,1},... | collective-permute-start | bytes 245768 | tf_op jit(solution)/shard_map/ppermute | solution.py:481
  79.6 2.8 %spread.6 = (bf16[64,32,128]{2,1,0:T(8,128)(2,1)}, bf16[64,32,128]{2,1,0:T(8,128)(2,1)}) custom-call(s32[2]{0:T(128)S(1)} %pad_add_fusion.flags, f32[2112,128]{1,0:T(8,128)S(1)} %get-tuple-element.67.own.conv_grad, f32[3,64,128]{2,1,0:T(8,128)S(1)} %get-tuple-element.74.south, ...), custom_call_target="tpu_custom_call", output_to_operand_aliasing={{0}: (12, {}), {1}: (13, {})} | custom-call | flops 16777216 | bytes 3145728 | tf_op jit(solution)/shard_map/spread/pallas_call | solution.py:358
  82.4 2.8 %spread.7 = (bf16[64,32,128]{2,1,0:T(8,128)(2,1)}, bf16[64,32,128]{2,1,0:T(8,128)(2,1)}) custom-call(s32[2]{0:T(128)S(1)} %pad_add_fusion.flags, f32[2112,128]{1,0:T(8,128)S(1)} %get-tuple-element.67.own.conv_grad, f32[3,64,128]{2,1,0:T(8,128)S(1)} %get-tuple-element.74.south, ...), custom_call_target="tpu_custom_call", output_to_operand_aliasing={{0}: (12, {}), {1}: (13, {})} | custom-call | flops 16777216 | bytes 3145728 | tf_op jit(solution)/shard_map/spread/pallas_call | solution.py:358
  85.2 1.4 %collective-permute-done.15 = f32[160,128]{1,0:T(8,128)S(1)} collective-permute-done((f32[160,128]{1,0:T(8,128)S(1)}, f32[160,128]{1,0:T(8,128)S(1)}, u32[]{:S(2)}, u32[]{:S(2)}) %collective-permute-start.15) | collective-permute-done | bytes 81952 | tf_op jit(solution)/shard_map/ppermute | solution.py:481
  86.6 0.8 collective-permute-start.16
  87.4 0.9 %collective-permute-done.16 = f32[160,128]{1,0:T(8,128)S(1)} collective-permute-done((f32[160,128]{1,0:T(8,128)S(1)}, f32[160,128]{1,0:T(8,128)S(1)}, u32[]{:S(2)}, u32[]{:S(2)}) %collective-permute-start.16) | collective-permute-done | bytes 81952 | tf_op jit(solution)/shard_map/ppermute | solution.py:496
  88.4 0.9 %unpack.1 = (f32[49,64]{1,0:T(8,128)}, f32[64,256]{1,0:T(8,128)}, f32[64,256]{1,0:T(8,128)}, f32[1,256]{1,0:T(1,128)}, f32[5,64]{1,0:T(8,128)}) custom-call(f32[320,128]{1,0:T(8,128)S(1)} %pad_maximum_fusion.sums, f32[49,128]{1,0:T(8,128)S(1)} %copy-done.4), custom_call_target="tpu_custom_call" | custom-call | flops 131072 | bytes 262144 | tf_op jit(solution)/shard_map/unpack/pallas_call | solution.py:32
  (29 shorter events, 0.2 us)
Async XLA Ops:
  0.6 9.3 %copy-start = (bf16[64,49]{0,1:T(8,128)(2,1)S(1)}, bf16[64,49]{0,1:T(8,128)(2,1)}, u32[]{:S(2)}) copy-start(bf16[64,49]{0,1:T(8,128)(2,1)} %param.16) | copy-start | bytes 18820
  0.7 10.4 %copy-start.1 = (bf16[64,32,128]{2,1,0:T(8,128)(2,1)S(1)}, bf16[64,32,128]{2,1,0:T(8,128)(2,1)}, u32[]{:S(2)}) copy-start(bf16[64,32,128]{2,1,0:T(8,128)(2,1)} %state.9) | copy-start | bytes 1572868
  0.7 14.4 %copy-start.6 = (s32[32,128]{1,0:T(8,128)S(1)}, s32[32,128]{1,0:T(8,128)}, u32[]{:S(2)}) copy-start(s32[32,128]{1,0:T(8,128)} %param.25) | copy-start | bytes 49156
  0.7 14.5 %copy-start.7 = (bf16[64]{0:T(256)(128)(2,1)S(1)}, bf16[64]{0:T(256)(128)(2,1)}, u32[]{:S(2)}) copy-start(bf16[64]{0:T(256)(128)(2,1)} %param.17) | copy-start | bytes 388
  0.7 14.5 %copy-start.8 = (bf16[64]{0:T(256)(128)(2,1)S(1)}, bf16[64]{0:T(256)(128)(2,1)}, u32[]{:S(2)}) copy-start(bf16[64]{0:T(256)(128)(2,1)} %param.18) | copy-start | bytes 388
  0.7 14.5 %copy-start.9 = (bf16[64]{0:T(256)(128)(2,1)S(1)}, bf16[64]{0:T(256)(128)(2,1)}, u32[]{:S(2)}) copy-start(bf16[64]{0:T(256)(128)(2,1)} %param.19) | copy-start | bytes 388
  0.7 14.5 %copy-start.10 = (bf16[64]{0:T(256)(128)(2,1)S(1)}, bf16[64]{0:T(256)(128)(2,1)}, u32[]{:S(2)}) copy-start(bf16[64]{0:T(256)(128)(2,1)} %param.23) | copy-start | bytes 388
  0.7 14.5 %copy-start.11 = (bf16[64]{0:T(256)(128)(2,1)S(1)}, bf16[64]{0:T(256)(128)(2,1)}, u32[]{:S(2)}) copy-start(bf16[64]{0:T(256)(128)(2,1)} %param.24) | copy-start | bytes 388
  1.8 16.6 %copy-start.2 = (bf16[64,32,128]{2,1,0:T(8,128)(2,1)S(1)}, bf16[64,32,128]{2,1,0:T(8,128)(2,1)}, u32[]{:S(2)}) copy-start(bf16[64,32,128]{2,1,0:T(8,128)(2,1)} %cot.9) | copy-start | bytes 1572868
  1.8 16.6 %copy-start.3 = (bf16[64,256]{1,0:T(8,128)(2,1)S(1)}, bf16[64,256]{1,0:T(8,128)(2,1)}, u32[]{:S(2)}) copy-start(bf16[64,256]{1,0:T(8,128)(2,1)} %w_in.1) | copy-start | bytes 98308
  1.9 9.1 %collective-permute-start.1 = (f32[3,64,128]{2,1,0:T(8,128)S(1)}, f32[3,64,128]{2,1,0:T(8,128)S(1)}, u32[]{:S(2)}, u32[]{:S(2)}) collective-permute-start(f32[3,64,128]{2,1,0:T(8,128)S(1)} %get-tuple-element.107), channel_id=1, source_target_pairs={{32,64},{33,65},{34,66},{35,67},{36,68},{37,69},{38,70},{39,71},{4... | collective-permute-start | bytes 294920 | tf_op jit(solution)/shard_map/ppermute | solution.py:425
  2.7 8.3 %collective-permute-start = (f32[3,64,128]{2,1,0:T(8,128)S(1)}, f32[3,64,128]{2,1,0:T(8,128)S(1)}, u32[]{:S(2)}, u32[]{:S(2)}) collective-permute-start(f32[3,64,128]{2,1,0:T(8,128)S(1)} %get-tuple-element.108), channel_id=1, source_target_pairs={{0,32},{1,33},{2,34},{3,35},{4,36},{5,37},{6,38},{7,39},{8,40},{9,... | collective-permute-start | bytes 294920 | tf_op jit(solution)/shard_map/ppermute | solution.py:424
  12.1 3.9 %collective-permute-start.2 = (f32[2,40,128]{2,1,0:T(8,128)S(1)}, f32[2,40,128]{2,1,0:T(8,128)S(1)}, u32[]{:S(2)}, u32[]{:S(2)}) collective-permute-start(f32[2,40,128]{2,1,0:T(8,128)S(1)} %get-tuple-element.56), channel_id=1, source_target_pairs={{0,1},{1,2},{2,3},{3,4},{4,5},{5,6},{6,7},{7,8},{8,9},{9,10},{10,1... | collective-permute-start | bytes 122888 | tf_op jit(solution)/shard_map/ppermute | solution.py:448
  14.9 3.4 %collective-permute-start.3 = (f32[2,40,128]{2,1,0:T(8,128)S(1)}, f32[2,40,128]{2,1,0:T(8,128)S(1)}, u32[]{:S(2)}, u32[]{:S(2)}) collective-permute-start(f32[2,40,128]{2,1,0:T(8,128)S(1)} %get-tuple-element.57), channel_id=1, source_target_pairs={{1,0},{2,1},{3,2},{4,3},{5,4},{6,5},{7,6},{8,7},{9,8},{10,9},{11,1... | collective-permute-start | bytes 122888 | tf_op jit(solution)/shard_map/ppermute | solution.py:449
  34.0 3.5 %collective-permute-start.4 = (f32[160,128]{1,0:T(8,128)S(1)}, f32[160,128]{1,0:T(8,128)S(1)}, u32[]{:S(2)}, u32[]{:S(2)}) collective-permute-start(f32[160,128]{1,0:T(8,128)S(1)} %slice_select_fusion), channel_id=1, source_target_pairs={{0,1},{1,0},{2,3},{3,2},{4,5},{5,4},{6,7},{7,6},{8,9},{9,8},{10,11... | collective-permute-start | bytes 245768 | tf_op jit(solution)/shard_map/ppermute | solution.py:476
  37.5 5.8 %collective-permute-start.5 = (f32[160,128]{1,0:T(8,128)S(1)}, f32[160,128]{1,0:T(8,128)S(1)}, u32[]{:S(2)}, u32[]{:S(2)}) collective-permute-start(f32[160,128]{1,0:T(8,128)S(1)} %select_add_fusion), channel_id=1, source_target_pairs={{0,16},{1,17},{2,18},{3,19},{4,20},{5,21},{6,22},{7,23},{8,24},{9,... | collective-permute-start | bytes 245768 | tf_op jit(solution)/shard_map/ppermute | solution.py:481
  37.8 12.4 %collective-permute-start.8 = (f32[3,64,128]{2,1,0:T(8,128)S(1)}, f32[3,64,128]{2,1,0:T(8,128)S(1)}, u32[]{:S(2)}, u32[]{:S(2)}) collective-permute-start(f32[3,64,128]{2,1,0:T(8,128)S(1)} %get-tuple-element.103), channel_id=1, source_target_pairs={{32,64},{33,65},{34,66},{35,67},{36,68},{37,69},{38,70},{39,71},{4... | collective-permute-start | bytes 294920 | tf_op jit(solution)/shard_map/ppermute | solution.py:425
  38.5 26.8 %copy-start.5 = (bf16[49,512]{1,0:T(8,128)(2,1)S(1)}, bf16[49,512]{1,0:T(8,128)(2,1)}, u32[]{:S(2)}) copy-start(bf16[49,512]{1,0:T(8,128)(2,1)} %constant.42) | copy-start | bytes 150532
  38.5 11.7 %collective-permute-start.7 = (f32[3,64,128]{2,1,0:T(8,128)S(1)}, f32[3,64,128]{2,1,0:T(8,128)S(1)}, u32[]{:S(2)}, u32[]{:S(2)}) collective-permute-start(f32[3,64,128]{2,1,0:T(8,128)S(1)} %get-tuple-element.104), channel_id=1, source_target_pairs={{0,32},{1,33},{2,34},{3,35},{4,36},{5,37},{6,38},{7,39},{8,40},{9,... | collective-permute-start | bytes 294920 | tf_op jit(solution)/shard_map/ppermute | solution.py:424
  43.3 7.0 %collective-permute-start.6 = (f32[160,128]{1,0:T(8,128)S(1)}, f32[160,128]{1,0:T(8,128)S(1)}, u32[]{:S(2)}, u32[]{:S(2)}) collective-permute-start(f32[160,128]{1,0:T(8,128)S(1)} %add.30), channel_id=1, source_target_pairs={{0,144},{1,145},{2,146},{3,147},{4,148},{5,149},{6,150},{7,151},{8... | collective-permute-start | bytes 245768 | tf_op jit(solution)/shard_map/ppermute | solution.py:481
  50.3 3.4 %collective-permute-start.9 = (f32[160,128]{1,0:T(8,128)S(1)}, f32[160,128]{1,0:T(8,128)S(1)}, u32[]{:S(2)}, u32[]{:S(2)}) collective-permute-start(f32[160,128]{1,0:T(8,128)S(1)} %add.31), channel_id=1, source_target_pairs={{0,32},{1,33},{2,34},{3,35},{4,36},{5,37},{6,38},{7,39},{8,40},{9,... | collective-permute-start | bytes 245768 | tf_op jit(solution)/shard_map/ppermute | solution.py:481
  53.7 7.7 %collective-permute-start.10 = (f32[160,128]{1,0:T(8,128)S(1)}, f32[160,128]{1,0:T(8,128)S(1)}, u32[]{:S(2)}, u32[]{:S(2)}) collective-permute-start(f32[160,128]{1,0:T(8,128)S(1)} %add.32), channel_id=1, source_target_pairs={{0,96},{1,97},{2,98},{3,99},{4,100},{5,101},{6,102},{7,103},{8,104... | collective-permute-start | bytes 245768 | tf_op jit(solution)/shard_map/ppermute | solution.py:481
  58.9 3.5 %collective-permute-start.11 = (f32[2,40,128]{2,1,0:T(8,128)S(1)}, f32[2,40,128]{2,1,0:T(8,128)S(1)}, u32[]{:S(2)}, u32[]{:S(2)}) collective-permute-start(f32[2,40,128]{2,1,0:T(8,128)S(1)} %get-tuple-element.71), channel_id=1, source_target_pairs={{0,1},{1,2},{2,3},{3,4},{4,5},{5,6},{6,7},{7,8},{8,9},{9,10},{10,1... | collective-permute-start | bytes 122888 | tf_op jit(solution)/shard_map/ppermute | solution.py:448
  61.4 3.4 %collective-permute-start.12 = (f32[2,40,128]{2,1,0:T(8,128)S(1)}, f32[2,40,128]{2,1,0:T(8,128)S(1)}, u32[]{:S(2)}, u32[]{:S(2)}) collective-permute-start(f32[2,40,128]{2,1,0:T(8,128)S(1)} %get-tuple-element.72), channel_id=1, source_target_pairs={{1,0},{2,1},{3,2},{4,3},{5,4},{6,5},{7,6},{8,7},{9,8},{10,9},{11,1... | collective-permute-start | bytes 122888 | tf_op jit(solution)/shard_map/ppermute | solution.py:449
  64.8 3.5 %collective-permute-start.13 = (f32[160,128]{1,0:T(8,128)S(1)}, f32[160,128]{1,0:T(8,128)S(1)}, u32[]{:S(2)}, u32[]{:S(2)}) collective-permute-start(f32[160,128]{1,0:T(8,128)S(1)} %add.33), channel_id=1, source_target_pairs={{0,2},{1,3},{2,0},{3,1},{4,6},{5,7},{6,4},{7,5},{8,10},{9,11},{10,... | collective-permute-start | bytes 245768 | tf_op jit(solution)/shard_map/ppermute | solution.py:481
  68.3 8.4 %collective-permute-start.14 = (f32[160,128]{1,0:T(8,128)S(1)}, f32[160,128]{1,0:T(8,128)S(1)}, u32[]{:S(2)}, u32[]{:S(2)}) collective-permute-start(f32[160,128]{1,0:T(8,128)S(1)} %add.34), channel_id=1, source_target_pairs={{0,4},{1,5},{2,6},{3,7},{4,0},{5,1},{6,2},{7,3},{8,12},{9,13},{10,... | collective-permute-start | bytes 245768 | tf_op jit(solution)/shard_map/ppermute | solution.py:481
  76.7 9.9 %collective-permute-start.15 = (f32[160,128]{1,0:T(8,128)S(1)}, f32[160,128]{1,0:T(8,128)S(1)}, u32[]{:S(2)}, u32[]{:S(2)}) collective-permute-start(f32[160,128]{1,0:T(8,128)S(1)} %add.35), channel_id=1, source_target_pairs={{0,8},{1,9},{2,10},{3,11},{4,12},{5,13},{6,14},{7,15},{8,0},{9,1},... | collective-permute-start | bytes 245768 | tf_op jit(solution)/shard_map/ppermute | solution.py:481
  82.4 6.0 %copy-start.4 = (f32[49,128]{1,0:T(8,128)S(1)}, f32[49,128]{1,0:T(8,128)}, u32[]{:S(2)}) copy-start(f32[49,128]{1,0:T(8,128)} %constant.40.clone.pick) | copy-start | bytes 75268
  86.6 1.7 %collective-permute-start.16 = (f32[160,128]{1,0:T(8,128)S(1)}, f32[160,128]{1,0:T(8,128)S(1)}, u32[]{:S(2)}, u32[]{:S(2)}) collective-permute-start(f32[160,128]{1,0:T(8,128)S(1)} %add.36), channel_id=1, source_target_pairs={{0,1},{1,0},{2,3},{3,2},{4,5},{5,4},{6,7},{7,6},{8,9},{9,8},{10,11... | collective-permute-start | bytes 245768 | tf_op jit(solution)/shard_map/ppermute | solution.py:496

commit v4 on v3

--- a/solution.py
+++ b/solution.py
@@ -480,19 +480,19 @@
     def hop(x, *flips):
         return x + lax.ppermute(x, AXES, chip_pairs(*flips))
 
-    mine = hop(mine, 1, 0, 0)
-    mine, from_a, from_b = tie(hop(mine, 3, 0, 0), from_a, from_b)
+    mine = hop(mine, 0, 1, 0)
+    mine, from_a, from_b = tie(hop(mine, 0, 3, 0), from_a, from_b)
     north, south, to_west, to_east = settle_edges(flags, from_a, from_b, conv_grad)
-    mine, to_west, to_east = tie(hop(mine, 0, 1, 0), to_west, to_east)
+    mine, to_west, to_east = tie(hop(mine, 0, 0, 4), to_west, to_east)
     west, east = exchange_columns(to_west, to_east)
-    mine, west, east = tie(hop(mine, 0, 3, 0), west, east)
+    mine, west, east = tie(hop(mine, 0, 0, 2), west, east)
     done = finish(0, (), south, north, west, east)
-    mine, *done = tie(hop(mine, 0, 0, 1), *done)
+    mine, *done = tie(hop(mine, 1, 0, 0), *done)
     done = finish(1, done, south, north, west, east)
-    mine, *done = tie(hop(mine, 0, 0, 2), *done)
+    mine, *done = tie(hop(mine, 3, 0, 0), *done)
     done = finish(2, done, south, north, west, east)
     done = finish(3, done, south, north, west, east)
-    mine, *done = tie(hop(mine, 0, 0, 4), *done)
+    mine, *done = tie(hop(mine, 0, 0, 1), *done)
     other = lax.ppermute(mine, "lon", core_pairs())
     total = jnp.concatenate([jnp.where(odd, other, mine), jnp.where(odd, mine, other)], axis=0)
     return total, done

time: 89.6 us -> 88.9 us (level)
  waiting for transfers between devices: 15.9 us -> 10.8 us
  starting transfers between devices: 37.2 us -> 41.5 us
    ppermute x7, waiting for transfers between devices: 7.5 us -> 2.46 us  [hop(): return x + lax.ppermute(x, AXES, chip_pairs(*flips))]
    ppermute x2, starting transfers between devices: 5.26 us -> 8.71 us  [exchange_columns(): west = lax.ppermute(to_east, 'lon', up)]
    ppermute x7, starting transfers between devices: 17.6 us -> 16.4 us  [hop(): return x + lax.ppermute(x, AXES, chip_pairs(*flips))]
    ppermute x1, starting transfers between devices: 0.82 us -> 1.89 us  [reduce_and_spread(): other = lax.ppermute(mine, 'lon', core_pairs())]
    ppermute x2, starting transfers between devices: 9.46 us -> 10.4 us  [exchange_rows(): from_a = lax.ppermute(jnp.where(even, top, bottom), AXES, first)]
  transfers between devices with their start and end apart: 17 -> 17, of which waited for: 10 -> 8; matrix products, arithmetic and copies ran while one was open for 5% -> 5% of each run, Pallas kernels for 14% -> 14%
where the time goes in v4:
time: 88.9 us; the launch traced here: 88.6 us
  starting transfers between devices  41.5 us (47%)
  Pallas kernels  29.8 us (34%)
  waiting for transfers between devices  10.8 us (12%)
  local copies, waits for them, and re-layouts  3.08 us (3%)
  matrix products  1.22 us (1%)
  other arithmetic  1.11 us (1%)
  between operations  1.01 us (1%)
    pallas_call x4, Pallas kernels, call(): pl.pallas_call(body, out_shape=out_shape, in_specs=specs, out_specs=jax.t...  18.7 us
    ppermute x7, starting transfers between devices, hop(): return x + lax.ppermute(x, AXES, chip_pairs(*flips))  16.4 us
    pallas_call x4, Pallas kernels, spread_part(): pl.pallas_call(functools.partial(spread_body, first=c * PART % 32), grid=...  11.1 us
    ppermute x2, starting transfers between devices, exchange_rows(): from_a = lax.ppermute(jnp.where(even, top, bottom), AXES, first)  10.4 us
    ppermute x2, starting transfers between devices, exchange_columns(): west = lax.ppermute(to_east, 'lon', up)  8.71 us
    ppermute x2, waiting for transfers between devices, exchange_columns(): east = lax.ppermute(to_west, 'lon', down)  4.65 us
    ppermute x1, starting transfers between devices, reduce_and_spread(): lax.ppermute(jnp.where(odd, low, high), 'lon', core_pairs())  2.57 us
    ppermute x7, waiting for transfers between devices, hop(): return x + lax.ppermute(x, AXES, chip_pairs(*flips))  2.46 us
  transfers between devices with their start and end apart: 17, of which 8 were waited for; matrix products, arithmetic and copies ran while one was open for 5% of the time, Pallas kernels for 14%

profile of v4, /device:TPU:1, one launch (start us, length us, event | category | flops | bytes accessed | tf_op | source)
XLA Modules:
  0.0 88.6 jit_solution(7828102210363880320)
XLA Ops:
  0.6 0.0 copy-start
  0.7 0.0 copy-start.7
  0.7 0.0 copy-start.8
  0.7 0.0 copy-start.9
  0.7 0.0 copy-start.10
  0.7 0.0 copy-start.11
  0.7 1.1 %fusion.3 = (bf16[64,3,128]{2,1,0:T(4,128)(2,1)S(1)}, bf16[64,3,128]{2,1,0:T(4,128)(2,1)S(1)}) fusion(bf16[64,32,128]{2,1,0:T(8,128)(2,1)} %state.9), kind=kLoop, calls=%fused_computation.17 | loop fusion | bytes 196608 | tf_op jit(solution)/shard_map/slice | solution.py:518
  1.8 0.0 copy-start.2
  1.8 0.0 copy-start.3
  1.9 0.8 collective-permute-start.1
  2.7 4.7 %collective-permute-start = (f32[3,64,128]{2,1,0:T(8,128)S(1)}, f32[3,64,128]{2,1,0:T(8,128)S(1)}, u32[]{:S(2)}, u32[]{:S(2)}) collective-permute-start(f32[3,64,128]{2,1,0:T(8,128)S(1)} %get-tuple-element.108), channel_id=1, source_target_pairs={{0,32},{1,33},{2,34},{3,35},{4,36},{5,37},{6,38},{7,39},{8,40},{9,... | collective-permute-start | bytes 294920 | tf_op jit(solution)/shard_map/ppermute | solution.py:424
  7.4 0.7 broadcast_in_dim.15
  8.2 0.9 copy.34
  9.0 0.8 fusion.2
  9.8 0.1 pad.4.clone
  9.9 1.0 %convolution_bitcast_fusion.1.taps = f32[64,512]{1,0:T(8,128)S(1)} fusion(bf16[49,512]{1,0:T(8,128)(2,1)} %constant.41, bf16[64,49]{0,1:T(8,128)(2,1)S(1)} %copy-done), kind=kOutput, calls=%fused_computation.1 | convolution fusion | flops 3211264 | bytes 187520 | tf_op jit(solution)/shard_map/dot_general | solution.py:523
  10.9 0.1 pad_add_fusion.flags
  11.0 0.0 collective-permute-done.1.from_b
  11.0 0.0 collective-permute-done.from_a
  11.0 0.0 copy-done.1
  11.0 1.1 %edges.2 = (f32[3,64,128]{2,1,0:T(8,128)S(1)}, f32[3,64,128]{2,1,0:T(8,128)S(1)}, f32[2,40,128]{2,1,0:T(8,128)S(1)}, f32[2,40,128]{2,1,0:T(8,128)S(1)}) custom-call(s32[2]{0:T(128)S(1)} %pad_add_fusion.flags, f32[3,64,128]{2,1,0:T(8,128)S(1)} %collective-permute-done.from_a, f32[3,64,128]{2,1,0:T(8,128)S(1)} %collective-permute-done.1.from_b, ...), custom_call_target="tpu_custom_call" | custom-call | flops 1048576 | bytes 2097152 | tf_op jit(solution)/shard_map/edges/pallas_call | solution.py:32
  12.1 2.8 %collective-permute-start.2 = (f32[2,40,128]{2,1,0:T(8,128)S(1)}, f32[2,40,128]{2,1,0:T(8,128)S(1)}, u32[]{:S(2)}, u32[]{:S(2)}) collective-permute-start(f32[2,40,128]{2,1,0:T(8,128)S(1)} %get-tuple-element.56), channel_id=1, source_target_pairs={{0,1},{1,2},{2,3},{3,4},{4,5},{5,6},{6,7},{7,8},{8,9},{9,10},{10,1... | collective-permute-start | bytes 122888 | tf_op jit(solution)/shard_map/ppermute | solution.py:448
  14.9 0.0 collective-permute-start.3
  14.9 0.1 maximum_maximum_fusion.w_in_t
  15.1 0.1 copy.36.w_out
  15.3 0.8 collective-permute-done.2.west
  16.0 2.3 %collective-permute-done.3.east = f32[2,40,128]{2,1,0:T(8,128)S(1)} collective-permute-done((f32[2,40,128]{2,1,0:T(8,128)S(1)}, f32[2,40,128]{2,1,0:T(8,128)S(1)}, u32[]{:S(2)}, u32[]{:S(2)}) %collective-permute-start.3) | collective-permute-done | bytes 40992 | tf_op jit(solution)/shard_map/ppermute | solution.py:449
  18.4 0.1 broadcast_in_dim.12.chan
  18.5 0.0 copy-done.2
  18.5 15.4 %main.1 = (f32[2112,128]{1,0:T(8,128)S(1)}, f32[2112,128]{1,0:T(8,128)S(1)}, f32[3,64,128]{2,1,0:T(8,128)S(1)}, f32[3,64,128]{2,1,0:T(8,128)S(1)}, f32[320,128]{1,0:T(8,128)S(1)}) custom-call(bf16[64,32,128]{2,1,0:T(8,128)(2,1)S(1)} %copy-done.1, f32[3,64,128]{2,1,0:T(8,128)S(1)} %get-tuple-element.54.south, f32[3,64,128]{2,1,0:T(8,128)S(1)} %get-tuple-element.55.north, ...), custom_call_target="tpu_custom_call" | custom-call | flops 1073741824 | bytes 8388608 | tf_op jit(solution)/shard_map/main/pallas_call | solution.py:32
  34.0 2.6 %collective-permute-start.4 = (f32[160,128]{1,0:T(8,128)S(1)}, f32[160,128]{1,0:T(8,128)S(1)}, u32[]{:S(2)}, u32[]{:S(2)}) collective-permute-start(f32[160,128]{1,0:T(8,128)S(1)} %slice_select_fusion), channel_id=1, source_target_pairs={{0,1},{1,0},{2,3},{3,2},{4,5},{5,4},{6,7},{7,6},{8,9},{9,8},{10,11... | collective-permute-start | bytes 245768 | tf_op jit(solution)/shard_map/ppermute | solution.py:476
  36.5 0.9 %collective-permute-done.4 = f32[160,128]{1,0:T(8,128)S(1)} collective-permute-done((f32[160,128]{1,0:T(8,128)S(1)}, f32[160,128]{1,0:T(8,128)S(1)}, u32[]{:S(2)}, u32[]{:S(2)}) %collective-permute-start.4) | collective-permute-done | bytes 81952 | tf_op jit(solution)/shard_map/ppermute | solution.py:476
  37.5 0.1 collective-permute-start.5
  37.6 0.7 collective-permute-start.8
  38.3 0.0 copy-start.5
  38.3 5.7 %collective-permute-start.7 = (f32[3,64,128]{2,1,0:T(8,128)S(1)}, f32[3,64,128]{2,1,0:T(8,128)S(1)}, u32[]{:S(2)}, u32[]{:S(2)}) collective-permute-start(f32[3,64,128]{2,1,0:T(8,128)S(1)} %get-tuple-element.104), channel_id=1, source_target_pairs={{0,32},{1,33},{2,34},{3,35},{4,36},{5,37},{6,38},{7,39},{8,40},{9,... | collective-permute-start | bytes 294920 | tf_op jit(solution)/shard_map/ppermute | solution.py:424
  44.0 0.0 collective-permute-done.5
  44.0 3.0 %collective-permute-start.6 = (f32[160,128]{1,0:T(8,128)S(1)}, f32[160,128]{1,0:T(8,128)S(1)}, u32[]{:S(2)}, u32[]{:S(2)}) collective-permute-start(f32[160,128]{1,0:T(8,128)S(1)} %add.30), channel_id=1, source_target_pairs={{0,96},{1,97},{2,98},{3,99},{4,100},{5,101},{6,102},{7,103},{8,104... | collective-permute-start | bytes 245768 | tf_op jit(solution)/shard_map/ppermute | solution.py:481
  47.0 1.9 %collective-permute-done.6 = f32[160,128]{1,0:T(8,128)S(1)} collective-permute-done((f32[160,128]{1,0:T(8,128)S(1)}, f32[160,128]{1,0:T(8,128)S(1)}, u32[]{:S(2)}, u32[]{:S(2)}) %collective-permute-start.6) | collective-permute-done | bytes 81952 | tf_op jit(solution)/shard_map/ppermute | solution.py:481
  48.9 0.0 collective-permute-done.8.from_b
  48.9 0.0 collective-permute-done.7.from_a
  48.9 5.6 %collective-permute-start.9 = (f32[160,128]{1,0:T(8,128)S(1)}, f32[160,128]{1,0:T(8,128)S(1)}, u32[]{:S(2)}, u32[]{:S(2)}) collective-permute-start(f32[160,128]{1,0:T(8,128)S(1)} %add.31), channel_id=1, source_target_pairs={{0,8},{1,9},{2,10},{3,11},{4,12},{5,13},{6,14},{7,15},{8,0},{9,1},... | collective-permute-start | bytes 245768 | tf_op jit(solution)/shard_map/ppermute | solution.py:481
  54.5 1.3 %edges.3 = (f32[3,64,128]{2,1,0:T(8,128)S(1)}, f32[3,64,128]{2,1,0:T(8,128)S(1)}, f32[2,40,128]{2,1,0:T(8,128)S(1)}, f32[2,40,128]{2,1,0:T(8,128)S(1)}) custom-call(s32[2]{0:T(128)S(1)} %pad_add_fusion.flags, f32[3,64,128]{2,1,0:T(8,128)S(1)} %collective-permute-done.7.from_a, f32[3,64,128]{2,1,0:T(8,128)S(1)} %collective-permute-done.8.from_b, ...), custom_call_target="tpu_custom_call" | custom-call | flops 1048576 | bytes 2097152 | tf_op jit(solution)/shard_map/edges/pallas_call | solution.py:32
  55.8 0.6 collective-permute-done.9
  56.4 3.5 %collective-permute-start.10 = (f32[160,128]{1,0:T(8,128)S(1)}, f32[160,128]{1,0:T(8,128)S(1)}, u32[]{:S(2)}, u32[]{:S(2)}) collective-permute-start(f32[160,128]{1,0:T(8,128)S(1)} %add.32), channel_id=1, source_target_pairs={{0,4},{1,5},{2,6},{3,7},{4,0},{5,1},{6,2},{7,3},{8,12},{9,13},{10,... | collective-permute-start | bytes 245768 | tf_op jit(solution)/shard_map/ppermute | solution.py:481
  59.9 5.9 %collective-permute-start.11 = (f32[2,40,128]{2,1,0:T(8,128)S(1)}, f32[2,40,128]{2,1,0:T(8,128)S(1)}, u32[]{:S(2)}, u32[]{:S(2)}) collective-permute-start(f32[2,40,128]{2,1,0:T(8,128)S(1)} %get-tuple-element.71), channel_id=1, source_target_pairs={{0,1},{1,2},{2,3},{3,4},{4,5},{5,6},{6,7},{7,8},{8,9},{9,10},{10,1... | collective-permute-start | bytes 122888 | tf_op jit(solution)/shard_map/ppermute | solution.py:448
  65.8 0.0 collective-permute-start.12
  65.8 0.0 collective-permute-done.10
  65.8 1.1 %collective-permute-done.11.west = f32[2,40,128]{2,1,0:T(8,128)S(1)} collective-permute-done((f32[2,40,128]{2,1,0:T(8,128)S(1)}, f32[2,40,128]{2,1,0:T(8,128)S(1)}, u32[]{:S(2)}, u32[]{:S(2)}) %collective-permute-start.11) | collective-permute-done | bytes 40992 | tf_op jit(solution)/shard_map/ppermute | solution.py:448
  66.9 2.3 %collective-permute-done.12.east = f32[2,40,128]{2,1,0:T(8,128)S(1)} collective-permute-done((f32[2,40,128]{2,1,0:T(8,128)S(1)}, f32[2,40,128]{2,1,0:T(8,128)S(1)}, u32[]{:S(2)}, u32[]{:S(2)}) %collective-permute-start.12) | collective-permute-done | bytes 40992 | tf_op jit(solution)/shard_map/ppermute | solution.py:449
  69.2 1.2 %collective-permute-start.13 = (f32[160,128]{1,0:T(8,128)S(1)}, f32[160,128]{1,0:T(8,128)S(1)}, u32[]{:S(2)}, u32[]{:S(2)}) collective-permute-start(f32[160,128]{1,0:T(8,128)S(1)} %add.33), channel_id=1, source_target_pairs={{0,16},{1,17},{2,18},{3,19},{4,20},{5,21},{6,22},{7,23},{8,24},{9,... | collective-permute-start | bytes 245768 | tf_op jit(solution)/shard_map/ppermute | solution.py:481
  70.4 0.2 convolution_bitcast_fusion.turned_taps
  70.6 2.7 %spread.4 = (bf16[64,32,128]{2,1,0:T(8,128)(2,1)}, bf16[64,32,128]{2,1,0:T(8,128)(2,1)}) custom-call(s32[2]{0:T(128)S(1)} %pad_add_fusion.flags, f32[2112,128]{1,0:T(8,128)S(1)} %get-tuple-element.67.own.conv_grad, f32[3,64,128]{2,1,0:T(8,128)S(1)} %get-tuple-element.74.south, f32[3,64,128]{2,1,0:T(8,128)S(1)} %get-tuple-element.75.north, ...), custom_call_target="tpu_custom_call" | custom-call | flops 16777216 | bytes 3145728 | tf_op jit(solution)/shard_map/spread/pallas_call | solution.py:358
  73.4 0.0 collective-permute-done.13
  73.4 2.9 %collective-permute-start.14 = (f32[160,128]{1,0:T(8,128)S(1)}, f32[160,128]{1,0:T(8,128)S(1)}, u32[]{:S(2)}, u32[]{:S(2)}) collective-permute-start(f32[160,128]{1,0:T(8,128)S(1)} %add.34), channel_id=1, source_target_pairs={{0,144},{1,145},{2,146},{3,147},{4,148},{5,149},{6,150},{7,151},{8... | collective-permute-start | bytes 245768 | tf_op jit(solution)/shard_map/ppermute | solution.py:481
  76.3 2.8 %spread.5 = (bf16[64,32,128]{2,1,0:T(8,128)(2,1)}, bf16[64,32,128]{2,1,0:T(8,128)(2,1)}) custom-call(s32[2]{0:T(128)S(1)} %pad_add_fusion.flags, f32[2112,128]{1,0:T(8,128)S(1)} %get-tuple-element.67.own.conv_grad, f32[3,64,128]{2,1,0:T(8,128)S(1)} %get-tuple-element.74.south, ...), custom_call_target="tpu_custom_call", output_to_operand_aliasing={{0}: (12, {}), {1}: (13, {})} | custom-call | flops 16777216 | bytes 3145728 | tf_op jit(solution)/shard_map/spread/pallas_call | solution.py:358
  79.1 0.0 collective-permute-done.14
  79.1 0.1 collective-permute-start.15
  79.2 2.8 %spread.6 = (bf16[64,32,128]{2,1,0:T(8,128)(2,1)}, bf16[64,32,128]{2,1,0:T(8,128)(2,1)}) custom-call(s32[2]{0:T(128)S(1)} %pad_add_fusion.flags, f32[2112,128]{1,0:T(8,128)S(1)} %get-tuple-element.67.own.conv_grad, f32[3,64,128]{2,1,0:T(8,128)S(1)} %get-tuple-element.74.south, ...), custom_call_target="tpu_custom_call", output_to_operand_aliasing={{0}: (12, {}), {1}: (13, {})} | custom-call | flops 16777216 | bytes 3145728 | tf_op jit(solution)/shard_map/spread/pallas_call | solution.py:358
  82.0 2.8 %spread.7 = (bf16[64,32,128]{2,1,0:T(8,128)(2,1)}, bf16[64,32,128]{2,1,0:T(8,128)(2,1)}) custom-call(s32[2]{0:T(128)S(1)} %pad_add_fusion.flags, f32[2112,128]{1,0:T(8,128)S(1)} %get-tuple-element.67.own.conv_grad, f32[3,64,128]{2,1,0:T(8,128)S(1)} %get-tuple-element.74.south, ...), custom_call_target="tpu_custom_call", output_to_operand_aliasing={{0}: (12, {}), {1}: (13, {})} | custom-call | flops 16777216 | bytes 3145728 | tf_op jit(solution)/shard_map/spread/pallas_call | solution.py:358
  84.8 0.0 collective-permute-done.15
  84.8 1.9 %collective-permute-start.16 = (f32[160,128]{1,0:T(8,128)S(1)}, f32[160,128]{1,0:T(8,128)S(1)}, u32[]{:S(2)}, u32[]{:S(2)}) collective-permute-start(f32[160,128]{1,0:T(8,128)S(1)} %add.36), channel_id=1, source_target_pairs={{0,1},{1,0},{2,3},{3,2},{4,5},{5,4},{6,7},{7,6},{8,9},{9,8},{10,11... | collective-permute-start | bytes 245768 | tf_op jit(solution)/shard_map/ppermute | solution.py:496
  86.7 0.9 %collective-permute-done.16 = f32[160,128]{1,0:T(8,128)S(1)} collective-permute-done((f32[160,128]{1,0:T(8,128)S(1)}, f32[160,128]{1,0:T(8,128)S(1)}, u32[]{:S(2)}, u32[]{:S(2)}) %collective-permute-start.16) | collective-permute-done | bytes 81952 | tf_op jit(solution)/shard_map/ppermute | solution.py:496
  87.7 0.9 %unpack.1 = (f32[49,64]{1,0:T(8,128)}, f32[64,256]{1,0:T(8,128)}, f32[64,256]{1,0:T(8,128)}, f32[1,256]{1,0:T(1,128)}, f32[5,64]{1,0:T(8,128)}) custom-call(f32[320,128]{1,0:T(8,128)S(1)} %pad_maximum_fusion.sums, f32[49,128]{1,0:T(8,128)S(1)} %copy-done.4), custom_call_target="tpu_custom_call" | custom-call | flops 131072 | bytes 262144 | tf_op jit(solution)/shard_map/unpack/pallas_call | solution.py:32
  (29 shorter events, 0.2 us)
Async XLA Ops:
  0.6 9.3 %copy-start = (bf16[64,49]{0,1:T(8,128)(2,1)S(1)}, bf16[64,49]{0,1:T(8,128)(2,1)}, u32[]{:S(2)}) copy-start(bf16[64,49]{0,1:T(8,128)(2,1)} %param.16) | copy-start | bytes 18820
  0.7 10.4 %copy-start.1 = (bf16[64,32,128]{2,1,0:T(8,128)(2,1)S(1)}, bf16[64,32,128]{2,1,0:T(8,128)(2,1)}, u32[]{:S(2)}) copy-start(bf16[64,32,128]{2,1,0:T(8,128)(2,1)} %state.9) | copy-start | bytes 1572868
  0.7 14.4 %copy-start.6 = (s32[32,128]{1,0:T(8,128)S(1)}, s32[32,128]{1,0:T(8,128)}, u32[]{:S(2)}) copy-start(s32[32,128]{1,0:T(8,128)} %param.25) | copy-start | bytes 49156
  0.7 14.5 %copy-start.7 = (bf16[64]{0:T(256)(128)(2,1)S(1)}, bf16[64]{0:T(256)(128)(2,1)}, u32[]{:S(2)}) copy-start(bf16[64]{0:T(256)(128)(2,1)} %param.17) | copy-start | bytes 388
  0.7 14.5 %copy-start.8 = (bf16[64]{0:T(256)(128)(2,1)S(1)}, bf16[64]{0:T(256)(128)(2,1)}, u32[]{:S(2)}) copy-start(bf16[64]{0:T(256)(128)(2,1)} %param.18) | copy-start | bytes 388
  0.7 14.5 %copy-start.9 = (bf16[64]{0:T(256)(128)(2,1)S(1)}, bf16[64]{0:T(256)(128)(2,1)}, u32[]{:S(2)}) copy-start(bf16[64]{0:T(256)(128)(2,1)} %param.19) | copy-start | bytes 388
  0.7 14.5 %copy-start.10 = (bf16[64]{0:T(256)(128)(2,1)S(1)}, bf16[64]{0:T(256)(128)(2,1)}, u32[]{:S(2)}) copy-start(bf16[64]{0:T(256)(128)(2,1)} %param.23) | copy-start | bytes 388
  0.7 14.5 %copy-start.11 = (bf16[64]{0:T(256)(128)(2,1)S(1)}, bf16[64]{0:T(256)(128)(2,1)}, u32[]{:S(2)}) copy-start(bf16[64]{0:T(256)(128)(2,1)} %param.24) | copy-start | bytes 388
  1.8 16.6 %copy-start.2 = (bf16[64,32,128]{2,1,0:T(8,128)(2,1)S(1)}, bf16[64,32,128]{2,1,0:T(8,128)(2,1)}, u32[]{:S(2)}) copy-start(bf16[64,32,128]{2,1,0:T(8,128)(2,1)} %cot.9) | copy-start | bytes 1572868
  1.8 16.6 %copy-start.3 = (bf16[64,256]{1,0:T(8,128)(2,1)S(1)}, bf16[64,256]{1,0:T(8,128)(2,1)}, u32[]{:S(2)}) copy-start(bf16[64,256]{1,0:T(8,128)(2,1)} %w_in.1) | copy-start | bytes 98308
  1.9 9.1 %collective-permute-start.1 = (f32[3,64,128]{2,1,0:T(8,128)S(1)}, f32[3,64,128]{2,1,0:T(8,128)S(1)}, u32[]{:S(2)}, u32[]{:S(2)}) collective-permute-start(f32[3,64,128]{2,1,0:T(8,128)S(1)} %get-tuple-element.107), channel_id=1, source_target_pairs={{32,64},{33,65},{34,66},{35,67},{36,68},{37,69},{38,70},{39,71},{4... | collective-permute-start | bytes 294920 | tf_op jit(solution)/shard_map/ppermute | solution.py:425
  2.7 8.3 %collective-permute-start = (f32[3,64,128]{2,1,0:T(8,128)S(1)}, f32[3,64,128]{2,1,0:T(8,128)S(1)}, u32[]{:S(2)}, u32[]{:S(2)}) collective-permute-start(f32[3,64,128]{2,1,0:T(8,128)S(1)} %get-tuple-element.108), channel_id=1, source_target_pairs={{0,32},{1,33},{2,34},{3,35},{4,36},{5,37},{6,38},{7,39},{8,40},{9,... | collective-permute-start | bytes 294920 | tf_op jit(solution)/shard_map/ppermute | solution.py:424
  12.1 3.9 %collective-permute-start.2 = (f32[2,40,128]{2,1,0:T(8,128)S(1)}, f32[2,40,128]{2,1,0:T(8,128)S(1)}, u32[]{:S(2)}, u32[]{:S(2)}) collective-permute-start(f32[2,40,128]{2,1,0:T(8,128)S(1)} %get-tuple-element.56), channel_id=1, source_target_pairs={{0,1},{1,2},{2,3},{3,4},{4,5},{5,6},{6,7},{7,8},{8,9},{9,10},{10,1... | collective-permute-start | bytes 122888 | tf_op jit(solution)/shard_map/ppermute | solution.py:448
  14.9 3.4 %collective-permute-start.3 = (f32[2,40,128]{2,1,0:T(8,128)S(1)}, f32[2,40,128]{2,1,0:T(8,128)S(1)}, u32[]{:S(2)}, u32[]{:S(2)}) collective-permute-start(f32[2,40,128]{2,1,0:T(8,128)S(1)} %get-tuple-element.57), channel_id=1, source_target_pairs={{1,0},{2,1},{3,2},{4,3},{5,4},{6,5},{7,6},{8,7},{9,8},{10,9},{11,1... | collective-permute-start | bytes 122888 | tf_op jit(solution)/shard_map/ppermute | solution.py:449
  34.0 3.5 %collective-permute-start.4 = (f32[160,128]{1,0:T(8,128)S(1)}, f32[160,128]{1,0:T(8,128)S(1)}, u32[]{:S(2)}, u32[]{:S(2)}) collective-permute-start(f32[160,128]{1,0:T(8,128)S(1)} %slice_select_fusion), channel_id=1, source_target_pairs={{0,1},{1,0},{2,3},{3,2},{4,5},{5,4},{6,7},{7,6},{8,9},{9,8},{10,11... | collective-permute-start | bytes 245768 | tf_op jit(solution)/shard_map/ppermute | solution.py:476
  37.5 6.5 %collective-permute-start.5 = (f32[160,128]{1,0:T(8,128)S(1)}, f32[160,128]{1,0:T(8,128)S(1)}, u32[]{:S(2)}, u32[]{:S(2)}) collective-permute-start(f32[160,128]{1,0:T(8,128)S(1)} %select_add_fusion), channel_id=1, source_target_pairs={{0,32},{1,33},{2,34},{3,35},{4,36},{5,37},{6,38},{7,39},{8,40},{9,... | collective-permute-start | bytes 245768 | tf_op jit(solution)/shard_map/ppermute | solution.py:481
  37.6 11.3 %collective-permute-start.8 = (f32[3,64,128]{2,1,0:T(8,128)S(1)}, f32[3,64,128]{2,1,0:T(8,128)S(1)}, u32[]{:S(2)}, u32[]{:S(2)}) collective-permute-start(f32[3,64,128]{2,1,0:T(8,128)S(1)} %get-tuple-element.103), channel_id=1, source_target_pairs={{32,64},{33,65},{34,66},{35,67},{36,68},{37,69},{38,70},{39,71},{4... | collective-permute-start | bytes 294920 | tf_op jit(solution)/shard_map/ppermute | solution.py:425
  38.3 32.2 %copy-start.5 = (bf16[49,512]{1,0:T(8,128)(2,1)S(1)}, bf16[49,512]{1,0:T(8,128)(2,1)}, u32[]{:S(2)}) copy-start(bf16[49,512]{1,0:T(8,128)(2,1)} %constant.42) | copy-start | bytes 150532
  38.3 10.6 %collective-permute-start.7 = (f32[3,64,128]{2,1,0:T(8,128)S(1)}, f32[3,64,128]{2,1,0:T(8,128)S(1)}, u32[]{:S(2)}, u32[]{:S(2)}) collective-permute-start(f32[3,64,128]{2,1,0:T(8,128)S(1)} %get-tuple-element.104), channel_id=1, source_target_pairs={{0,32},{1,33},{2,34},{3,35},{4,36},{5,37},{6,38},{7,39},{8,40},{9,... | collective-permute-start | bytes 294920 | tf_op jit(solution)/shard_map/ppermute | solution.py:424
  44.0 4.9 %collective-permute-start.6 = (f32[160,128]{1,0:T(8,128)S(1)}, f32[160,128]{1,0:T(8,128)S(1)}, u32[]{:S(2)}, u32[]{:S(2)}) collective-permute-start(f32[160,128]{1,0:T(8,128)S(1)} %add.30), channel_id=1, source_target_pairs={{0,96},{1,97},{2,98},{3,99},{4,100},{5,101},{6,102},{7,103},{8,104... | collective-permute-start | bytes 245768 | tf_op jit(solution)/shard_map/ppermute | solution.py:481
  48.9 7.5 %collective-permute-start.9 = (f32[160,128]{1,0:T(8,128)S(1)}, f32[160,128]{1,0:T(8,128)S(1)}, u32[]{:S(2)}, u32[]{:S(2)}) collective-permute-start(f32[160,128]{1,0:T(8,128)S(1)} %add.31), channel_id=1, source_target_pairs={{0,8},{1,9},{2,10},{3,11},{4,12},{5,13},{6,14},{7,15},{8,0},{9,1},... | collective-permute-start | bytes 245768 | tf_op jit(solution)/shard_map/ppermute | solution.py:481
  56.4 9.4 %collective-permute-start.10 = (f32[160,128]{1,0:T(8,128)S(1)}, f32[160,128]{1,0:T(8,128)S(1)}, u32[]{:S(2)}, u32[]{:S(2)}) collective-permute-start(f32[160,128]{1,0:T(8,128)S(1)} %add.32), channel_id=1, source_target_pairs={{0,4},{1,5},{2,6},{3,7},{4,0},{5,1},{6,2},{7,3},{8,12},{9,13},{10,... | collective-permute-start | bytes 245768 | tf_op jit(solution)/shard_map/ppermute | solution.py:481
  59.9 7.0 %collective-permute-start.11 = (f32[2,40,128]{2,1,0:T(8,128)S(1)}, f32[2,40,128]{2,1,0:T(8,128)S(1)}, u32[]{:S(2)}, u32[]{:S(2)}) collective-permute-start(f32[2,40,128]{2,1,0:T(8,128)S(1)} %get-tuple-element.71), channel_id=1, source_target_pairs={{0,1},{1,2},{2,3},{3,4},{4,5},{5,6},{6,7},{7,8},{8,9},{9,10},{10,1... | collective-permute-start | bytes 122888 | tf_op jit(solution)/shard_map/ppermute | solution.py:448
  65.8 3.4 %collective-permute-start.12 = (f32[2,40,128]{2,1,0:T(8,128)S(1)}, f32[2,40,128]{2,1,0:T(8,128)S(1)}, u32[]{:S(2)}, u32[]{:S(2)}) collective-permute-start(f32[2,40,128]{2,1,0:T(8,128)S(1)} %get-tuple-element.72), channel_id=1, source_target_pairs={{1,0},{2,1},{3,2},{4,3},{5,4},{6,5},{7,6},{8,7},{9,8},{10,9},{11,1... | collective-permute-start | bytes 122888 | tf_op jit(solution)/shard_map/ppermute | solution.py:449
  69.2 4.2 %collective-permute-start.13 = (f32[160,128]{1,0:T(8,128)S(1)}, f32[160,128]{1,0:T(8,128)S(1)}, u32[]{:S(2)}, u32[]{:S(2)}) collective-permute-start(f32[160,128]{1,0:T(8,128)S(1)} %add.33), channel_id=1, source_target_pairs={{0,16},{1,17},{2,18},{3,19},{4,20},{5,21},{6,22},{7,23},{8,24},{9,... | collective-permute-start | bytes 245768 | tf_op jit(solution)/shard_map/ppermute | solution.py:481
  73.4 5.7 %collective-permute-start.14 = (f32[160,128]{1,0:T(8,128)S(1)}, f32[160,128]{1,0:T(8,128)S(1)}, u32[]{:S(2)}, u32[]{:S(2)}) collective-permute-start(f32[160,128]{1,0:T(8,128)S(1)} %add.34), channel_id=1, source_target_pairs={{0,144},{1,145},{2,146},{3,147},{4,148},{5,149},{6,150},{7,151},{8... | collective-permute-start | bytes 245768 | tf_op jit(solution)/shard_map/ppermute | solution.py:481
  79.1 5.7 %collective-permute-start.15 = (f32[160,128]{1,0:T(8,128)S(1)}, f32[160,128]{1,0:T(8,128)S(1)}, u32[]{:S(2)}, u32[]{:S(2)}) collective-permute-start(f32[160,128]{1,0:T(8,128)S(1)} %add.35), channel_id=1, source_target_pairs={{0,2},{1,3},{2,0},{3,1},{4,6},{5,7},{6,4},{7,5},{8,10},{9,11},{10,... | collective-permute-start | bytes 245768 | tf_op jit(solution)/shard_map/ppermute | solution.py:481
  82.0 5.7 %copy-start.4 = (f32[49,128]{1,0:T(8,128)S(1)}, f32[49,128]{1,0:T(8,128)}, u32[]{:S(2)}) copy-start(f32[49,128]{1,0:T(8,128)} %constant.40.clone.pick) | copy-start | bytes 75268
  84.8 2.8 %collective-permute-start.16 = (f32[160,128]{1,0:T(8,128)S(1)}, f32[160,128]{1,0:T(8,128)S(1)}, u32[]{:S(2)}, u32[]{:S(2)}) collective-permute-start(f32[160,128]{1,0:T(8,128)S(1)} %add.36), channel_id=1, source_target_pairs={{0,1},{1,0},{2,3},{3,2},{4,5},{5,4},{6,7},{7,6},{8,9},{9,8},{10,11... | collective-permute-start | bytes 245768 | tf_op jit(solution)/shard_map/ppermute | solution.py:496
